TPU v7x, 1024 devices: a whole 4x4x32 slice. The times are simulated.
1024 devices in a mesh: energy: 128 (over z_hi, y, x, core), mom: 8 (over z_lo).
Axes of the slice: x: 4, y: 4, z: 32 (z_hi: 4, z_lo: 8; z = z_hi * 8 + z_lo), core: 2. Of those that a mesh axis runs over, the one named last changes fastest.
Arguments:
- green: bfloat16 [8, 128, 4, 2, 128, 128], P('mom', 'energy'), may hold values from -6 to 6
- grad: bfloat16 [8, 4, 2, 2, 128, 128], P('mom'), may hold values from -0.375 to 0.375
- coupling: float32 [8, 4], replicated, may hold values from 0.05 to 0.3
- occupation: float32 [4], replicated, may hold values from 0.1 to 2
- offsets: int32 [4], replicated, may hold values from 1 to 4, as said below
- neighbours: int32 [4, 2], replicated, may hold values from 0 to 3
- qtable: int32 [8, 8], P('mom'), may hold values from 0 to 7
Outputs:
- sigma: float32 [8, 128, 4, 2, 128, 128], P('mom', 'energy')
Inputs may be any that keep to these rules, and one draw needn't show every extreme that they name: `offsets`: some mode has offset 1 and some mode has offset 4.
All inputs are finite; a program needn't handle non-finite values.
Results may differ from a plain program's by a relative error of at most 0.0029.
Values may be sent and summed in bfloat16 or wider, within the bound.
No kernel may reach another device: no remote copies, remote signals or barrier semaphores. Data moves between devices by JAX's collectives and lax.ppermute only.
A program may use at most 32 MiB of HBM per device.

v0:
```python
import jax
import jax.numpy as jnp
from jax import lax
from jax.sharding import PartitionSpec as P

MAXOFF = 4


def laid_out(blocks, dim):
    dims = list(blocks.shape[1:])
    dims[dim] *= blocks.shape[0]
    return jnp.moveaxis(blocks, 0, dim).reshape(dims)


def from_everyone(x, axis):
    copies = jnp.broadcast_to(x, (lax.axis_size(axis), *x.shape))
    return lax.all_to_all(copies, axis, split_axis=0, concat_axis=0, tiled=True)


def gather_directly(x, axis, dim):
    return laid_out(from_everyone(x, axis), dim)


def passed_along(value, axis, steps):
    count = lax.axis_size(axis)
    initial, last = (max(0, -steps), min(count, count - steps))
    return lax.ppermute(value, axis, [(source, source + steps) for source in range(initial, last)])


def shards(green, grad, coupling, occupation, offsets, neighbours, qtable):
    clusters = grad.shape[1]
    momenta = coupling.shape[0]
    orbits = grad.shape[4]
    high = lax.Precision.HIGHEST
    pick = (neighbours[:, :, None] == jnp.arange(clusters, dtype=jnp.int32)[None, None, :]).astype(
        jnp.bfloat16
    )
    grad_re = grad[:, :, :, 0]
    grad_im = grad[:, :, :, 1]
    left_block = jnp.concatenate(
        [
            jnp.concatenate([grad_re, -grad_im], axis=-1),
            jnp.concatenate([grad_im, grad_re], axis=-1),
        ],
        axis=-2,
    )
    trans_re = jnp.swapaxes(grad_re, -1, -2)
    trans_im = jnp.swapaxes(grad_im, -1, -2)
    right_block = jnp.concatenate(
        [
            jnp.concatenate([trans_re, -trans_im], axis=-1),
            jnp.concatenate([trans_im, trans_re], axis=-1),
        ],
        axis=-2,
    )
    piece = gather_directly(green, "mom", 0)
    count = piece.shape[0]
    chosen = jnp.einsum(
        "csx,jxrab->jcsrab", pick, piece[:, 0], preferred_element_type=jnp.float32
    ).astype(jnp.bfloat16)
    chosen = chosen.reshape(count, clusters, chosen.shape[2], 2 * orbits, orbits)
    matches = (qtable[:, :, None] == jnp.arange(momenta, dtype=jnp.int32)[None, None, :]).astype(
        jnp.float32
    )
    weights = jnp.einsum("kjq,qn->kjn", matches, coupling, precision=high)
    product = jnp.einsum(
        "kcsxy,jcsyd->kjcsxd", left_block, chosen, preferred_element_type=jnp.float32
    ).astype(jnp.bfloat16)
    shape = product.shape
    product = product.reshape(shape[0], shape[1], shape[2], shape[3], 2, orbits, orbits)
    product = jnp.swapaxes(product, 4, 5).reshape(
        shape[0], shape[1], shape[2], shape[3], orbits, 2 * orbits
    )
    triple = jnp.einsum(
        "kjcsay,kcsyz->kjcsaz", product, right_block, preferred_element_type=jnp.float32
    )
    triple = triple.reshape(shape[0], shape[1], shape[2], shape[3], orbits, 2, orbits)
    accum = jnp.einsum("kjn,kjcsare->kncrae", weights, triple, precision=high)
    levels = jnp.arange(1, MAXOFF + 1, dtype=jnp.int32)
    select = (offsets[None, :] == levels[:, None]).astype(jnp.float32)
    emitted = jnp.einsum(
        "dn,kncrab->dkcrab", select * (1.0 + occupation[None, :]), accum, precision=high
    )
    absorbed = jnp.einsum("dn,kncrab->dkcrab", select * occupation[None, :], accum, precision=high)
    upward = jnp.zeros(emitted.shape[1:], jnp.float32)
    downward = jnp.zeros(emitted.shape[1:], jnp.float32)
    for level in range(MAXOFF - 1, -1, -1):
        upward = passed_along(upward + emitted[level], "energy", 1)
        downward = passed_along(downward + absorbed[level], "energy", -1)
    total = upward + downward
    return total[:, None]


def solution(mesh):
    in_specs = (
        P("mom", "energy", None, None, None, None),
        P("mom", None, None, None, None, None),
        P(),
        P(),
        P(),
        P(),
        P("mom", None),
    )
    out_specs = P("mom", "energy", None, None, None, None)
    return jax.shard_map(shards, mesh=mesh, in_specs=in_specs, out_specs=out_specs, check_vma=False)
```

profile of v0, /device:TPU:768, one launch (start us, length us, event | category | flops | bytes accessed | tf_op | source)
XLA Modules:
  0.0 413.9 jit_solution(15173541283485910743)
XLA Ops:
  0.0 0.0 copy-start
  0.0 1.2 copy.18
  1.2 2.2 broadcast_in_dim.4
  3.3 0.0 copy-start.8
  3.3 0.0 copy-start.7
  3.3 0.0 copy-start.1
  3.3 5.2 %all-to-all-start = ((bf16[8,1,1,4,2,128,128]{6,3,5,4,2,1,0:T(4,128)(2,1)}), bf16[8,1,1,4,2,128,128]{6,3,5,4,2,1,0:T(4,128)(2,1)S(1)}, u32[]{:S(2)}, u32[]{:S(2)}) async-start(bf16[8,1,1,4,2,128,128]{6,3,5,4,2,1,0:T(4,128)(2,1)} %broadcast_in_dim.4), calls=%async_computation | async-start | bytes 4194304 | tf_op jit(solution)/shard_map/all_to_all | solution.py:17
  8.5 0.0 copy-start.5
  8.5 0.0 copy-done
  8.5 0.0 copy-done.8
  8.5 0.2 convolution_bitcast_fusion.1
  8.7 0.0 copy-done.7
  8.7 0.0 copy-done.1
  8.7 0.7 fusion.42
  9.5 1.1 slice_bitcast_fusion
  10.6 0.0 copy-start.2
  10.6 0.0 copy-start.3
  10.6 94.0 %all-to-all-done = bf16[8,1,1,4,2,128,128]{6,3,5,4,2,1,0:T(4,128)(2,1)S(1)} async-done(((bf16[8,1,1,4,2,128,128]{6,3,5,4,2,1,0:T(4,128)(2,1)}), bf16[8,1,1,4,2,128,128]{6,3,5,4,2,1,0:T(4,128)(2,1)S(1)}, u32[]{:S(2)}, u32[]{:S(2)}) %all-to-all-start) | async-done | bytes 2097184 | tf_op jit(solution)/shard_map/all_to_all | solution.py:17
  104.6 0.0 copy-done.5
  104.6 0.0 copy-start.4
  104.6 1.7 convolution_convert_fusion
  106.4 0.0 copy-done.2
  106.4 0.0 copy-done.3
  106.4 0.0 copy-done.4
  106.4 3.5 convert_bitcast_fusion
  109.9 6.9 %reshape.97 = bf16[1,8,4,2,2,128,128]{5,4,6,1,3,2,0:T(2,128)(2,1)} reshape(bf16[1,8,4,2,256,128]{4,5,1,3,2,0:T(8,128)(2,1)} %convert_bitcast_fusion) | data formatting | bytes 8388608 | tf_op jit(solution)/shard_map/reshape | solution.py:70
  116.8 16.0 %copy.20 = bf16[1,8,4,2,128,2,128]{6,5,4,3,1,2,0:T(2,128)(2,1)} copy(bf16[1,8,4,2,128,2,128]{4,5,6,1,3,2,0:T(2,128)(2,1)} %bitcast.90) | data formatting | bytes 8388608 | tf_op jit(solution)/shard_map/transpose | solution.py:71
  132.8 7.6 %reshape.98 = bf16[8,4,2,128,256]{4,3,2,0,1:T(8,128)(2,1)} reshape(bf16[1,8,4,2,128,2,128]{6,5,4,3,1,2,0:T(2,128)(2,1)} %copy.20) | data formatting | bytes 8388608 | tf_op jit(solution)/shard_map/reshape.8
  140.4 5.5 %fusion.9 = f32[4,256,8,128,1]{3,1,4,2,0:T(8,128)} fusion(bf16[8,4,2,128,256]{4,3,2,0,1:T(8,128)(2,1)} %reshape.98, bf16[1,4,2,128,128]{3,4,2,1,0:T(8,128)(2,1)S(1)} %get-tuple-element.6, bf16[1,4,2,128,128]{3,4,2,1,0:T(8,128)(2,1)S(1)} %get-tuple-element.5, bf16[1,4,2,128,128]{3,4,2,1,0:T(8,128)(2,1)S(1)} %fusion.43), kind=kOutput, calls=%fused_computation.12 | convolution fusion | flops 1077936128 | bytes 9175040 | tf_op jit(solution)/shard_map/kjcsay,kcsyz->kjcsaz/dot_general | solution.py:74
  145.9 5.5 %copy.21 = f32[8,4,128,2,128]{4,0,3,2,1:T(8,128)} copy(f32[8,4,128,2,128]{2,4,3,0,1:T(8,128)} %bitcast.89) | data formatting | bytes 8388608 | tf_op jit(solution)/shard_map/reshape.14
  151.3 0.0 copy-start.6
  151.3 5.8 %convolution_bitcast_fusion = f32[4,4,2,128,128]{4,0,2,3,1:T(4,128)S(1)} fusion(f32[8,4,128,2,128]{4,0,3,2,1:T(8,128)} %copy.21, f32[8,4,1,1,1]{0,1,4,3,2:T(4,128)S(1)} %convolution_bitcast_fusion.1), kind=kOutput, calls=%fused_computation.9 | convolution fusion | flops 50331648 | bytes 6291584 | tf_op jit(solution)/shard_map/kjn,kjcsare->kncrae/dot_general | solution.py:78
  157.2 0.0 copy-done.6
  157.2 3.9 fusion.5
  161.1 0.5 slice.52
  161.6 11.6 %collective-permute-start.4 = (f32[1,4,2,128,128]{4,0,3,2,1:T(1,128)S(1)}, f32[1,4,2,128,128]{4,0,3,2,1:T(1,128)S(1)}, u32[]{:S(2)}, u32[]{:S(2)}) collective-permute-start(f32[1,4,2,128,128]{4,0,3,2,1:T(1,128)S(1)} %slice.52), channel_id=1, source_target_pairs={{8,0},{16,8},{24,16},{32,24},{40,32},{48,40},{56,48},{64,56},{72,6... | collective-permute-start | bytes 1572872 | tf_op jit(solution)/shard_map/ppermute | solution.py:27
  173.2 3.9 fusion.7
  177.1 0.5 slice.48
  177.7 1.9 collective-permute-start
  179.6 132.9 %collective-permute-done.4 = f32[1,4,2,128,128]{4,0,3,2,1:T(1,128)S(1)} collective-permute-done((f32[1,4,2,128,128]{4,0,3,2,1:T(1,128)S(1)}, f32[1,4,2,128,128]{4,0,3,2,1:T(1,128)S(1)}, u32[]{:S(2)}, u32[]{:S(2)}) %collective-permute-start.4) | collective-permute-done | bytes 524320 | tf_op jit(solution)/shard_map/ppermute | solution.py:27
  312.5 0.8 slice_add_fusion.2
  313.4 16.9 %collective-permute-start.5 = (f32[1,4,2,128,128]{4,0,3,2,1:T(1,128)S(1)}, f32[1,4,2,128,128]{4,0,3,2,1:T(1,128)S(1)}, u32[]{:S(2)}, u32[]{:S(2)}) collective-permute-start(f32[1,4,2,128,128]{4,0,3,2,1:T(1,128)S(1)} %slice_add_fusion.2), channel_id=1, source_target_pairs={{8,0},{16,8},{24,16},{32,24},{40,32},{48,40},{56,48},{64,56},{72,6... | collective-permute-start | bytes 1572872 | tf_op jit(solution)/shard_map/ppermute | solution.py:27
  330.3 0.0 collective-permute-done
  330.3 0.8 slice_add_fusion.5
  331.1 1.9 collective-permute-start.1
  333.1 13.5 %collective-permute-done.5 = f32[1,4,2,128,128]{4,0,3,2,1:T(1,128)S(1)} collective-permute-done((f32[1,4,2,128,128]{4,0,3,2,1:T(1,128)S(1)}, f32[1,4,2,128,128]{4,0,3,2,1:T(1,128)S(1)}, u32[]{:S(2)}, u32[]{:S(2)}) %collective-permute-start.5) | collective-permute-done | bytes 524320 | tf_op jit(solution)/shard_map/ppermute | solution.py:27
  346.6 0.8 slice_add_fusion.1
  347.4 16.8 %collective-permute-start.6 = (f32[1,4,2,128,128]{4,0,3,2,1:T(1,128)S(1)}, f32[1,4,2,128,128]{4,0,3,2,1:T(1,128)S(1)}, u32[]{:S(2)}, u32[]{:S(2)}) collective-permute-start(f32[1,4,2,128,128]{4,0,3,2,1:T(1,128)S(1)} %slice_add_fusion.1), channel_id=1, source_target_pairs={{8,0},{16,8},{24,16},{32,24},{40,32},{48,40},{56,48},{64,56},{72,6... | collective-permute-start | bytes 1572872 | tf_op jit(solution)/shard_map/ppermute | solution.py:27
  364.2 0.0 collective-permute-done.1
  364.2 0.8 slice_add_fusion.4
  365.0 1.9 collective-permute-start.2
  366.9 3.9 collective-permute-done.6
  370.8 0.6 slice_add_fusion
  371.5 16.7 %collective-permute-start.7 = (f32[1,4,2,128,128]{4,0,3,2,1:T(1,128)S(1)}, f32[1,4,2,128,128]{4,0,3,2,1:T(1,128)S(1)}, u32[]{:S(2)}, u32[]{:S(2)}) collective-permute-start(f32[1,4,2,128,128]{4,0,3,2,1:T(1,128)S(1)} %slice_add_fusion), channel_id=1, source_target_pairs={{8,0},{16,8},{24,16},{32,24},{40,32},{48,40},{56,48},{64,56},{72,6... | collective-permute-start | bytes 1572872 | tf_op jit(solution)/shard_map/ppermute | solution.py:27
  388.2 0.3 collective-permute-done.2
  388.5 0.6 slice_add_fusion.3
  389.1 1.9 collective-permute-start.3
  391.0 3.9 collective-permute-done.7
  394.9 17.6 %collective-permute-done.3 = f32[1,4,2,128,128]{4,0,3,2,1:T(1,128)S(1)} collective-permute-done((f32[1,4,2,128,128]{4,0,3,2,1:T(1,128)S(1)}, f32[1,4,2,128,128]{4,0,3,2,1:T(1,128)S(1)}, u32[]{:S(2)}, u32[]{:S(2)}) %collective-permute-start.3) | collective-permute-done | bytes 524320 | tf_op jit(solution)/shard_map/ppermute | solution.py:27
  412.5 1.3 add.40
  (3 shorter events, 0.0 us)
Async XLA Ops:
  0.0 8.5 %copy-start = (f32[8,4]{0,1:T(4,128)S(1)}, f32[8,4]{0,1:T(4,128)}, u32[]{:S(2)}) copy-start(f32[8,4]{0,1:T(4,128)} %param.9) | copy-start | bytes 388
  3.3 5.2 %copy-start.8 = (s32[1,8]{1,0:T(1,128)S(1)}, s32[1,8]{1,0:T(1,128)}, u32[]{:S(2)}) copy-start(s32[1,8]{1,0:T(1,128)} %param.13) | copy-start | bytes 100
  3.3 5.4 %copy-start.7 = (f32[4]{0:T(128)S(1)}, f32[4]{0:T(128)}, u32[]{:S(2)}) copy-start(f32[4]{0:T(128)} %param.10) | copy-start | bytes 52
  3.3 5.4 %copy-start.1 = (bf16[1,4,2,2,128,128]{5,4,3,2,1,0:T(8,128)(2,1)S(1)}, bf16[1,4,2,2,128,128]{5,4,3,2,1,0:T(8,128)(2,1)}, u32[]{:S(2)}) copy-start(bf16[1,4,2,2,128,128]{5,4,3,2,1,0:T(8,128)(2,1)} %param.8) | copy-start | bytes 1572868
  3.3 101.3 %all-to-all-start = ((bf16[8,1,1,4,2,128,128]{6,3,5,4,2,1,0:T(4,128)(2,1)}), bf16[8,1,1,4,2,128,128]{6,3,5,4,2,1,0:T(4,128)(2,1)S(1)}, u32[]{:S(2)}, u32[]{:S(2)}) async-start(bf16[8,1,1,4,2,128,128]{6,3,5,4,2,1,0:T(4,128)(2,1)} %broadcast_in_dim.4), calls=%async_computation | async-start | bytes 4194304 | tf_op jit(solution)/shard_map/all_to_all | solution.py:17
  8.5 96.1 %copy-start.5 = (s32[4,2]{0,1:T(2,128)S(1)}, s32[4,2]{0,1:T(2,128)}, u32[]{:S(2)}) copy-start(s32[4,2]{0,1:T(2,128)} %param.12) | copy-start | bytes 100
  10.6 95.8 %copy-start.2 = (bf16[1,4,2,128,128]{4,3,2,1,0:T(8,128)(2,1)S(1)}, bf16[1,4,2,128,128]{4,3,2,1,0:T(8,128)(2,1)}, u32[]{:S(2)}) copy-start(bf16[1,4,2,128,128]{4,3,2,1,0:T(8,128)(2,1)} %fusion.42) | copy-start | bytes 786436
  10.6 95.8 %copy-start.3 = (bf16[1,4,2,128,128]{4,3,2,1,0:T(8,128)(2,1)S(1)}, bf16[1,4,2,128,128]{4,3,2,1,0:T(8,128)(2,1)}, u32[]{:S(2)}) copy-start(bf16[1,4,2,128,128]{4,3,2,1,0:T(8,128)(2,1)} %get-tuple-element.7) | copy-start | bytes 786436
  104.6 1.8 copy-start.4
  151.3 5.8 %copy-start.6 = (s32[4]{0:T(128)S(1)}, s32[4]{0:T(128)}, u32[]{:S(2)}) copy-start(s32[4]{0:T(128)} %param.11) | copy-start | bytes 52
  161.6 150.9 %collective-permute-start.4 = (f32[1,4,2,128,128]{4,0,3,2,1:T(1,128)S(1)}, f32[1,4,2,128,128]{4,0,3,2,1:T(1,128)S(1)}, u32[]{:S(2)}, u32[]{:S(2)}) collective-permute-start(f32[1,4,2,128,128]{4,0,3,2,1:T(1,128)S(1)} %slice.52), channel_id=1, source_target_pairs={{8,0},{16,8},{24,16},{32,24},{40,32},{48,40},{56,48},{64,56},{72,6... | collective-permute-start | bytes 1572872 | tf_op jit(solution)/shard_map/ppermute | solution.py:27
  177.7 152.6 %collective-permute-start = (f32[1,4,2,128,128]{4,0,3,2,1:T(1,128)S(1)}, f32[1,4,2,128,128]{4,0,3,2,1:T(1,128)S(1)}, u32[]{:S(2)}, u32[]{:S(2)}) collective-permute-start(f32[1,4,2,128,128]{4,0,3,2,1:T(1,128)S(1)} %slice.48), channel_id=1, source_target_pairs={{0,8},{8,16},{16,24},{24,32},{32,40},{40,48},{48,56},{56,64},{64,7... | collective-permute-start | bytes 1572872 | tf_op jit(solution)/shard_map/ppermute | solution.py:27
  313.4 33.2 %collective-permute-start.5 = (f32[1,4,2,128,128]{4,0,3,2,1:T(1,128)S(1)}, f32[1,4,2,128,128]{4,0,3,2,1:T(1,128)S(1)}, u32[]{:S(2)}, u32[]{:S(2)}) collective-permute-start(f32[1,4,2,128,128]{4,0,3,2,1:T(1,128)S(1)} %slice_add_fusion.2), channel_id=1, source_target_pairs={{8,0},{16,8},{24,16},{32,24},{40,32},{48,40},{56,48},{64,56},{72,6... | collective-permute-start | bytes 1572872 | tf_op jit(solution)/shard_map/ppermute | solution.py:27
  331.1 33.0 %collective-permute-start.1 = (f32[1,4,2,128,128]{4,0,3,2,1:T(1,128)S(1)}, f32[1,4,2,128,128]{4,0,3,2,1:T(1,128)S(1)}, u32[]{:S(2)}, u32[]{:S(2)}) collective-permute-start(f32[1,4,2,128,128]{4,0,3,2,1:T(1,128)S(1)} %slice_add_fusion.5), channel_id=1, source_target_pairs={{0,8},{8,16},{16,24},{24,32},{32,40},{40,48},{48,56},{56,64},{64,7... | collective-permute-start | bytes 1572872 | tf_op jit(solution)/shard_map/ppermute | solution.py:27
  347.4 23.4 %collective-permute-start.6 = (f32[1,4,2,128,128]{4,0,3,2,1:T(1,128)S(1)}, f32[1,4,2,128,128]{4,0,3,2,1:T(1,128)S(1)}, u32[]{:S(2)}, u32[]{:S(2)}) collective-permute-start(f32[1,4,2,128,128]{4,0,3,2,1:T(1,128)S(1)} %slice_add_fusion.1), channel_id=1, source_target_pairs={{8,0},{16,8},{24,16},{32,24},{40,32},{48,40},{56,48},{64,56},{72,6... | collective-permute-start | bytes 1572872 | tf_op jit(solution)/shard_map/ppermute | solution.py:27
  365.0 23.5 %collective-permute-start.2 = (f32[1,4,2,128,128]{4,0,3,2,1:T(1,128)S(1)}, f32[1,4,2,128,128]{4,0,3,2,1:T(1,128)S(1)}, u32[]{:S(2)}, u32[]{:S(2)}) collective-permute-start(f32[1,4,2,128,128]{4,0,3,2,1:T(1,128)S(1)} %slice_add_fusion.4), channel_id=1, source_target_pairs={{0,8},{8,16},{16,24},{24,32},{32,40},{40,48},{48,56},{56,64},{64,7... | collective-permute-start | bytes 1572872 | tf_op jit(solution)/shard_map/ppermute | solution.py:27
  371.5 23.4 %collective-permute-start.7 = (f32[1,4,2,128,128]{4,0,3,2,1:T(1,128)S(1)}, f32[1,4,2,128,128]{4,0,3,2,1:T(1,128)S(1)}, u32[]{:S(2)}, u32[]{:S(2)}) collective-permute-start(f32[1,4,2,128,128]{4,0,3,2,1:T(1,128)S(1)} %slice_add_fusion), channel_id=1, source_target_pairs={{8,0},{16,8},{24,16},{32,24},{40,32},{48,40},{56,48},{64,56},{72,6... | collective-permute-start | bytes 1572872 | tf_op jit(solution)/shard_map/ppermute | solution.py:27
  389.1 23.4 %collective-permute-start.3 = (f32[1,4,2,128,128]{4,0,3,2,1:T(1,128)S(1)}, f32[1,4,2,128,128]{4,0,3,2,1:T(1,128)S(1)}, u32[]{:S(2)}, u32[]{:S(2)}) collective-permute-start(f32[1,4,2,128,128]{4,0,3,2,1:T(1,128)S(1)} %slice_add_fusion.3), channel_id=1, source_target_pairs={{0,8},{8,16},{16,24},{24,32},{32,40},{40,48},{48,56},{56,64},{64,7... | collective-permute-start | bytes 1572872 | tf_op jit(solution)/shard_map/ppermute | solution.py:27
where the time goes:
time: 415 us; the launch traced here: 414 us
  waiting for transfers between devices  266 us (64%)
  starting transfers between devices  74.9 us (18%)
  local copies, waits for them, and re-layouts  41.5 us (10%)
  matrix products  24.5 us (6%)
  other arithmetic  6.6 us (2%)
    ppermute x8, waiting for transfers between devices, passed_along(): lax.ppermute(value, axis, [(source, source + steps) for source in range(i...  172 us
    all_to_all x1, waiting for transfers between devices, from_everyone(): return lax.all_to_all(copies, axis, split_axis=0, concat_axis=0, tiled=True)  94 us
    ppermute x8, starting transfers between devices, passed_along(): lax.ppermute(value, axis, [(source, source + steps) for source in range(i...  69.7 us
    transpose x1, local copies, waits for them, and re-layouts, shards(): jnp.swapaxes(product, 4, 5)  16 us
    another operation x3, local copies, waits for them, and re-layouts  14.2 us
  transfers between devices with their start and end apart: 9, of which 7 were waited for; matrix products, arithmetic and copies ran while one was open for 3% of the time, Pallas kernels for 0%

commit v1 on v0

v1 whole, which is shorter than its diff:
```python
import jax
import jax.numpy as jnp
from jax import lax
from jax.experimental import pallas as pl
from jax.experimental.pallas import tpu as pltpu
from jax.sharding import Mesh
from jax.sharding import PartitionSpec as P

PLANE = ("y", "x", "core")
LINE = ("zh", "mom")


def mix_kernel(coupling, occupation, offsets, qtable, before, here, after, out, window, terms):
    momenta, quad = here.shape[:2]
    modes = occupation.shape[0]
    for j in range(momenta):
        for i in range(quad):
            window[j, i] = before[j, i].astype(jnp.float32)
            window[j, quad + i] = here[j, i].astype(jnp.float32)
            window[j, 2 * quad + i] = after[j, i].astype(jnp.float32)
    for m in range(modes):
        absorb = occupation[m]
        emit = 1.0 + absorb
        shift = offsets[m]
        for j in range(momenta):
            for i in range(quad):
                terms[m, j, i] = emit * window[j, quad + i - shift] + absorb * window[j, quad + i + shift]

    def one(k, carry):
        total = [jnp.zeros(here.shape[2:], jnp.float32) for _ in range(quad)]
        for j in range(momenta):
            row = qtable[k, j]
            for m in range(modes):
                weight = coupling[row, m]
                for i in range(quad):
                    total[i] = total[i] + weight * terms[m, j, i]
        for i in range(quad):
            out[k, i] = total[i].astype(out.dtype)
        return carry

    lax.fori_loop(0, momenta, one, 0)


def mixed(coupling, occupation, offsets, qtable, before, here, after):
    smem = pl.BlockSpec(memory_space=pltpu.SMEM)
    vmem = pl.BlockSpec(memory_space=pltpu.VMEM)
    momenta, quad, rows, lanes = here.shape
    modes = occupation.shape[0]
    return pl.pallas_call(
        mix_kernel,
        out_shape=jax.ShapeDtypeStruct(here.shape, jnp.bfloat16),
        in_specs=[smem] * 4 + [vmem] * 3,
        out_specs=vmem,
        scratch_shapes=[
            pltpu.VMEM((momenta, 3 * quad, rows, lanes), jnp.float32),
            pltpu.VMEM((modes, momenta, quad, rows, lanes), jnp.float32),
        ],
    )(coupling, occupation, offsets, qtable, before, here, after)


def dress_kernel(neighbours, grad, mixed_ref, out):
    clusters, listed = grad.shape[:2]
    for c in range(clusters):
        total = None
        for s in range(listed):
            near = neighbours[c, s]
            re = mixed_ref[near, 0]
            im = mixed_ref[near, 1]
            d_re = grad[c, s, 0]
            d_im = grad[c, s, 1]
            left = jnp.concatenate([d_re, d_im], axis=1)
            middle = jnp.concatenate(
                [jnp.concatenate([re, im], axis=1), jnp.concatenate([-im, re], axis=1)], axis=0
            )
            right = jnp.concatenate([left, jnp.concatenate([-d_im, d_re], axis=1)], axis=0)
            prod = jnp.dot(left, middle, preferred_element_type=jnp.float32)
            high = prod.astype(jnp.bfloat16)
            low = (prod - high.astype(jnp.float32)).astype(jnp.bfloat16)
            part = lax.dot_general(
                high, right, (((1,), (1,)), ((), ())), preferred_element_type=jnp.float32
            ) + lax.dot_general(
                low, right, (((1,), (1,)), ((), ())), preferred_element_type=jnp.float32
            )
            total = part if total is None else total + part
        orbits = out.shape[-1]
        out[c, 0] = total[:, :orbits]
        out[c, 1] = total[:, orbits:]


def dressed(neighbours, grad, mixed_blocks):
    smem = pl.BlockSpec(memory_space=pltpu.SMEM)
    vmem = pl.BlockSpec(memory_space=pltpu.VMEM)
    return pl.pallas_call(
        dress_kernel,
        out_shape=jax.ShapeDtypeStruct(mixed_blocks.shape, jnp.float32),
        in_specs=[smem, vmem, vmem],
        out_specs=vmem,
    )(neighbours, grad, mixed_blocks)


def swap(x, axis):
    return lax.all_to_all(x, axis, split_axis=0, concat_axis=0, tiled=True)


def shards(green, grad, coupling, occupation, offsets, neighbours, qtable):
    clusters, parts, orbits = green.shape[2:5]
    momenta = lax.axis_size("mom")
    plane = lax.axis_size("y") * lax.axis_size("x") * lax.axis_size("core")
    quads = lax.axis_size("zh") * momenta
    rows = clusters * parts * orbits // plane
    quad = plane // momenta
    table = swap(jnp.broadcast_to(qtable, (momenta, momenta)), "mom")
    pieces = swap(green.reshape(plane, rows, orbits), PLANE)
    here = swap(pieces, "mom")
    before = lax.ppermute(here, LINE, [(z, z + 1) for z in range(quads - 1)])
    after = lax.ppermute(here, LINE, [(z + 1, z) for z in range(quads - 1)])
    shape = (momenta, quad, rows, orbits)
    total = mixed(
        coupling, occupation, offsets, table,
        before.reshape(shape), here.reshape(shape), after.reshape(shape),
    )
    total = swap(swap(total.reshape(plane, rows, orbits), "mom"), PLANE)
    out = dressed(neighbours, grad[0], total.reshape(clusters, parts, orbits, orbits))
    return out[None, None]


def solution(mesh):
    split = Mesh(mesh.devices.reshape(4, 4, 4, 2, 8), ("zh", "y", "x", "core", "mom"))
    energy = ("zh", "y", "x", "core")
    in_specs = (
        P("mom", energy, None, None, None, None),
        P("mom", None, None, None, None, None),
        P(),
        P(),
        P(),
        P(),
        P("mom", None),
    )
    out_specs = P("mom", energy, None, None, None, None)
    return jax.shard_map(shards, mesh=split, in_specs=in_specs, out_specs=out_specs, check_vma=False)
```

time: 415 us -> 117 us (0.28)
  the two profiles are of different devices: /device:TPU:768 before, /device:TPU:1 now
where the time goes in v1:
time: 117 us; the launch traced here: 116 us
  blocking collectives  59.9 us (51%)
  starting transfers between devices  29.7 us (25%)
  waiting for transfers between devices  16.8 us (14%)
  Pallas kernels  6.57 us (6%)
  local copies, waits for them, and re-layouts  3.41 us (3%)
    all_to_all x3, blocking collectives, swap(): return lax.all_to_all(x, axis, split_axis=0, concat_axis=0, tiled=True)  59.9 us
    all_to_all x2, starting transfers between devices, swap(): return lax.all_to_all(x, axis, split_axis=0, concat_axis=0, tiled=True)  23.5 us
    all_to_all x2, waiting for transfers between devices, swap(): return lax.all_to_all(x, axis, split_axis=0, concat_axis=0, tiled=True)  16.8 us
    ppermute x1, starting transfers between devices, shards(): before = lax.ppermute(here, LINE, [(z, z + 1) for z in range(quads - 1)])  4.93 us
    pallas_call x1, Pallas kernels, mixed(): pl.pallas_call(mix_kernel, out_shape=jax.ShapeDtypeStruct(here.shape, jnp...  3.43 us
    pallas_call x1, Pallas kernels, dressed(): pl.pallas_call(dress_kernel, out_shape=jax.ShapeDtypeStruct(mixed_blocks....  3.14 us
    unnamed x18, local copies, waits for them, and re-layouts  2.81 us
  transfers between devices with their start and end apart: 4, of which 2 were waited for; matrix products, arithmetic and copies ran while one was open for 2% of the time, Pallas kernels for 0%

profile of v1, /device:TPU:1, one launch (start us, length us, event | category | flops | bytes accessed | tf_op | source)
XLA Modules:
  0.0 116.5 jit_solution(8523543618851439428)
XLA Ops:
  0.0 26.6 %all_to_all.28 = bf16[32,32,128]{2,1,0:T(8,128)(2,1)S(1)} all-to-all(bf16[32,32,128]{2,1,0:T(8,128)(2,1)} %bitcast.16), channel_id=1, replica_groups=mesh['zh'=4,'y'=4,'x'=4,'core'=2,'mom'=8] {'y','x','core'}, dimensions={0} | all-to-all | bytes 524288 | tf_op jit(solution)/shard_map/all_to_all | solution.py:102
  26.6 17.3 %all_to_all.29 = bf16[32,32,128]{2,1,0:T(8,128)(2,1)S(1)} all-to-all(bf16[32,32,128]{2,1,0:T(8,128)(2,1)S(1)} %all_to_all.28), channel_id=1, replica_groups=mesh['zh'=4,'y'=4,'x'=4,'core'=2,'mom'=8] {'mom'}, dimensions={0} | all-to-all | bytes 524288 | tf_op jit(solution)/shard_map/all_to_all | solution.py:102
  43.9 0.0 copy-start
  43.9 0.0 copy-start.7
  43.9 4.9 %collective-permute-start = (bf16[32,32,128]{2,1,0:T(8,128)(2,1)S(1)}, bf16[32,32,128]{2,1,0:T(8,128)(2,1)S(1)}, u32[]{:S(2)}, u32[]{:S(2)}) collective-permute-start(bf16[32,32,128]{2,1,0:T(8,128)(2,1)S(1)} %all_to_all.29), channel_id=1, source_target_pairs={{0,1},{1,2},{2,3},{3,4},{4,5},{5,6},{6,7},{7,256},{256,257},{257,2... | collective-permute-start | bytes 786440 | tf_op jit(solution)/shard_map/ppermute | solution.py:115
  48.9 1.3 %collective-permute-start.1 = (bf16[32,32,128]{2,1,0:T(8,128)(2,1)S(1)}, bf16[32,32,128]{2,1,0:T(8,128)(2,1)S(1)}, u32[]{:S(2)}, u32[]{:S(2)}) collective-permute-start(bf16[32,32,128]{2,1,0:T(8,128)(2,1)S(1)} %all_to_all.29), channel_id=1, source_target_pairs={{1,0},{2,1},{3,2},{4,3},{5,4},{6,5},{7,6},{256,7},{257,256},{258,2... | collective-permute-start | bytes 786440 | tf_op jit(solution)/shard_map/ppermute | solution.py:116
  50.2 0.0 copy-done.7
  50.2 0.6 broadcast_in_dim.8
  50.8 0.0 copy-start.5
  50.8 12.9 %all-to-all-start = ((s32[8,1,8]{2,1,0:T(1,128)}), s32[8,1,8]{2,1,0:T(1,128)S(1)}, u32[]{:S(2)}, u32[]{:S(2)}) async-start(s32[8,1,8]{2,1,0:T(1,128)} %broadcast_in_dim.8), calls=%async_computation | async-start | bytes 8192 | tf_op jit(solution)/shard_map/all_to_all | solution.py:102
  63.7 0.0 copy-done.5
  63.7 0.7 copy.10.coupling
  64.4 8.5 %all-to-all-done = s32[8,1,8]{2,1,0:T(1,128)S(1)} async-done(((s32[8,1,8]{2,1,0:T(1,128)}), s32[8,1,8]{2,1,0:T(1,128)S(1)}, u32[]{:S(2)}, u32[]{:S(2)}) %all-to-all-start) | async-done | bytes 288 | tf_op jit(solution)/shard_map/all_to_all | solution.py:102
  72.9 0.0 copy-start.4
  72.9 0.0 collective-permute-done
  72.9 0.0 copy-start.2
  72.9 0.0 collective-permute-done.1
  72.9 0.0 copy-start.3
  72.9 0.0 copy-done
  73.0 0.6 copy-done.4
  73.5 0.1 copy-done.2
  73.6 0.1 copy-done.3
  73.7 3.4 %shard_map.76 = bf16[8,4,32,128]{3,2,1,0:T(8,128)(2,1)} custom-call(f32[8,4]{1,0:T(8,128)} %copy.10.coupling, f32[4]{0:T(128)} %occupation.1, s32[4]{0:T(128)} %offsets.1, s32[8,8]{1,0:T(8,128)} %bitcast.17, bf16[8,4,32,128]{3,2,1,0:T(8,128)(2,1)} %bitcast.14, bf16[8,4,32,128]{3,2,1,0:T(8,128)(2,1)} %bitcast.10, bf16[8,4,32,128]{3,2,1,0:T(8,128)(2,1)} %bitcast.15), custom_call_target="tpu_custom_call" | custom-call | tf_op jit(solution)/shard_map/pallas_call | solution.py:49
  77.1 16.0 %all_to_all.30 = bf16[32,32,128]{2,1,0:T(8,128)(2,1)} all-to-all(bf16[32,32,128]{2,1,0:T(8,128)(2,1)} %bitcast.12), channel_id=1, replica_groups=mesh['zh'=4,'y'=4,'x'=4,'core'=2,'mom'=8] {'mom'}, dimensions={0} | all-to-all | bytes 524288 | tf_op jit(solution)/shard_map/all_to_all | solution.py:102
  93.1 0.0 copy-start.6
  93.1 10.6 %all-to-all-start.4 = ((bf16[32,32,128]{2,1,0:T(8,128)(2,1)}), bf16[32,32,128]{2,1,0:T(8,128)(2,1)S(1)}, u32[]{:S(2)}, u32[]{:S(2)}) async-start(bf16[32,32,128]{2,1,0:T(8,128)(2,1)} %all_to_all.30), calls=%async_computation.4 | async-start | bytes 524288 | tf_op jit(solution)/shard_map/all_to_all | solution.py:102
  103.7 0.0 copy-done.6
  103.7 0.7 copy.11.neighbours
  104.3 8.3 %all-to-all-done.4 = bf16[32,32,128]{2,1,0:T(8,128)(2,1)S(1)} async-done(((bf16[32,32,128]{2,1,0:T(8,128)(2,1)}), bf16[32,32,128]{2,1,0:T(8,128)(2,1)S(1)}, u32[]{:S(2)}, u32[]{:S(2)}) %all-to-all-start.4) | async-done | bytes 262176 | tf_op jit(solution)/shard_map/all_to_all | solution.py:102
  112.7 0.0 copy-start.1
  112.7 0.7 copy-done.1
  113.3 3.1 %shard_map.77 = f32[4,2,128,128]{3,2,1,0:T(8,128)} custom-call(s32[4,2]{1,0:T(4,128)} %copy.11.neighbours, bf16[4,2,2,128,128]{4,3,2,1,0:T(8,128)(2,1)} %bitcast.13, bf16[4,2,128,128]{3,2,1,0:T(8,128)(2,1)} %bitcast.11), custom_call_target="tpu_custom_call" | custom-call | tf_op jit(solution)/shard_map/pallas_call | solution.py:93
Async XLA Ops:
  43.9 29.0 %copy-start = (bf16[32,32,128]{2,1,0:T(8,128)(2,1)}, bf16[32,32,128]{2,1,0:T(8,128)(2,1)S(1)}, u32[]{:S(2)}) copy-start(bf16[32,32,128]{2,1,0:T(8,128)(2,1)S(1)} %all_to_all.29) | copy-start | bytes 786436
  43.9 6.2 %copy-start.7 = (s32[1,8]{1,0:T(1,128)S(1)}, s32[1,8]{1,0:T(1,128)}, u32[]{:S(2)}) copy-start(s32[1,8]{1,0:T(1,128)} %param.13) | copy-start | bytes 100
  43.9 29.0 %collective-permute-start = (bf16[32,32,128]{2,1,0:T(8,128)(2,1)S(1)}, bf16[32,32,128]{2,1,0:T(8,128)(2,1)S(1)}, u32[]{:S(2)}, u32[]{:S(2)}) collective-permute-start(bf16[32,32,128]{2,1,0:T(8,128)(2,1)S(1)} %all_to_all.29), channel_id=1, source_target_pairs={{0,1},{1,2},{2,3},{3,4},{4,5},{5,6},{6,7},{7,256},{256,257},{257,2... | collective-permute-start | bytes 786440 | tf_op jit(solution)/shard_map/ppermute | solution.py:115
  48.9 24.0 %collective-permute-start.1 = (bf16[32,32,128]{2,1,0:T(8,128)(2,1)S(1)}, bf16[32,32,128]{2,1,0:T(8,128)(2,1)S(1)}, u32[]{:S(2)}, u32[]{:S(2)}) collective-permute-start(bf16[32,32,128]{2,1,0:T(8,128)(2,1)S(1)} %all_to_all.29), channel_id=1, source_target_pairs={{1,0},{2,1},{3,2},{4,3},{5,4},{6,5},{7,6},{256,7},{257,256},{258,2... | collective-permute-start | bytes 786440 | tf_op jit(solution)/shard_map/ppermute | solution.py:116
  50.8 13.0 %copy-start.5 = (f32[8,4]{0,1:T(4,128)S(1)}, f32[8,4]{0,1:T(4,128)}, u32[]{:S(2)}) copy-start(f32[8,4]{0,1:T(4,128)} %param.9) | copy-start | bytes 388
  50.8 22.1 %all-to-all-start = ((s32[8,1,8]{2,1,0:T(1,128)}), s32[8,1,8]{2,1,0:T(1,128)S(1)}, u32[]{:S(2)}, u32[]{:S(2)}) async-start(s32[8,1,8]{2,1,0:T(1,128)} %broadcast_in_dim.8), calls=%async_computation | async-start | bytes 8192 | tf_op jit(solution)/shard_map/all_to_all | solution.py:102
  72.9 0.6 copy-start.4
  72.9 0.7 copy-start.2
  72.9 0.8 copy-start.3
  93.1 10.6 %copy-start.6 = (s32[4,2]{0,1:T(2,128)S(1)}, s32[4,2]{0,1:T(2,128)}, u32[]{:S(2)}) copy-start(s32[4,2]{0,1:T(2,128)} %param.12) | copy-start | bytes 100
  93.1 19.5 %all-to-all-start.4 = ((bf16[32,32,128]{2,1,0:T(8,128)(2,1)}), bf16[32,32,128]{2,1,0:T(8,128)(2,1)S(1)}, u32[]{:S(2)}, u32[]{:S(2)}) async-start(bf16[32,32,128]{2,1,0:T(8,128)(2,1)} %all_to_all.30), calls=%async_computation.4 | async-start | bytes 524288 | tf_op jit(solution)/shard_map/all_to_all | solution.py:102
  112.7 0.7 copy-start.1

commit v2 on v1

v2 whole, which is shorter than its diff:
```python
import jax
import jax.numpy as jnp
from jax import lax
from jax.experimental import pallas as pl
from jax.experimental.pallas import tpu as pltpu
from jax.sharding import Mesh
from jax.sharding import PartitionSpec as P


PLANE = ("y", "x", "core")
LINE = ("zh", "mom")


def mix_kernel(coupling, occupation, offsets, table, before, here, after, out, window, terms, mixed, sems, done):
    momenta, quad = here.shape[:2]
    modes = occupation.shape[0]
    me = lax.axis_index("mom")
    copies = [
        pltpu.make_async_copy(source, window.at[:, pl.ds(n * quad, quad)], sems.at[n])
        for n, source in enumerate((before, here, after))
    ]
    for copy in copies:
        copy.start()
    for copy in copies:
        copy.wait()
    for m in range(modes):
        absorb = occupation[m]
        emit = 1.0 + absorb
        shift = offsets[m]
        for j in range(momenta):
            for i in range(quad):
                lower = window[j, quad + i - shift].astype(jnp.float32)
                upper = window[j, quad + i + shift].astype(jnp.float32)
                terms[m, j, i] = emit * lower + absorb * upper

    def one(k, carry):
        total = [jnp.zeros(here.shape[2:], jnp.float32) for _ in range(quad)]
        for j in range(momenta):
            row = table[k ^ me, j]
            for m in range(modes):
                weight = coupling[row, m]
                for i in range(quad):
                    total[i] = total[i] + weight * terms[m, j, i]
        for i in range(quad):
            mixed[k, i] = total[i].astype(mixed.dtype)
        return carry

    lax.fori_loop(0, momenta, one, 0)
    copy = pltpu.make_async_copy(mixed, out, done)
    copy.start()
    copy.wait()


def mixed(coupling, occupation, offsets, table, before, here, after):
    smem = pl.BlockSpec(memory_space=pltpu.SMEM)
    free = pl.BlockSpec(memory_space=pl.ANY)
    momenta, quad, rows, lanes = here.shape
    modes = occupation.shape[0]
    return pl.pallas_call(
        mix_kernel,
        out_shape=jax.ShapeDtypeStruct(here.shape, jnp.bfloat16),
        in_specs=[smem] * 4 + [free] * 3,
        out_specs=free,
        scratch_shapes=[
            pltpu.VMEM((momenta, 3 * quad, rows, lanes), jnp.bfloat16),
            pltpu.VMEM((modes, momenta, quad, rows, lanes), jnp.float32),
            pltpu.VMEM((momenta, quad, rows, lanes), jnp.bfloat16),
            pltpu.SemaphoreType.DMA((3,)),
            pltpu.SemaphoreType.DMA,
        ],
        compiler_params=pltpu.CompilerParams(vmem_limit_bytes=16 << 20),
    )(coupling, occupation, offsets, table, before, here, after)


def dress_kernel(neighbours, grad, mixed_in, out, near, slopes, result, sems, done):
    clusters, listed = grad.shape[:2]
    orbits = out.shape[-1]
    first = pltpu.make_async_copy(mixed_in, near, sems.at[clusters])
    copies = [pltpu.make_async_copy(grad.at[c], slopes.at[c], sems.at[c]) for c in range(clusters)]
    first.start()
    for copy in copies:
        copy.start()
    first.wait()
    results = []
    for c in range(clusters):
        copies[c].wait()
        total = None
        for s in range(listed):
            spot = neighbours[c, s]
            re = near[spot, 0]
            im = near[spot, 1]
            d_re = slopes[c, s, 0]
            d_im = slopes[c, s, 1]
            left = jnp.concatenate([d_re, d_im], axis=1)
            middle = jnp.concatenate(
                [jnp.concatenate([re, im], axis=1), jnp.concatenate([-im, re], axis=1)], axis=0
            )
            right = jnp.concatenate([left, jnp.concatenate([-d_im, d_re], axis=1)], axis=0)
            prod = jnp.dot(left, middle, preferred_element_type=jnp.float32)
            high = prod.astype(jnp.bfloat16)
            low = (prod - high.astype(jnp.float32)).astype(jnp.bfloat16)
            part = lax.dot_general(
                jnp.concatenate([high, low], axis=0),
                right,
                (((1,), (1,)), ((), ())),
                preferred_element_type=jnp.float32,
            )
            part = part[:orbits] + part[orbits:]
            total = part if total is None else total + part
        result[c, 0] = total[:, :orbits]
        result[c, 1] = total[:, orbits:]
        copy = pltpu.make_async_copy(result.at[c], out.at[c], done.at[c])
        copy.start()
        results.append(copy)
    for copy in results:
        copy.wait()


def dressed(neighbours, grad, mixed_blocks):
    smem = pl.BlockSpec(memory_space=pltpu.SMEM)
    free = pl.BlockSpec(memory_space=pl.ANY)
    clusters = grad.shape[0]
    return pl.pallas_call(
        dress_kernel,
        out_shape=jax.ShapeDtypeStruct(mixed_blocks.shape, jnp.float32),
        in_specs=[smem, free, free],
        out_specs=free,
        scratch_shapes=[
            pltpu.VMEM(mixed_blocks.shape, mixed_blocks.dtype),
            pltpu.VMEM(grad.shape, grad.dtype),
            pltpu.VMEM(mixed_blocks.shape, jnp.float32),
            pltpu.SemaphoreType.DMA((clusters + 1,)),
            pltpu.SemaphoreType.DMA((clusters,)),
        ],
        compiler_params=pltpu.CompilerParams(vmem_limit_bytes=16 << 20),
    )(neighbours, grad, mixed_blocks)


def swap(x, axis):
    return lax.all_to_all(x, axis, split_axis=0, concat_axis=0, tiled=True)


def paired(x, bit, momenta):
    other = lax.ppermute(x, "mom", [(k, k ^ bit) for k in range(momenta)])
    return jnp.concatenate([x, other])


def shards(green, grad, coupling, occupation, offsets, neighbours, qtable):
    clusters, parts, orbits = green.shape[2:5]
    momenta = lax.axis_size("mom")
    plane = lax.axis_size("y") * lax.axis_size("x") * lax.axis_size("core")
    quads = lax.axis_size("zh") * momenta
    rows = clusters * parts * orbits // plane
    quad = plane // momenta
    pieces = swap(green.reshape(plane, rows, orbits), PLANE)
    table = paired(qtable, 1, momenta)
    table = paired(table, 2, momenta)
    here = swap(pieces, "mom")
    table = paired(table, 4, momenta)
    before = lax.ppermute(here, LINE, [(z, z + 1) for z in range(quads - 1)])
    after = lax.ppermute(here, LINE, [(z + 1, z) for z in range(quads - 1)])
    shape = (momenta, quad, rows, orbits)
    total = mixed(
        coupling, occupation, offsets, table,
        before.reshape(shape), here.reshape(shape), after.reshape(shape),
    )
    total = swap(swap(total.reshape(plane, rows, orbits), "mom"), PLANE)
    out = dressed(neighbours, grad[0], total.reshape(clusters, parts, orbits, orbits))
    return out[None, None]


def solution(mesh):
    split = Mesh(mesh.devices.reshape(4, 4, 4, 2, 8), ("zh", "y", "x", "core", "mom"))
    energy = ("zh", "y", "x", "core")
    in_specs = (
        P("mom", energy, None, None, None, None),
        P("mom", None, None, None, None, None),
        P(),
        P(),
        P(),
        P(),
        P("mom", None),
    )
    out_specs = P("mom", energy, None, None, None, None)
    return jax.shard_map(shards, mesh=split, in_specs=in_specs, out_specs=out_specs, check_vma=False)
```

time: 117 us -> 116 us (level)
  blocking collectives: 59.9 us -> 49.8 us
  waiting for transfers between devices: 16.8 us -> 25.8 us
  starting transfers between devices: 29.7 us -> 32.6 us
  local copies, waits for them, and re-layouts: 3.41 us -> 0.85 us
    ppermute x0 -> x3, starting transfers between devices: none -> 12.1 us  [paired(): other = lax.ppermute(x, 'mom', [(k, k ^ bit) for k in range(momenta)])]
    all_to_all x3 -> x2, blocking collectives: 59.9 us -> 49.8 us  [swap(): return lax.all_to_all(x, axis, split_axis=0, concat_axis=0, tiled=True)]
    all_to_all x2, starting transfers between devices: 23.5 us -> 14.4 us  [swap(): return lax.all_to_all(x, axis, split_axis=0, concat_axis=0, tiled=True)]
    ppermute x0 -> x3, waiting for transfers between devices: none -> 5.59 us  [paired(): other = lax.ppermute(x, 'mom', [(k, k ^ bit) for k in range(momenta)])]
    all_to_all x2, waiting for transfers between devices: 16.8 us -> 20.2 us  [swap(): return lax.all_to_all(x, axis, split_axis=0, concat_axis=0, tiled=True)]
    unnamed x18 -> x14, local copies, waits for them, and re-layouts: 2.81 us -> 0.85 us
  transfers between devices with their start and end apart: 4 -> 7, of which waited for: 2 -> 4; matrix products, arithmetic and copies ran while one was open for 2% -> 0% of each run, Pallas kernels for 0% -> 0%
where the time goes in v2:
time: 116 us; the launch traced here: 115 us
  blocking collectives  49.8 us (43%)
  starting transfers between devices  32.6 us (28%)
  waiting for transfers between devices  25.8 us (22%)
  Pallas kernels  6.04 us (5%)
    all_to_all x2, blocking collectives, swap(): return lax.all_to_all(x, axis, split_axis=0, concat_axis=0, tiled=True)  49.8 us
    all_to_all x2, waiting for transfers between devices, swap(): return lax.all_to_all(x, axis, split_axis=0, concat_axis=0, tiled=True)  20.2 us
    all_to_all x2, starting transfers between devices, swap(): return lax.all_to_all(x, axis, split_axis=0, concat_axis=0, tiled=True)  14.4 us
    ppermute x3, starting transfers between devices, paired(): other = lax.ppermute(x, 'mom', [(k, k ^ bit) for k in range(momenta)])  12.1 us
    ppermute x3, waiting for transfers between devices, paired(): other = lax.ppermute(x, 'mom', [(k, k ^ bit) for k in range(momenta)])  5.59 us
    ppermute x1, starting transfers between devices, shards(): before = lax.ppermute(here, LINE, [(z, z + 1) for z in range(quads - 1)])  4.79 us
    pallas_call x1, Pallas kernels, dressed(): pl.pallas_call(dress_kernel, out_shape=jax.ShapeDtypeStruct(mixed_blocks....  3.64 us
    pallas_call x1, Pallas kernels, mixed(): pl.pallas_call(mix_kernel, out_shape=jax.ShapeDtypeStruct(here.shape, jnp...  2.4 us
  transfers between devices with their start and end apart: 7, of which 4 were waited for; matrix products, arithmetic and copies ran while one was open for 0% of the time, Pallas kernels for 0%

profile of v2, /device:TPU:1, one launch (start us, length us, event | category | flops | bytes accessed | tf_op | source)
XLA Modules:
  0.0 115.3 jit_solution(16416883416436839002)
XLA Ops:
  0.0 27.3 %all_to_all.20 = bf16[32,32,128]{2,1,0:T(8,128)(2,1)} all-to-all(bf16[32,32,128]{2,1,0:T(8,128)(2,1)} %bitcast.14), channel_id=1, replica_groups=mesh['zh'=4,'y'=4,'x'=4,'core'=2,'mom'=8] {'y','x','core'}, dimensions={0} | all-to-all | bytes 524288 | tf_op jit(solution)/shard_map/all_to_all | solution.py:140
  27.3 0.0 copy-start.3
  27.3 3.5 %all-to-all-start.1 = ((bf16[32,32,128]{2,1,0:T(8,128)(2,1)}), bf16[32,32,128]{2,1,0:T(8,128)(2,1)S(1)}, u32[]{:S(2)}, u32[]{:S(2)}) async-start(bf16[32,32,128]{2,1,0:T(8,128)(2,1)} %all_to_all.20), calls=%async_computation.1 | async-start | bytes 524288 | tf_op jit(solution)/shard_map/all_to_all | solution.py:140
  30.9 0.0 copy-done.3
  30.9 3.2 %collective-permute-start = (s32[1,8]{1,0:T(1,128)S(1)}, s32[1,8]{1,0:T(1,128)S(1)}, u32[]{:S(2)}, u32[]{:S(2)}) collective-permute-start(s32[1,8]{1,0:T(1,128)S(1)} %copy-done.3), channel_id=1, source_target_pairs={{0,1},{1,0},{2,3},{3,2},{4,5},{5,4},{6,7},{7,6},{8,9},{9,8},{10,11... | collective-permute-start | bytes 104 | tf_op jit(solution)/shard_map/ppermute | solution.py:144
  34.1 11.4 %all-to-all-done.1 = bf16[32,32,128]{2,1,0:T(8,128)(2,1)S(1)} async-done(((bf16[32,32,128]{2,1,0:T(8,128)(2,1)}), bf16[32,32,128]{2,1,0:T(8,128)(2,1)S(1)}, u32[]{:S(2)}, u32[]{:S(2)}) %all-to-all-start.1) | async-done | bytes 262176 | tf_op jit(solution)/shard_map/all_to_all | solution.py:140
  45.5 4.8 %collective-permute-start.3 = (bf16[32,32,128]{2,1,0:T(8,128)(2,1)S(1)}, bf16[32,32,128]{2,1,0:T(8,128)(2,1)S(1)}, u32[]{:S(2)}, u32[]{:S(2)}) collective-permute-start(bf16[32,32,128]{2,1,0:T(8,128)(2,1)S(1)} %all-to-all-done.1), channel_id=1, source_target_pairs={{0,1},{1,2},{2,3},{3,4},{4,5},{5,6},{6,7},{7,256},{256,257},{257,2... | collective-permute-start | bytes 786440 | tf_op jit(solution)/shard_map/ppermute | solution.py:160
  50.3 1.3 %collective-permute-start.4 = (bf16[32,32,128]{2,1,0:T(8,128)(2,1)S(1)}, bf16[32,32,128]{2,1,0:T(8,128)(2,1)S(1)}, u32[]{:S(2)}, u32[]{:S(2)}) collective-permute-start(bf16[32,32,128]{2,1,0:T(8,128)(2,1)S(1)} %all-to-all-done.1), channel_id=1, source_target_pairs={{1,0},{2,1},{3,2},{4,3},{5,4},{6,5},{7,6},{256,7},{257,256},{258,2... | collective-permute-start | bytes 786440 | tf_op jit(solution)/shard_map/ppermute | solution.py:161
  51.6 0.0 collective-permute-done
  51.7 0.0 copy-start.4
  51.7 3.7 %collective-permute-start.1 = (s32[2,8]{1,0:T(2,128)S(1)}, s32[2,8]{1,0:T(2,128)S(1)}, u32[]{:S(2)}, u32[]{:S(2)}) collective-permute-start(s32[2,8]{1,0:T(2,128)S(1)} %pad_add_fusion.2), channel_id=1, source_target_pairs={{0,2},{1,3},{2,0},{3,1},{4,6},{5,7},{6,4},{7,5},{8,10},{9,11},{10,... | collective-permute-start | bytes 200 | tf_op jit(solution)/shard_map/ppermute | solution.py:144
  55.4 2.6 %collective-permute-done.1 = s32[2,8]{1,0:T(2,128)S(1)} collective-permute-done((s32[2,8]{1,0:T(2,128)S(1)}, s32[2,8]{1,0:T(2,128)S(1)}, u32[]{:S(2)}, u32[]{:S(2)}) %collective-permute-start.1) | collective-permute-done | bytes 96 | tf_op jit(solution)/shard_map/ppermute | solution.py:144
  58.0 5.2 %collective-permute-start.2 = (s32[4,8]{1,0:T(4,128)S(1)}, s32[4,8]{1,0:T(4,128)S(1)}, u32[]{:S(2)}, u32[]{:S(2)}) collective-permute-start(s32[4,8]{1,0:T(4,128)S(1)} %pad_add_fusion.1), channel_id=1, source_target_pairs={{0,4},{1,5},{2,6},{3,7},{4,0},{5,1},{6,2},{7,3},{8,12},{9,13},{10,... | collective-permute-start | bytes 392 | tf_op jit(solution)/shard_map/ppermute | solution.py:144
  63.2 0.0 copy-done.4
  63.2 0.1 copy.8.coupling
  63.3 2.9 %collective-permute-done.2 = s32[4,8]{1,0:T(4,128)S(1)} collective-permute-done((s32[4,8]{1,0:T(4,128)S(1)}, s32[4,8]{1,0:T(4,128)S(1)}, u32[]{:S(2)}, u32[]{:S(2)}) %collective-permute-start.2) | collective-permute-done | bytes 160 | tf_op jit(solution)/shard_map/ppermute | solution.py:144
  66.3 0.0 collective-permute-done.3
  66.3 0.0 collective-permute-done.4
  66.3 0.0 copy-start.1
  66.3 0.0 copy-start.2
  66.3 0.6 copy-done.1
  67.0 0.0 copy-done.2
  67.0 2.4 %shard_map.73 = bf16[8,4,32,128]{3,2,1,0:T(8,128)(2,1)S(1)} custom-call(f32[8,4]{1,0:T(8,128)S(1)} %copy.8.coupling, f32[4]{0:T(128)S(1)} %copy-done.1, s32[4]{0:T(128)S(1)} %copy-done.2, s32[8,8]{1,0:T(8,128)S(1)} %pad_add_fusion.table, bf16[8,4,32,128]{3,2,1,0:T(8,128)(2,1)S(1)} %bitcast.12, bf16[8,4,32,128]{3,2,1,0:T(8,128)(2,1)S(1)} %bitcast.8, ...), custom_call_target="tpu_custom_call" | custom-call | tf_op jit(solution)/shard_map/pallas_call | solution.py:59
  69.4 0.0 copy-start
  69.4 22.5 %all_to_all.21 = bf16[32,32,128]{2,1,0:T(8,128)(2,1)} all-to-all(bf16[32,32,128]{2,1,0:T(8,128)(2,1)S(1)} %bitcast.10), channel_id=1, replica_groups=mesh['zh'=4,'y'=4,'x'=4,'core'=2,'mom'=8] {'mom'}, dimensions={0} | all-to-all | bytes 524288 | tf_op jit(solution)/shard_map/all_to_all | solution.py:140
  91.9 0.0 copy-start.5
  91.9 10.8 %all-to-all-start.3 = ((bf16[32,32,128]{2,1,0:T(8,128)(2,1)}), bf16[32,32,128]{2,1,0:T(8,128)(2,1)S(1)}, u32[]{:S(2)}, u32[]{:S(2)}) async-start(bf16[32,32,128]{2,1,0:T(8,128)(2,1)} %all_to_all.21), calls=%async_computation.3 | async-start | bytes 524288 | tf_op jit(solution)/shard_map/all_to_all | solution.py:140
  102.7 0.0 copy-done.5
  102.8 0.1 copy.9.neighbours
  102.8 8.8 %all-to-all-done.3 = bf16[32,32,128]{2,1,0:T(8,128)(2,1)S(1)} async-done(((bf16[32,32,128]{2,1,0:T(8,128)(2,1)}), bf16[32,32,128]{2,1,0:T(8,128)(2,1)S(1)}, u32[]{:S(2)}, u32[]{:S(2)}) %all-to-all-start.3) | async-done | bytes 262176 | tf_op jit(solution)/shard_map/all_to_all | solution.py:140
  111.7 0.0 copy-done
  111.7 3.6 %shard_map.74 = f32[4,2,128,128]{3,2,1,0:T(8,128)} custom-call(s32[4,2]{1,0:T(4,128)S(1)} %copy.9.neighbours, bf16[4,2,2,128,128]{4,3,2,1,0:T(8,128)(2,1)S(1)} %bitcast.11, bf16[4,2,128,128]{3,2,1,0:T(8,128)(2,1)S(1)} %bitcast.9), custom_call_target="tpu_custom_call" | custom-call | tf_op jit(solution)/shard_map/pallas_call | solution.py:123
  (3 shorter events, 0.0 us)
Async XLA Ops:
  27.3 3.6 %copy-start.3 = (s32[1,8]{1,0:T(1,128)S(1)}, s32[1,8]{1,0:T(1,128)}, u32[]{:S(2)}) copy-start(s32[1,8]{1,0:T(1,128)} %param.13) | copy-start | bytes 100
  27.3 18.2 %all-to-all-start.1 = ((bf16[32,32,128]{2,1,0:T(8,128)(2,1)}), bf16[32,32,128]{2,1,0:T(8,128)(2,1)S(1)}, u32[]{:S(2)}, u32[]{:S(2)}) async-start(bf16[32,32,128]{2,1,0:T(8,128)(2,1)} %all_to_all.20), calls=%async_computation.1 | async-start | bytes 524288 | tf_op jit(solution)/shard_map/all_to_all | solution.py:140
  30.9 20.8 %collective-permute-start = (s32[1,8]{1,0:T(1,128)S(1)}, s32[1,8]{1,0:T(1,128)S(1)}, u32[]{:S(2)}, u32[]{:S(2)}) collective-permute-start(s32[1,8]{1,0:T(1,128)S(1)} %copy-done.3), channel_id=1, source_target_pairs={{0,1},{1,0},{2,3},{3,2},{4,5},{5,4},{6,7},{7,6},{8,9},{9,8},{10,11... | collective-permute-start | bytes 104 | tf_op jit(solution)/shard_map/ppermute | solution.py:144
  45.5 20.8 %collective-permute-start.3 = (bf16[32,32,128]{2,1,0:T(8,128)(2,1)S(1)}, bf16[32,32,128]{2,1,0:T(8,128)(2,1)S(1)}, u32[]{:S(2)}, u32[]{:S(2)}) collective-permute-start(bf16[32,32,128]{2,1,0:T(8,128)(2,1)S(1)} %all-to-all-done.1), channel_id=1, source_target_pairs={{0,1},{1,2},{2,3},{3,4},{4,5},{5,6},{6,7},{7,256},{256,257},{257,2... | collective-permute-start | bytes 786440 | tf_op jit(solution)/shard_map/ppermute | solution.py:160
  50.3 16.0 %collective-permute-start.4 = (bf16[32,32,128]{2,1,0:T(8,128)(2,1)S(1)}, bf16[32,32,128]{2,1,0:T(8,128)(2,1)S(1)}, u32[]{:S(2)}, u32[]{:S(2)}) collective-permute-start(bf16[32,32,128]{2,1,0:T(8,128)(2,1)S(1)} %all-to-all-done.1), channel_id=1, source_target_pairs={{1,0},{2,1},{3,2},{4,3},{5,4},{6,5},{7,6},{256,7},{257,256},{258,2... | collective-permute-start | bytes 786440 | tf_op jit(solution)/shard_map/ppermute | solution.py:161
  51.7 11.6 %copy-start.4 = (f32[8,4]{0,1:T(4,128)S(1)}, f32[8,4]{0,1:T(4,128)}, u32[]{:S(2)}) copy-start(f32[8,4]{0,1:T(4,128)} %param.9) | copy-start | bytes 388
  51.7 6.4 %collective-permute-start.1 = (s32[2,8]{1,0:T(2,128)S(1)}, s32[2,8]{1,0:T(2,128)S(1)}, u32[]{:S(2)}, u32[]{:S(2)}) collective-permute-start(s32[2,8]{1,0:T(2,128)S(1)} %pad_add_fusion.2), channel_id=1, source_target_pairs={{0,2},{1,3},{2,0},{3,1},{4,6},{5,7},{6,4},{7,5},{8,10},{9,11},{10,... | collective-permute-start | bytes 200 | tf_op jit(solution)/shard_map/ppermute | solution.py:144
  58.0 8.2 %collective-permute-start.2 = (s32[4,8]{1,0:T(4,128)S(1)}, s32[4,8]{1,0:T(4,128)S(1)}, u32[]{:S(2)}, u32[]{:S(2)}) collective-permute-start(s32[4,8]{1,0:T(4,128)S(1)} %pad_add_fusion.1), channel_id=1, source_target_pairs={{0,4},{1,5},{2,6},{3,7},{4,0},{5,1},{6,2},{7,3},{8,12},{9,13},{10,... | collective-permute-start | bytes 392 | tf_op jit(solution)/shard_map/ppermute | solution.py:144
  66.3 0.7 copy-start.1
  66.3 0.7 copy-start.2
  69.4 42.3 %copy-start = (bf16[1,4,2,2,128,128]{5,4,3,2,1,0:T(8,128)(2,1)S(1)}, bf16[1,4,2,2,128,128]{5,4,3,2,1,0:T(8,128)(2,1)}, u32[]{:S(2)}) copy-start(bf16[1,4,2,2,128,128]{5,4,3,2,1,0:T(8,128)(2,1)} %param.8) | copy-start | bytes 1572868
  91.9 10.8 %copy-start.5 = (s32[4,2]{0,1:T(2,128)S(1)}, s32[4,2]{0,1:T(2,128)}, u32[]{:S(2)}) copy-start(s32[4,2]{0,1:T(2,128)} %param.12) | copy-start | bytes 100
  91.9 19.8 %all-to-all-start.3 = ((bf16[32,32,128]{2,1,0:T(8,128)(2,1)}), bf16[32,32,128]{2,1,0:T(8,128)(2,1)S(1)}, u32[]{:S(2)}, u32[]{:S(2)}) async-start(bf16[32,32,128]{2,1,0:T(8,128)(2,1)} %all_to_all.21), calls=%async_computation.3 | async-start | bytes 524288 | tf_op jit(solution)/shard_map/all_to_all | solution.py:140

commit v3 on v1

v3 whole, which is shorter than its diff:
```python
import jax
import jax.numpy as jnp
from jax import lax
from jax.experimental import pallas as pl
from jax.experimental.pallas import tpu as pltpu
from jax.sharding import Mesh
from jax.sharding import PartitionSpec as P


PLANE = ("y", "x", "core")
LINE = ("zh", "mom")


def mix_kernel(coupling, rates, table, before, here, after, out, terms):
    momenta, quad = here.shape[:2]
    modes = rates.shape[1]
    me = lax.axis_index("mom")

    def term(m, carry):
        emit = rates[0, m]
        absorb = rates[1, m]
        for level in range(1, quad + 1):

            @pl.when(table[momenta, m] == level)
            def _():
                for j in range(momenta):
                    for i in range(quad):
                        down = here[j, i - level] if i >= level else before[j, quad + i - level]
                        up = here[j, i + level] if i + level < quad else after[j, i + level - quad]
                        terms[m, j, i] = emit * down.astype(jnp.float32) + absorb * up.astype(jnp.float32)

        return carry

    lax.fori_loop(0, modes, term, 0)

    def one(k, carry):
        total = [jnp.zeros(here.shape[2:], jnp.float32) for _ in range(quad)]
        far = k ^ me
        spot = (far >> 2) + (far & 2) + ((far & 1) << 2)
        for j in range(momenta):
            row = table[spot, j]
            for m in range(modes):
                weight = coupling[row, m]
                for i in range(quad):
                    total[i] = total[i] + weight * terms[m, j, i]
        for i in range(quad):
            out[k, i] = total[i].astype(out.dtype)
        return carry

    lax.fori_loop(0, momenta, one, 0)


def mixed(coupling, rates, table, before, here, after):
    smem = pl.BlockSpec(memory_space=pltpu.SMEM)
    vmem = pl.BlockSpec(memory_space=pltpu.VMEM)
    momenta, quad, rows, lanes = here.shape
    modes = rates.shape[1]
    return pl.pallas_call(
        mix_kernel,
        out_shape=jax.ShapeDtypeStruct(here.shape, jnp.bfloat16),
        in_specs=[smem] * 3 + [vmem] * 3,
        out_specs=vmem,
        scratch_shapes=[pltpu.VMEM((modes, momenta, quad, rows, lanes), jnp.float32)],
        compiler_params=pltpu.CompilerParams(vmem_limit_bytes=16 << 20),
    )(coupling, rates, table, before, here, after)


def dress_kernel(neighbours, grad, near, out, result, done):
    clusters, listed = grad.shape[:2]
    orbits = out.shape[-1]
    copies = []
    for c in range(clusters):
        total = None
        for s in range(listed):
            spot = neighbours[c, s]
            re = near[spot, 0]
            im = near[spot, 1]
            d_re = grad[c, s, 0]
            d_im = grad[c, s, 1]
            left = jnp.concatenate([d_re, d_im], axis=1)
            middle = jnp.concatenate(
                [jnp.concatenate([re, im], axis=1), jnp.concatenate([-im, re], axis=1)], axis=0
            )
            right = jnp.concatenate([left, jnp.concatenate([-d_im, d_re], axis=1)], axis=0)
            prod = jnp.dot(left, middle, preferred_element_type=jnp.float32)
            high = prod.astype(jnp.bfloat16)
            low = (prod - high.astype(jnp.float32)).astype(jnp.bfloat16)
            part = lax.dot_general(
                jnp.concatenate([high, low], axis=0),
                right,
                (((1,), (1,)), ((), ())),
                preferred_element_type=jnp.float32,
            )
            part = part[:orbits] + part[orbits:]
            total = part if total is None else total + part
        result[c, 0] = total[:, :orbits]
        result[c, 1] = total[:, orbits:]
        copy = pltpu.make_async_copy(result.at[c], out.at[c], done.at[c])
        copy.start()
        copies.append(copy)
    for copy in copies:
        copy.wait()


def dressed(neighbours, grad, mixed_blocks):
    smem = pl.BlockSpec(memory_space=pltpu.SMEM)
    vmem = pl.BlockSpec(memory_space=pltpu.VMEM)
    clusters = grad.shape[0]
    return pl.pallas_call(
        dress_kernel,
        out_shape=jax.ShapeDtypeStruct(mixed_blocks.shape, jnp.float32),
        in_specs=[smem, vmem, vmem],
        out_specs=pl.BlockSpec(memory_space=pl.ANY),
        scratch_shapes=[
            pltpu.VMEM(mixed_blocks.shape, jnp.float32),
            pltpu.SemaphoreType.DMA((clusters,)),
        ],
        compiler_params=pltpu.CompilerParams(vmem_limit_bytes=16 << 20),
    )(neighbours, grad, mixed_blocks)


def swap(x, axis):
    return lax.all_to_all(x, axis, split_axis=0, concat_axis=0, tiled=True)


def paired(x, bit, momenta):
    other = lax.ppermute(x, "mom", [(k, k ^ bit) for k in range(momenta)])
    return jnp.concatenate([x, other])


def shards(green, grad, coupling, occupation, offsets, neighbours, qtable):
    clusters, parts, orbits = green.shape[2:5]
    momenta = lax.axis_size("mom")
    plane = lax.axis_size("y") * lax.axis_size("x") * lax.axis_size("core")
    quads = lax.axis_size("zh") * momenta
    rows = clusters * parts * orbits // plane
    quad = plane // momenta
    pieces = swap(green.reshape(plane, rows, orbits), PLANE)
    table = paired(qtable, 4, momenta)
    rates = jnp.stack([1.0 + occupation, occupation])
    here = swap(pieces, "mom")
    table = paired(table, 2, momenta)
    before = lax.ppermute(here, LINE, [(z, z + 1) for z in range(quads - 1)])
    after = lax.ppermute(here, LINE, [(z + 1, z) for z in range(quads - 1)])
    table = paired(table, 1, momenta)
    spread = jnp.pad(offsets, (0, momenta - offsets.shape[0]))
    table = jnp.concatenate([table, spread[None]])
    shape = (momenta, quad, rows, orbits)
    total = mixed(
        coupling, rates, table,
        before.reshape(shape), here.reshape(shape), after.reshape(shape),
    )
    total = swap(swap(total.reshape(plane, rows, orbits), "mom"), PLANE)
    out = dressed(neighbours, grad[0], total.reshape(clusters, parts, orbits, orbits))
    return out[None, None]


def solution(mesh):
    split = Mesh(mesh.devices.reshape(4, 4, 4, 2, 8), ("zh", "y", "x", "core", "mom"))
    energy = ("zh", "y", "x", "core")
    in_specs = (
        P("mom", energy, None, None, None, None),
        P("mom", None, None, None, None, None),
        P(),
        P(),
        P(),
        P(),
        P("mom", None),
    )
    out_specs = P("mom", energy, None, None, None, None)
    return jax.shard_map(shards, mesh=split, in_specs=in_specs, out_specs=out_specs, check_vma=False)
```

time: 117 us -> 110 us (0.940)
  blocking collectives: 59.9 us -> 49.9 us
  starting transfers between devices: 29.7 us -> 34.2 us
  waiting for transfers between devices: 16.8 us -> 20.3 us
  local copies, waits for them, and re-layouts: 3.41 us -> 0.24 us
  Pallas kernels: 6.57 us -> 4.68 us
    ppermute x0 -> x3, starting transfers between devices: none -> 13.7 us  [paired(): other = lax.ppermute(x, 'mom', [(k, k ^ bit) for k in range(momenta)])]
    all_to_all x3 -> x2, blocking collectives: 59.9 us -> 49.9 us  [swap(): return lax.all_to_all(x, axis, split_axis=0, concat_axis=0, tiled=True)]
    all_to_all x2, starting transfers between devices: 23.5 us -> 14.4 us  [swap(): return lax.all_to_all(x, axis, split_axis=0, concat_axis=0, tiled=True)]
    ppermute x0 -> x3, waiting for transfers between devices: none -> 4 us  [paired(): other = lax.ppermute(x, 'mom', [(k, k ^ bit) for k in range(momenta)])]
    unnamed x18 -> x14, local copies, waits for them, and re-layouts: 2.81 us -> 0.2 us
  transfers between devices with their start and end apart: 4 -> 7, of which waited for: 2 -> 4; matrix products, arithmetic and copies ran while one was open for 2% -> 0% of each run, Pallas kernels for 0% -> 0%
where the time goes in v3:
time: 110 us
  blocking collectives  49.9 us (45%)
  starting transfers between devices  34.2 us (31%)
  waiting for transfers between devices  20.3 us (18%)
  Pallas kernels  4.68 us (4%)
    all_to_all x2, blocking collectives, swap(): return lax.all_to_all(x, axis, split_axis=0, concat_axis=0, tiled=True)  49.9 us
    all_to_all x2, waiting for transfers between devices, swap(): return lax.all_to_all(x, axis, split_axis=0, concat_axis=0, tiled=True)  16.3 us
    all_to_all x2, starting transfers between devices, swap(): return lax.all_to_all(x, axis, split_axis=0, concat_axis=0, tiled=True)  14.4 us
    ppermute x3, starting transfers between devices, paired(): other = lax.ppermute(x, 'mom', [(k, k ^ bit) for k in range(momenta)])  13.7 us
    ppermute x1, starting transfers between devices, shards(): before = lax.ppermute(here, LINE, [(z, z + 1) for z in range(quads - 1)])  4.8 us
    ppermute x3, waiting for transfers between devices, paired(): other = lax.ppermute(x, 'mom', [(k, k ^ bit) for k in range(momenta)])  4 us
    pallas_call x1, Pallas kernels, mixed(): pl.pallas_call(mix_kernel, out_shape=jax.ShapeDtypeStruct(here.shape, jnp...  2.5 us
  transfers between devices with their start and end apart: 7, of which 4 were waited for; matrix products, arithmetic and copies ran while one was open for 0% of the time, Pallas kernels for 0%

profile of v3, /device:TPU:1, one launch (start us, length us, event | category | flops | bytes accessed | tf_op | source)
XLA Modules:
  0.0 109.5 jit_solution(10506821628871741450)
XLA Ops:
  0.0 27.3 %all_to_all.20 = bf16[32,32,128]{2,1,0:T(8,128)(2,1)} all-to-all(bf16[32,32,128]{2,1,0:T(8,128)(2,1)} %bitcast.19), channel_id=1, replica_groups=mesh['zh'=4,'y'=4,'x'=4,'core'=2,'mom'=8] {'y','x','core'}, dimensions={0} | all-to-all | bytes 524288 | tf_op jit(solution)/shard_map/all_to_all | solution.py:123
  27.3 0.0 copy-start.1
  27.3 0.0 copy-start.4
  27.3 3.5 %all-to-all-start.1 = ((bf16[32,32,128]{2,1,0:T(8,128)(2,1)}), bf16[32,32,128]{2,1,0:T(8,128)(2,1)S(1)}, u32[]{:S(2)}, u32[]{:S(2)}) async-start(bf16[32,32,128]{2,1,0:T(8,128)(2,1)} %all_to_all.20), calls=%async_computation.1 | async-start | bytes 524288 | tf_op jit(solution)/shard_map/all_to_all | solution.py:123
  30.9 0.0 copy-done.1
  30.9 7.2 %collective-permute-start = (s32[1,8]{1,0:T(1,128)S(1)}, s32[1,8]{1,0:T(1,128)S(1)}, u32[]{:S(2)}, u32[]{:S(2)}) collective-permute-start(s32[1,8]{1,0:T(1,128)S(1)} %copy-done.1), channel_id=1, source_target_pairs={{0,4},{1,5},{2,6},{3,7},{4,0},{5,1},{6,2},{7,3},{8,12},{9,13},{10,... | collective-permute-start | bytes 104 | tf_op jit(solution)/shard_map/ppermute | solution.py:127
  38.1 0.0 copy-done.4
  38.1 0.0 copy-start.5
  38.1 7.4 %all-to-all-done.1 = bf16[32,32,128]{2,1,0:T(8,128)(2,1)S(1)} async-done(((bf16[32,32,128]{2,1,0:T(8,128)(2,1)}), bf16[32,32,128]{2,1,0:T(8,128)(2,1)S(1)}, u32[]{:S(2)}, u32[]{:S(2)}) %all-to-all-start.1) | async-done | bytes 262176 | tf_op jit(solution)/shard_map/all_to_all | solution.py:123
  45.5 4.8 %collective-permute-start.3 = (bf16[32,32,128]{2,1,0:T(8,128)(2,1)S(1)}, bf16[32,32,128]{2,1,0:T(8,128)(2,1)S(1)}, u32[]{:S(2)}, u32[]{:S(2)}) collective-permute-start(bf16[32,32,128]{2,1,0:T(8,128)(2,1)S(1)} %all-to-all-done.1), channel_id=1, source_target_pairs={{0,1},{1,2},{2,3},{3,4},{4,5},{5,6},{6,7},{7,256},{256,257},{257,2... | collective-permute-start | bytes 786440 | tf_op jit(solution)/shard_map/ppermute | solution.py:143
  50.4 1.3 %collective-permute-start.4 = (bf16[32,32,128]{2,1,0:T(8,128)(2,1)S(1)}, bf16[32,32,128]{2,1,0:T(8,128)(2,1)S(1)}, u32[]{:S(2)}, u32[]{:S(2)}) collective-permute-start(bf16[32,32,128]{2,1,0:T(8,128)(2,1)S(1)} %all-to-all-done.1), channel_id=1, source_target_pairs={{1,0},{2,1},{3,2},{4,3},{5,4},{6,5},{7,6},{256,7},{257,256},{258,2... | collective-permute-start | bytes 786440 | tf_op jit(solution)/shard_map/ppermute | solution.py:144
  51.7 0.0 collective-permute-done
  51.7 3.7 %collective-permute-start.1 = (s32[2,8]{1,0:T(2,128)S(1)}, s32[2,8]{1,0:T(2,128)S(1)}, u32[]{:S(2)}, u32[]{:S(2)}) collective-permute-start(s32[2,8]{1,0:T(2,128)S(1)} %pad_add_fusion.1), channel_id=1, source_target_pairs={{0,2},{1,3},{2,0},{3,1},{4,6},{5,7},{6,4},{7,5},{8,10},{9,11},{10,... | collective-permute-start | bytes 200 | tf_op jit(solution)/shard_map/ppermute | solution.py:127
  55.4 0.0 copy-done.5
  55.4 0.0 copy-start.2
  55.4 2.6 %collective-permute-done.1 = s32[2,8]{1,0:T(2,128)S(1)} collective-permute-done((s32[2,8]{1,0:T(2,128)S(1)}, s32[2,8]{1,0:T(2,128)S(1)}, u32[]{:S(2)}, u32[]{:S(2)}) %collective-permute-start.1) | collective-permute-done | bytes 96 | tf_op jit(solution)/shard_map/ppermute | solution.py:127
  58.1 2.9 %collective-permute-start.2 = (s32[4,8]{1,0:T(4,128)S(1)}, s32[4,8]{1,0:T(4,128)S(1)}, u32[]{:S(2)}, u32[]{:S(2)}) collective-permute-start(s32[4,8]{1,0:T(4,128)S(1)} %pad_add_fusion), channel_id=1, source_target_pairs={{0,1},{1,0},{2,3},{3,2},{4,5},{5,4},{6,7},{7,6},{8,9},{9,8},{10,11... | collective-permute-start | bytes 392 | tf_op jit(solution)/shard_map/ppermute | solution.py:127
  60.9 0.0 copy-done.2
  60.9 0.1 copy.8.coupling
  61.0 1.4 %collective-permute-done.2 = s32[4,8]{1,0:T(4,128)S(1)} collective-permute-done((s32[4,8]{1,0:T(4,128)S(1)}, s32[4,8]{1,0:T(4,128)S(1)}, u32[]{:S(2)}, u32[]{:S(2)}) %collective-permute-start.2) | collective-permute-done | bytes 160 | tf_op jit(solution)/shard_map/ppermute | solution.py:127
  62.4 0.0 collective-permute-done.3
  62.4 0.0 collective-permute-done.4
  62.4 2.5 %shard_map.73 = bf16[8,4,32,128]{3,2,1,0:T(8,128)(2,1)S(1)} custom-call(f32[8,4]{1,0:T(8,128)S(1)} %copy.8.coupling, f32[2,4]{1,0:T(2,128)S(1)} %pad_maximum_fusion.rates, s32[9,8]{1,0:T(8,128)S(1)} %concatenate.13.table, bf16[8,4,32,128]{3,2,1,0:T(8,128)(2,1)S(1)} %bitcast.17, bf16[8,4,32,128]{3,2,1,0:T(8,128)(2,1)S(1)} %bitcast.13, ...), custom_call_target="tpu_custom_call" | custom-call | tf_op jit(solution)/shard_map/pallas_call | solution.py:58
  64.9 0.0 copy-start
  64.9 22.6 %all_to_all.21 = bf16[32,32,128]{2,1,0:T(8,128)(2,1)} all-to-all(bf16[32,32,128]{2,1,0:T(8,128)(2,1)S(1)} %bitcast.15), channel_id=1, replica_groups=mesh['zh'=4,'y'=4,'x'=4,'core'=2,'mom'=8] {'mom'}, dimensions={0} | all-to-all | bytes 524288 | tf_op jit(solution)/shard_map/all_to_all | solution.py:123
  87.6 0.0 copy-start.3
  87.6 10.8 %all-to-all-start.3 = ((bf16[32,32,128]{2,1,0:T(8,128)(2,1)}), bf16[32,32,128]{2,1,0:T(8,128)(2,1)S(1)}, u32[]{:S(2)}, u32[]{:S(2)}) async-start(bf16[32,32,128]{2,1,0:T(8,128)(2,1)} %all_to_all.21), calls=%async_computation.3 | async-start | bytes 524288 | tf_op jit(solution)/shard_map/all_to_all | solution.py:123
  98.4 0.0 copy-done.3
  98.4 0.1 copy.9.neighbours
  98.5 8.8 %all-to-all-done.3 = bf16[32,32,128]{2,1,0:T(8,128)(2,1)S(1)} async-done(((bf16[32,32,128]{2,1,0:T(8,128)(2,1)}), bf16[32,32,128]{2,1,0:T(8,128)(2,1)S(1)}, u32[]{:S(2)}, u32[]{:S(2)}) %all-to-all-start.3) | async-done | bytes 262176 | tf_op jit(solution)/shard_map/all_to_all | solution.py:123
  107.4 0.0 copy-done
  107.4 2.2 %shard_map.74 = f32[4,2,128,128]{3,2,1,0:T(8,128)} custom-call(s32[4,2]{1,0:T(4,128)S(1)} %copy.9.neighbours, bf16[4,2,2,128,128]{4,3,2,1,0:T(8,128)(2,1)S(1)} %bitcast.16, bf16[4,2,128,128]{3,2,1,0:T(8,128)(2,1)S(1)} %bitcast.14), custom_call_target="tpu_custom_call" | custom-call | tf_op jit(solution)/shard_map/pallas_call | solution.py:109
  (6 shorter events, 0.1 us)
Async XLA Ops:
  27.3 3.6 %copy-start.1 = (s32[1,8]{1,0:T(1,128)S(1)}, s32[1,8]{1,0:T(1,128)}, u32[]{:S(2)}) copy-start(s32[1,8]{1,0:T(1,128)} %param.13) | copy-start | bytes 100
  27.3 10.7 %copy-start.4 = (f32[4]{0:T(128)S(1)}, f32[4]{0:T(128)}, u32[]{:S(2)}) copy-start(f32[4]{0:T(128)} %param.10) | copy-start | bytes 52
  27.3 18.2 %all-to-all-start.1 = ((bf16[32,32,128]{2,1,0:T(8,128)(2,1)}), bf16[32,32,128]{2,1,0:T(8,128)(2,1)S(1)}, u32[]{:S(2)}, u32[]{:S(2)}) async-start(bf16[32,32,128]{2,1,0:T(8,128)(2,1)} %all_to_all.20), calls=%async_computation.1 | async-start | bytes 524288 | tf_op jit(solution)/shard_map/all_to_all | solution.py:123
  30.9 20.8 %collective-permute-start = (s32[1,8]{1,0:T(1,128)S(1)}, s32[1,8]{1,0:T(1,128)S(1)}, u32[]{:S(2)}, u32[]{:S(2)}) collective-permute-start(s32[1,8]{1,0:T(1,128)S(1)} %copy-done.1), channel_id=1, source_target_pairs={{0,4},{1,5},{2,6},{3,7},{4,0},{5,1},{6,2},{7,3},{8,12},{9,13},{10,... | collective-permute-start | bytes 104 | tf_op jit(solution)/shard_map/ppermute | solution.py:127
  38.1 17.3 %copy-start.5 = (s32[4]{0:T(128)S(1)}, s32[4]{0:T(128)}, u32[]{:S(2)}) copy-start(s32[4]{0:T(128)} %param.11) | copy-start | bytes 52
  45.5 16.9 %collective-permute-start.3 = (bf16[32,32,128]{2,1,0:T(8,128)(2,1)S(1)}, bf16[32,32,128]{2,1,0:T(8,128)(2,1)S(1)}, u32[]{:S(2)}, u32[]{:S(2)}) collective-permute-start(bf16[32,32,128]{2,1,0:T(8,128)(2,1)S(1)} %all-to-all-done.1), channel_id=1, source_target_pairs={{0,1},{1,2},{2,3},{3,4},{4,5},{5,6},{6,7},{7,256},{256,257},{257,2... | collective-permute-start | bytes 786440 | tf_op jit(solution)/shard_map/ppermute | solution.py:143
  50.4 12.1 %collective-permute-start.4 = (bf16[32,32,128]{2,1,0:T(8,128)(2,1)S(1)}, bf16[32,32,128]{2,1,0:T(8,128)(2,1)S(1)}, u32[]{:S(2)}, u32[]{:S(2)}) collective-permute-start(bf16[32,32,128]{2,1,0:T(8,128)(2,1)S(1)} %all-to-all-done.1), channel_id=1, source_target_pairs={{1,0},{2,1},{3,2},{4,3},{5,4},{6,5},{7,6},{256,7},{257,256},{258,2... | collective-permute-start | bytes 786440 | tf_op jit(solution)/shard_map/ppermute | solution.py:144
  51.7 6.4 %collective-permute-start.1 = (s32[2,8]{1,0:T(2,128)S(1)}, s32[2,8]{1,0:T(2,128)S(1)}, u32[]{:S(2)}, u32[]{:S(2)}) collective-permute-start(s32[2,8]{1,0:T(2,128)S(1)} %pad_add_fusion.1), channel_id=1, source_target_pairs={{0,2},{1,3},{2,0},{3,1},{4,6},{5,7},{6,4},{7,5},{8,10},{9,11},{10,... | collective-permute-start | bytes 200 | tf_op jit(solution)/shard_map/ppermute | solution.py:127
  55.4 5.5 %copy-start.2 = (f32[8,4]{0,1:T(4,128)S(1)}, f32[8,4]{0,1:T(4,128)}, u32[]{:S(2)}) copy-start(f32[8,4]{0,1:T(4,128)} %param.9) | copy-start | bytes 388
  58.1 4.3 %collective-permute-start.2 = (s32[4,8]{1,0:T(4,128)S(1)}, s32[4,8]{1,0:T(4,128)S(1)}, u32[]{:S(2)}, u32[]{:S(2)}) collective-permute-start(s32[4,8]{1,0:T(4,128)S(1)} %pad_add_fusion), channel_id=1, source_target_pairs={{0,1},{1,0},{2,3},{3,2},{4,5},{5,4},{6,7},{7,6},{8,9},{9,8},{10,11... | collective-permute-start | bytes 392 | tf_op jit(solution)/shard_map/ppermute | solution.py:127
  64.9 42.4 %copy-start = (bf16[1,4,2,2,128,128]{5,4,3,2,1,0:T(8,128)(2,1)S(1)}, bf16[1,4,2,2,128,128]{5,4,3,2,1,0:T(8,128)(2,1)}, u32[]{:S(2)}) copy-start(bf16[1,4,2,2,128,128]{5,4,3,2,1,0:T(8,128)(2,1)} %param.8) | copy-start | bytes 1572868
  87.6 10.8 %copy-start.3 = (s32[4,2]{0,1:T(2,128)S(1)}, s32[4,2]{0,1:T(2,128)}, u32[]{:S(2)}) copy-start(s32[4,2]{0,1:T(2,128)} %param.12) | copy-start | bytes 100
  87.6 19.8 %all-to-all-start.3 = ((bf16[32,32,128]{2,1,0:T(8,128)(2,1)}), bf16[32,32,128]{2,1,0:T(8,128)(2,1)S(1)}, u32[]{:S(2)}, u32[]{:S(2)}) async-start(bf16[32,32,128]{2,1,0:T(8,128)(2,1)} %all_to_all.21), calls=%async_computation.3 | async-start | bytes 524288 | tf_op jit(solution)/shard_map/all_to_all | solution.py:123

commit v4 on v3

--- a/solution.py
+++ b/solution.py
@@ -11,58 +11,65 @@
 LINE = ("zh", "mom")
 
 
-def mix_kernel(coupling, rates, table, before, here, after, out, terms):
-    momenta, quad = here.shape[:2]
-    modes = rates.shape[1]
+def mix_kernel(levels, table, before, here, after, out, rows_of):
+    momenta, quad, rows, lanes = here.shape
+    shifts = levels.shape[0]
+    half = rows // 2
+    height = momenta * half
     me = lax.axis_index("mom")
+    sublane = lax.broadcasted_iota(jnp.int32, (half, lanes), 0)
+    lane = lax.broadcasted_iota(jnp.int32, (half, lanes), 1)
+    diagonal = sublane == lax.rem(lane, half)
+    values = levels[...]
+    strengths = [jnp.broadcast_to(values[:, q : q + 1], (shifts, lanes)) for q in range(momenta)]
+    for i in range(momenta):
+        index = jnp.broadcast_to(table[i : i + 1], (shifts, lanes))
+        weight = jnp.zeros((shifts, lanes), jnp.float32)
+        for q, strength in enumerate(strengths):
+            weight = jnp.where(index == q, strength, weight)
+        high = weight.astype(jnp.bfloat16).astype(jnp.float32)
+        for n, part in enumerate((high, weight - high)):
+            for d in range(shifts):
+                spread = jnp.broadcast_to(part[d : d + 1], (half, lanes))
+                block = jnp.where(diagonal, spread, 0.0).astype(jnp.bfloat16)
+                start = n * height + i * half
+                rows_of[start : start + half, d * lanes : (d + 1) * lanes] = block
 
-    def term(m, carry):
-        emit = rates[0, m]
-        absorb = rates[1, m]
-        for level in range(1, quad + 1):
+    def near(j, e):
+        if e < 0:
+            block = before[j, e + quad]
+        elif e < quad:
+            block = here[j, e]
+        else:
+            block = after[j, e - quad]
+        return jnp.concatenate([block[:half], block[half:]], axis=1)
 
-            @pl.when(table[momenta, m] == level)
-            def _():
-                for j in range(momenta):
-                    for i in range(quad):
-                        down = here[j, i - level] if i >= level else before[j, quad + i - level]
-                        up = here[j, i + level] if i + level < quad else after[j, i + level - quad]
-                        terms[m, j, i] = emit * down.astype(jnp.float32) + absorb * up.astype(jnp.float32)
-
-        return carry
-
-    lax.fori_loop(0, modes, term, 0)
-
-    def one(k, carry):
-        total = [jnp.zeros(here.shape[2:], jnp.float32) for _ in range(quad)]
-        far = k ^ me
-        spot = (far >> 2) + (far & 2) + ((far & 1) << 2)
-        for j in range(momenta):
-            row = table[spot, j]
-            for m in range(modes):
-                weight = coupling[row, m]
-                for i in range(quad):
-                    total[i] = total[i] + weight * terms[m, j, i]
-        for i in range(quad):
-            out[k, i] = total[i].astype(out.dtype)
-        return carry
-
-    lax.fori_loop(0, momenta, one, 0)
+    spots = []
+    for i in range(momenta):
+        spots.append(((i & 1) << 1 | (i & 2) << 1 | (i & 4) >> 2) ^ me)
+    for e in range(quad):
+        blocks = [near(j, e - level) for level in range(1, quad + 1) for j in range(momenta)]
+        blocks += [near(j, e + level) for level in range(1, quad + 1) for j in range(momenta)]
+        both = jnp.dot(rows_of[...], jnp.concatenate(blocks, axis=0), preferred_element_type=jnp.float32)
+        total = (both[:height] + both[height:]).astype(out.dtype)
+        for i in range(momenta):
+            piece = total[i * half : (i + 1) * half]
+            out[spots[i], e, :half] = piece[:, :lanes]
+            out[spots[i], e, half:] = piece[:, lanes:]
 
 
-def mixed(coupling, rates, table, before, here, after):
-    smem = pl.BlockSpec(memory_space=pltpu.SMEM)
+def mixed(levels, table, before, here, after):
     vmem = pl.BlockSpec(memory_space=pltpu.VMEM)
-    momenta, quad, rows, lanes = here.shape
-    modes = rates.shape[1]
+    momenta, _, rows, lanes = here.shape
+    shifts = levels.shape[0]
     return pl.pallas_call(
         mix_kernel,
         out_shape=jax.ShapeDtypeStruct(here.shape, jnp.bfloat16),
-        in_specs=[smem] * 3 + [vmem] * 3,
+        in_specs=[vmem] * 5,
         out_specs=vmem,
-        scratch_shapes=[pltpu.VMEM((modes, momenta, quad, rows, lanes), jnp.float32)],
+        scratch_shapes=[pltpu.VMEM((momenta * rows, shifts * lanes), jnp.bfloat16)],
         compiler_params=pltpu.CompilerParams(vmem_limit_bytes=16 << 20),
-    )(coupling, rates, table, before, here, after)
+    )(levels, table, before, here, after)
 
 
 def dress_kernel(neighbours, grad, near, out, result, done):
@@ -135,21 +142,19 @@
     quads = lax.axis_size("zh") * momenta
     rows = clusters * parts * orbits // plane
     quad = plane // momenta
+    shape = (momenta, quad, rows, orbits)
     pieces = swap(green.reshape(plane, rows, orbits), PLANE)
-    table = paired(qtable, 4, momenta)
     rates = jnp.stack([1.0 + occupation, occupation])
+    level = jnp.arange(1, quad + 1, dtype=jnp.int32)
+    chosen = jnp.where(offsets == level[:, None], rates[:, None], 0.0)
+    levels = jnp.sum(chosen[:, :, None] * coupling, axis=-1).reshape(2 * quad, momenta)
+    table = paired(jnp.repeat(qtable, orbits // momenta, axis=1), 2, momenta)
     here = swap(pieces, "mom")
-    table = paired(table, 2, momenta)
+    table = paired(table, 4, momenta)
     before = lax.ppermute(here, LINE, [(z, z + 1) for z in range(quads - 1)])
     after = lax.ppermute(here, LINE, [(z + 1, z) for z in range(quads - 1)])
     table = paired(table, 1, momenta)
-    spread = jnp.pad(offsets, (0, momenta - offsets.shape[0]))
-    table = jnp.concatenate([table, spread[None]])
-    shape = (momenta, quad, rows, orbits)
-    total = mixed(
-        coupling, rates, table,
-        before.reshape(shape), here.reshape(shape), after.reshape(shape),
-    )
+    total = mixed(levels, table, before.reshape(shape), here.reshape(shape), after.reshape(shape))
     total = swap(swap(total.reshape(plane, rows, orbits), "mom"), PLANE)
     out = dressed(neighbours, grad[0], total.reshape(clusters, parts, orbits, orbits))
     return out[None, None]

time: 110 us -> 108 us (0.982)
  waiting for transfers between devices: 20.3 us -> 12.7 us
  blocking collectives: 49.9 us -> 54.5 us
  Pallas kernels: 4.68 us -> 2.97 us
  starting transfers between devices: 34.2 us -> 35.6 us
  local copies, waits for them, and re-layouts: 0.24 us -> 1.55 us
    all_to_all x2, waiting for transfers between devices: 16.3 us -> 8.77 us  [swap(): return lax.all_to_all(x, axis, split_axis=0, concat_axis=0, tiled=True)]
    ppermute x3, starting transfers between devices: 13.7 us -> 20.1 us  [paired(): other = lax.ppermute(x, 'mom', [(k, k ^ bit) for k in range(momenta)])]
    all_to_all x2, blocking collectives: 49.9 us -> 54.5 us  [swap(): return lax.all_to_all(x, axis, split_axis=0, concat_axis=0, tiled=True)]
    ppermute x1, starting transfers between devices: 4.8 us -> 1.31 us  [shards(): before = lax.ppermute(here, LINE, [(z, z + 1) for z in range(quads - 1)])]
    pallas_call x1, Pallas kernels: 2.5 us -> 0.79 us  [mixed(): pl.pallas_call(mix_kernel, out_shape=jax.ShapeDtypeStruct(here.shape, jnp...]
    all_to_all x2, starting transfers between devices: 14.4 us -> 12.9 us  [swap(): return lax.all_to_all(x, axis, split_axis=0, concat_axis=0, tiled=True)]
    unnamed x14 -> x13, local copies, waits for them, and re-layouts: 0.2 us -> 1.4 us
  transfers between devices with their start and end apart: 7 -> 7, of which waited for: 4 -> 3; matrix products, arithmetic and copies ran while one was open for 0% -> 0% of each run, Pallas kernels for 0% -> 0%
where the time goes in v4:
time: 108 us
  blocking collectives  54.5 us (50%)
  starting transfers between devices  35.6 us (33%)
  waiting for transfers between devices  12.7 us (12%)
  Pallas kernels  2.97 us (3%)
  local copies, waits for them, and re-layouts  1.55 us (1%)
    all_to_all x2, blocking collectives, swap(): return lax.all_to_all(x, axis, split_axis=0, concat_axis=0, tiled=True)  54.5 us
    ppermute x3, starting transfers between devices, paired(): other = lax.ppermute(x, 'mom', [(k, k ^ bit) for k in range(momenta)])  20.1 us
    all_to_all x2, starting transfers between devices, swap(): return lax.all_to_all(x, axis, split_axis=0, concat_axis=0, tiled=True)  12.9 us
    all_to_all x2, waiting for transfers between devices, swap(): return lax.all_to_all(x, axis, split_axis=0, concat_axis=0, tiled=True)  8.77 us
    ppermute x3, waiting for transfers between devices, paired(): other = lax.ppermute(x, 'mom', [(k, k ^ bit) for k in range(momenta)])  3.94 us
    pallas_call x1, Pallas kernels, dressed(): pl.pallas_call(dress_kernel, out_shape=jax.ShapeDtypeStruct(mixed_blocks....  2.18 us
  transfers between devices with their start and end apart: 7, of which 3 were waited for; matrix products, arithmetic and copies ran while one was open for 0% of the time, Pallas kernels for 0%

profile of v4, /device:TPU:1, one launch (start us, length us, event | category | flops | bytes accessed | tf_op | source)
XLA Modules:
  0.0 107.7 jit_solution(16637139581380573627)
XLA Ops:
  0.0 27.3 %all_to_all.20 = bf16[32,32,128]{2,1,0:T(8,128)(2,1)} all-to-all(bf16[32,32,128]{2,1,0:T(8,128)(2,1)} %bitcast.20), channel_id=1, replica_groups=mesh['zh'=4,'y'=4,'x'=4,'core'=2,'mom'=8] {'y','x','core'}, dimensions={0} | all-to-all | bytes 524288 | tf_op jit(solution)/shard_map/all_to_all | solution.py:130
  27.3 3.4 %all-to-all-start.1 = ((bf16[32,32,128]{2,1,0:T(8,128)(2,1)}), bf16[32,32,128]{2,1,0:T(8,128)(2,1)S(1)}, u32[]{:S(2)}, u32[]{:S(2)}) async-start(bf16[32,32,128]{2,1,0:T(8,128)(2,1)} %all_to_all.20), calls=%async_computation.1 | async-start | bytes 524288 | tf_op jit(solution)/shard_map/all_to_all | solution.py:130
  30.7 0.0 copy-start.3
  30.7 0.6 copy-done.3
  31.4 0.1 broadcast_in_dim.32
  31.5 0.1 broadcast_in_dim.33
  31.5 0.0 copy-start.4
  31.5 4.3 %collective-permute-start = (s32[1,128]{1,0:T(1,128)S(1)}, s32[1,128]{1,0:T(1,128)S(1)}, u32[]{:S(2)}, u32[]{:S(2)}) collective-permute-start(s32[1,128]{1,0:T(1,128)S(1)} %broadcast_in_dim.33), channel_id=1, source_target_pairs={{0,2},{1,3},{2,0},{3,1},{4,6},{5,7},{6,4},{7,5},{8,10},{9,11},{10,... | collective-permute-start | bytes 1544 | tf_op jit(solution)/shard_map/ppermute | solution.py:134
  35.9 0.0 copy-done.4
  35.9 0.0 copy-start.5
  35.9 0.6 copy-done.5
  36.5 0.1 broadcast_compare_fusion
  36.6 0.9 collective-permute-done
  37.5 11.8 %collective-permute-start.1 = (s32[2,128]{1,0:T(2,128)S(1)}, s32[2,128]{1,0:T(2,128)S(1)}, u32[]{:S(2)}, u32[]{:S(2)}) collective-permute-start(s32[2,128]{1,0:T(2,128)S(1)} %pad_add_fusion.2), channel_id=1, source_target_pairs={{0,4},{1,5},{2,6},{3,7},{4,0},{5,1},{6,2},{7,3},{8,12},{9,13},{10,... | collective-permute-start | bytes 3080 | tf_op jit(solution)/shard_map/ppermute | solution.py:134
  49.3 0.0 copy-start.1
  49.3 0.0 all-to-all-done.1
  49.3 1.3 %collective-permute-start.3 = (bf16[32,32,128]{2,1,0:T(8,128)(2,1)S(1)}, bf16[32,32,128]{2,1,0:T(8,128)(2,1)S(1)}, u32[]{:S(2)}, u32[]{:S(2)}) collective-permute-start(bf16[32,32,128]{2,1,0:T(8,128)(2,1)S(1)} %all-to-all-done.1), channel_id=1, source_target_pairs={{0,1},{1,2},{2,3},{3,4},{4,5},{5,6},{6,7},{7,256},{256,257},{257,2... | collective-permute-start | bytes 786440 | tf_op jit(solution)/shard_map/ppermute | solution.py:154
  50.7 1.3 %collective-permute-start.4 = (bf16[32,32,128]{2,1,0:T(8,128)(2,1)S(1)}, bf16[32,32,128]{2,1,0:T(8,128)(2,1)S(1)}, u32[]{:S(2)}, u32[]{:S(2)}) collective-permute-start(bf16[32,32,128]{2,1,0:T(8,128)(2,1)S(1)} %all-to-all-done.1), channel_id=1, source_target_pairs={{1,0},{2,1},{3,2},{4,3},{5,4},{6,5},{7,6},{256,7},{257,256},{258,2... | collective-permute-start | bytes 786440 | tf_op jit(solution)/shard_map/ppermute | solution.py:155
  52.0 0.0 collective-permute-done.1
  52.0 4.0 %collective-permute-start.2 = (s32[4,128]{1,0:T(4,128)S(1)}, s32[4,128]{1,0:T(4,128)S(1)}, u32[]{:S(2)}, u32[]{:S(2)}) collective-permute-start(s32[4,128]{1,0:T(4,128)S(1)} %pad_add_fusion.1), channel_id=1, source_target_pairs={{0,1},{1,0},{2,3},{3,2},{4,5},{5,4},{6,7},{7,6},{8,9},{9,8},{10,11... | collective-permute-start | bytes 6152 | tf_op jit(solution)/shard_map/ppermute | solution.py:134
  56.0 0.0 copy-done.1
  56.0 0.1 multiply_reduce_fusion
  56.1 3.1 %collective-permute-done.2 = s32[4,128]{1,0:T(4,128)S(1)} collective-permute-done((s32[4,128]{1,0:T(4,128)S(1)}, s32[4,128]{1,0:T(4,128)S(1)}, u32[]{:S(2)}, u32[]{:S(2)}) %collective-permute-start.2) | collective-permute-done | bytes 2080 | tf_op jit(solution)/shard_map/ppermute | solution.py:134
  59.2 0.0 collective-permute-done.3
  59.2 0.0 collective-permute-done.4
  59.2 0.8 shard_map.76
  60.0 0.0 copy-start
  60.0 27.2 %all_to_all.21 = bf16[32,32,128]{2,1,0:T(8,128)(2,1)} all-to-all(bf16[32,32,128]{2,1,0:T(8,128)(2,1)S(1)} %bitcast.15), channel_id=1, replica_groups=mesh['zh'=4,'y'=4,'x'=4,'core'=2,'mom'=8] {'mom'}, dimensions={0} | all-to-all | bytes 524288 | tf_op jit(solution)/shard_map/all_to_all | solution.py:130
  87.2 0.0 copy-start.2
  87.2 9.5 %all-to-all-start.3 = ((bf16[32,32,128]{2,1,0:T(8,128)(2,1)}), bf16[32,32,128]{2,1,0:T(8,128)(2,1)S(1)}, u32[]{:S(2)}, u32[]{:S(2)}) async-start(bf16[32,32,128]{2,1,0:T(8,128)(2,1)} %all_to_all.21), calls=%async_computation.3 | async-start | bytes 524288 | tf_op jit(solution)/shard_map/all_to_all | solution.py:130
  96.7 0.0 copy-done.2
  96.7 0.1 copy.10.neighbours
  96.8 8.8 %all-to-all-done.3 = bf16[32,32,128]{2,1,0:T(8,128)(2,1)S(1)} async-done(((bf16[32,32,128]{2,1,0:T(8,128)(2,1)}), bf16[32,32,128]{2,1,0:T(8,128)(2,1)S(1)}, u32[]{:S(2)}, u32[]{:S(2)}) %all-to-all-start.3) | async-done | bytes 262176 | tf_op jit(solution)/shard_map/all_to_all | solution.py:130
  105.5 0.0 copy-done
  105.5 2.2 %shard_map.77 = f32[4,2,128,128]{3,2,1,0:T(8,128)} custom-call(s32[4,2]{1,0:T(4,128)S(1)} %copy.10.neighbours, bf16[4,2,2,128,128]{4,3,2,1,0:T(8,128)(2,1)S(1)} %bitcast.16, bf16[4,2,128,128]{3,2,1,0:T(8,128)(2,1)S(1)} %bitcast.13), custom_call_target="tpu_custom_call" | custom-call | tf_op jit(solution)/shard_map/pallas_call | solution.py:116
  (7 shorter events, 0.0 us)
Async XLA Ops:
  27.3 22.0 %all-to-all-start.1 = ((bf16[32,32,128]{2,1,0:T(8,128)(2,1)}), bf16[32,32,128]{2,1,0:T(8,128)(2,1)S(1)}, u32[]{:S(2)}, u32[]{:S(2)}) async-start(bf16[32,32,128]{2,1,0:T(8,128)(2,1)} %all_to_all.20), calls=%async_computation.1 | async-start | bytes 524288 | tf_op jit(solution)/shard_map/all_to_all | solution.py:130
  30.7 0.7 copy-start.3
  31.5 4.3 %copy-start.4 = (f32[4]{0:T(128)S(1)}, f32[4]{0:T(128)}, u32[]{:S(2)}) copy-start(f32[4]{0:T(128)} %param.10) | copy-start | bytes 52
  31.5 5.9 %collective-permute-start = (s32[1,128]{1,0:T(1,128)S(1)}, s32[1,128]{1,0:T(1,128)S(1)}, u32[]{:S(2)}, u32[]{:S(2)}) collective-permute-start(s32[1,128]{1,0:T(1,128)S(1)} %broadcast_in_dim.33), channel_id=1, source_target_pairs={{0,2},{1,3},{2,0},{3,1},{4,6},{5,7},{6,4},{7,5},{8,10},{9,11},{10,... | collective-permute-start | bytes 1544 | tf_op jit(solution)/shard_map/ppermute | solution.py:134
  35.9 0.7 copy-start.5
  37.5 14.5 %collective-permute-start.1 = (s32[2,128]{1,0:T(2,128)S(1)}, s32[2,128]{1,0:T(2,128)S(1)}, u32[]{:S(2)}, u32[]{:S(2)}) collective-permute-start(s32[2,128]{1,0:T(2,128)S(1)} %pad_add_fusion.2), channel_id=1, source_target_pairs={{0,4},{1,5},{2,6},{3,7},{4,0},{5,1},{6,2},{7,3},{8,12},{9,13},{10,... | collective-permute-start | bytes 3080 | tf_op jit(solution)/shard_map/ppermute | solution.py:134
  49.3 6.7 %copy-start.1 = (f32[8,4]{0,1:T(4,128)S(1)}, f32[8,4]{0,1:T(4,128)}, u32[]{:S(2)}) copy-start(f32[8,4]{0,1:T(4,128)} %param.9) | copy-start | bytes 388
  49.3 9.8 %collective-permute-start.3 = (bf16[32,32,128]{2,1,0:T(8,128)(2,1)S(1)}, bf16[32,32,128]{2,1,0:T(8,128)(2,1)S(1)}, u32[]{:S(2)}, u32[]{:S(2)}) collective-permute-start(bf16[32,32,128]{2,1,0:T(8,128)(2,1)S(1)} %all-to-all-done.1), channel_id=1, source_target_pairs={{0,1},{1,2},{2,3},{3,4},{4,5},{5,6},{6,7},{7,256},{256,257},{257,2... | collective-permute-start | bytes 786440 | tf_op jit(solution)/shard_map/ppermute | solution.py:154
  50.7 8.5 %collective-permute-start.4 = (bf16[32,32,128]{2,1,0:T(8,128)(2,1)S(1)}, bf16[32,32,128]{2,1,0:T(8,128)(2,1)S(1)}, u32[]{:S(2)}, u32[]{:S(2)}) collective-permute-start(bf16[32,32,128]{2,1,0:T(8,128)(2,1)S(1)} %all-to-all-done.1), channel_id=1, source_target_pairs={{1,0},{2,1},{3,2},{4,3},{5,4},{6,5},{7,6},{256,7},{257,256},{258,2... | collective-permute-start | bytes 786440 | tf_op jit(solution)/shard_map/ppermute | solution.py:155
  52.0 7.2 %collective-permute-start.2 = (s32[4,128]{1,0:T(4,128)S(1)}, s32[4,128]{1,0:T(4,128)S(1)}, u32[]{:S(2)}, u32[]{:S(2)}) collective-permute-start(s32[4,128]{1,0:T(4,128)S(1)} %pad_add_fusion.1), channel_id=1, source_target_pairs={{0,1},{1,0},{2,3},{3,2},{4,5},{5,4},{6,7},{7,6},{8,9},{9,8},{10,11... | collective-permute-start | bytes 6152 | tf_op jit(solution)/shard_map/ppermute | solution.py:134
  60.0 45.5 %copy-start = (bf16[1,4,2,2,128,128]{5,4,3,2,1,0:T(8,128)(2,1)S(1)}, bf16[1,4,2,2,128,128]{5,4,3,2,1,0:T(8,128)(2,1)}, u32[]{:S(2)}) copy-start(bf16[1,4,2,2,128,128]{5,4,3,2,1,0:T(8,128)(2,1)} %param.8) | copy-start | bytes 1572868
  87.2 9.5 %copy-start.2 = (s32[4,2]{0,1:T(2,128)S(1)}, s32[4,2]{0,1:T(2,128)}, u32[]{:S(2)}) copy-start(s32[4,2]{0,1:T(2,128)} %param.12) | copy-start | bytes 100
  87.2 18.4 %all-to-all-start.3 = ((bf16[32,32,128]{2,1,0:T(8,128)(2,1)}), bf16[32,32,128]{2,1,0:T(8,128)(2,1)S(1)}, u32[]{:S(2)}, u32[]{:S(2)}) async-start(bf16[32,32,128]{2,1,0:T(8,128)(2,1)} %all_to_all.21), calls=%async_computation.3 | async-start | bytes 524288 | tf_op jit(solution)/shard_map/all_to_all | solution.py:130

commit v5 on v4

--- a/solution.py
+++ b/solution.py
@@ -22,8 +22,13 @@
     diagonal = sublane == lax.rem(lane, half)
     values = levels[...]
     strengths = [jnp.broadcast_to(values[:, q : q + 1], (shifts, lanes)) for q in range(momenta)]
+    rows_in = table[...]
+    owner = lax.broadcasted_iota(jnp.int32, (momenta, lanes), 1) // half
+    indices = jnp.zeros((momenta, lanes), jnp.int32)
+    for j in range(momenta):
+        indices = jnp.where(owner == j, jnp.broadcast_to(rows_in[:, j : j + 1], (momenta, lanes)), indices)
     for i in range(momenta):
-        index = jnp.broadcast_to(table[i : i + 1], (shifts, lanes))
+        index = jnp.broadcast_to(indices[i : i + 1], (shifts, lanes))
         weight = jnp.zeros((shifts, lanes), jnp.float32)
         for q, strength in enumerate(strengths):
             weight = jnp.where(index == q, strength, weight)
@@ -44,9 +49,6 @@
             block = after[j, e - quad]
         return jnp.concatenate([block[:half], block[half:]], axis=1)
 
-    spots = []
-    for i in range(momenta):
-        spots.append(((i & 1) << 1 | (i & 2) << 1 | (i & 4) >> 2) ^ me)
     for e in range(quad):
         blocks = [near(j, e - level) for level in range(1, quad + 1) for j in range(momenta)]
         blocks += [near(j, e + level) for level in range(1, quad + 1) for j in range(momenta)]
@@ -54,8 +56,8 @@
         total = (both[:height] + both[height:]).astype(out.dtype)
         for i in range(momenta):
             piece = total[i * half : (i + 1) * half]
-            out[spots[i], e, :half] = piece[:, :lanes]
-            out[spots[i], e, half:] = piece[:, lanes:]
+            out[me ^ i, e, :half] = piece[:, :lanes]
+            out[me ^ i, e, half:] = piece[:, lanes:]
 
 
 def mixed(levels, table, before, here, after):
@@ -130,9 +132,8 @@
     return lax.all_to_all(x, axis, split_axis=0, concat_axis=0, tiled=True)
 
 
-def paired(x, bit, momenta):
-    other = lax.ppermute(x, "mom", [(k, k ^ bit) for k in range(momenta)])
-    return jnp.concatenate([x, other])
+def crossed(x, bits, momenta):
+    return lax.ppermute(x, "mom", [(k, k ^ bits) for k in range(momenta)])
 
 
 def shards(green, grad, coupling, occupation, offsets, neighbours, qtable):
@@ -148,12 +149,14 @@
     level = jnp.arange(1, quad + 1, dtype=jnp.int32)
     chosen = jnp.where(offsets == level[:, None], rates[:, None], 0.0)
     levels = jnp.sum(chosen[:, :, None] * coupling, axis=-1).reshape(2 * quad, momenta)
-    table = paired(jnp.repeat(qtable, orbits // momenta, axis=1), 2, momenta)
+    rows_in = [qtable]
+    for bits in range(1, 4):
+        rows_in.append(crossed(qtable, bits, momenta))
+    near = jnp.concatenate(rows_in)
     here = swap(pieces, "mom")
-    table = paired(table, 4, momenta)
+    table = jnp.concatenate([near, crossed(near, 4, momenta)])
     before = lax.ppermute(here, LINE, [(z, z + 1) for z in range(quads - 1)])
     after = lax.ppermute(here, LINE, [(z + 1, z) for z in range(quads - 1)])
-    table = paired(table, 1, momenta)
     total = mixed(levels, table, before.reshape(shape), here.reshape(shape), after.reshape(shape))
     total = swap(swap(total.reshape(plane, rows, orbits), "mom"), PLANE)
     out = dressed(neighbours, grad[0], total.reshape(clusters, parts, orbits, orbits))

time: 108 us -> 107 us (level)
  waiting for transfers between devices: 12.7 us -> 17.6 us
  blocking collectives: 54.5 us -> 50.9 us
  starting transfers between devices: 35.6 us -> 33.6 us
    ppermute x3 -> x4, starting transfers between devices: 20.1 us -> 13.3 us  [crossed(): return lax.ppermute(x, 'mom', [(k, k ^ bits) for k in range(momenta)])]
    all_to_all x2, waiting for transfers between devices: 8.77 us -> 13.5 us  [swap(): return lax.all_to_all(x, axis, split_axis=0, concat_axis=0, tiled=True)]
    all_to_all x2, blocking collectives: 54.5 us -> 50.9 us  [swap(): return lax.all_to_all(x, axis, split_axis=0, concat_axis=0, tiled=True)]
    ppermute x1, starting transfers between devices: 1.31 us -> 4.79 us  [shards(): before = lax.ppermute(here, LINE, [(z, z + 1) for z in range(quads - 1)])]
    all_to_all x2, starting transfers between devices: 12.9 us -> 14.1 us  [swap(): return lax.all_to_all(x, axis, split_axis=0, concat_axis=0, tiled=True)]
    ppermute x3 -> x4, waiting for transfers between devices: 3.94 us -> 4.12 us  [crossed(): return lax.ppermute(x, 'mom', [(k, k ^ bits) for k in range(momenta)])]
  transfers between devices with their start and end apart: 7 -> 8, of which waited for: 3 -> 3; matrix products, arithmetic and copies ran while one was open for 0% -> 0% of each run, Pallas kernels for 0% -> 0%
where the time goes in v5:
time: 107 us; the launch traced here: 106 us
  blocking collectives  50.9 us (48%)
  starting transfers between devices  33.6 us (31%)
  waiting for transfers between devices  17.6 us (16%)
  Pallas kernels  2.97 us (3%)
    all_to_all x2, blocking collectives, swap(): return lax.all_to_all(x, axis, split_axis=0, concat_axis=0, tiled=True)  50.9 us
    all_to_all x2, starting transfers between devices, swap(): return lax.all_to_all(x, axis, split_axis=0, concat_axis=0, tiled=True)  14.1 us
    all_to_all x2, waiting for transfers between devices, swap(): return lax.all_to_all(x, axis, split_axis=0, concat_axis=0, tiled=True)  13.5 us
    ppermute x4, starting transfers between devices, crossed(): return lax.ppermute(x, 'mom', [(k, k ^ bits) for k in range(momenta)])  13.3 us
    ppermute x1, starting transfers between devices, shards(): before = lax.ppermute(here, LINE, [(z, z + 1) for z in range(quads - 1)])  4.79 us
    ppermute x4, waiting for transfers between devices, crossed(): return lax.ppermute(x, 'mom', [(k, k ^ bits) for k in range(momenta)])  4.12 us
    pallas_call x1, Pallas kernels, dressed(): pl.pallas_call(dress_kernel, out_shape=jax.ShapeDtypeStruct(mixed_blocks....  2.18 us
  transfers between devices with their start and end apart: 8, of which 3 were waited for; matrix products, arithmetic and copies ran while one was open for 0% of the time, Pallas kernels for 0%

profile of v5, /device:TPU:1, one launch (start us, length us, event | category | flops | bytes accessed | tf_op | source)
XLA Modules:
  0.0 106.2 jit_solution(2740744604621051474)
XLA Ops:
  0.0 27.3 %all_to_all.20 = bf16[32,32,128]{2,1,0:T(8,128)(2,1)} all-to-all(bf16[32,32,128]{2,1,0:T(8,128)(2,1)} %bitcast.19), channel_id=1, replica_groups=mesh['zh'=4,'y'=4,'x'=4,'core'=2,'mom'=8] {'y','x','core'}, dimensions={0} | all-to-all | bytes 524288 | tf_op jit(solution)/shard_map/all_to_all | solution.py:132
  27.3 0.0 copy-start.2
  27.3 3.5 %all-to-all-start.1 = ((bf16[32,32,128]{2,1,0:T(8,128)(2,1)}), bf16[32,32,128]{2,1,0:T(8,128)(2,1)S(1)}, u32[]{:S(2)}, u32[]{:S(2)}) async-start(bf16[32,32,128]{2,1,0:T(8,128)(2,1)} %all_to_all.20), calls=%async_computation.1 | async-start | bytes 524288 | tf_op jit(solution)/shard_map/all_to_all | solution.py:132
  30.9 0.0 copy-done.2
  30.9 0.0 copy-start.4
  30.9 3.4 %collective-permute-start = (s32[1,8]{1,0:T(1,128)S(1)}, s32[1,8]{1,0:T(1,128)S(1)}, u32[]{:S(2)}, u32[]{:S(2)}) collective-permute-start(s32[1,8]{1,0:T(1,128)S(1)} %copy-done.2), channel_id=1, source_target_pairs={{0,1},{1,0},{2,3},{3,2},{4,5},{5,4},{6,7},{7,6},{8,9},{9,8},{10,11... | collective-permute-start | bytes 104 | tf_op jit(solution)/shard_map/ppermute | solution.py:136
  34.3 4.0 %collective-permute-start.1 = (s32[1,8]{1,0:T(1,128)S(1)}, s32[1,8]{1,0:T(1,128)S(1)}, u32[]{:S(2)}, u32[]{:S(2)}) collective-permute-start(s32[1,8]{1,0:T(1,128)S(1)} %copy-done.2), channel_id=1, source_target_pairs={{0,2},{1,3},{2,0},{3,1},{4,6},{5,7},{6,4},{7,5},{8,10},{9,11},{10,... | collective-permute-start | bytes 104 | tf_op jit(solution)/shard_map/ppermute | solution.py:136
  38.3 1.9 %collective-permute-start.2 = (s32[1,8]{1,0:T(1,128)S(1)}, s32[1,8]{1,0:T(1,128)S(1)}, u32[]{:S(2)}, u32[]{:S(2)}) collective-permute-start(s32[1,8]{1,0:T(1,128)S(1)} %copy-done.2), channel_id=1, source_target_pairs={{0,3},{1,2},{2,1},{3,0},{4,7},{5,6},{6,5},{7,4},{8,11},{9,10},{10,... | collective-permute-start | bytes 104 | tf_op jit(solution)/shard_map/ppermute | solution.py:136
  40.2 0.0 copy-done.4
  40.2 0.0 copy-start.5
  40.3 0.6 copy-done.5
  40.9 0.1 broadcast_compare_fusion
  41.0 4.6 %all-to-all-done.1 = bf16[32,32,128]{2,1,0:T(8,128)(2,1)S(1)} async-done(((bf16[32,32,128]{2,1,0:T(8,128)(2,1)}), bf16[32,32,128]{2,1,0:T(8,128)(2,1)S(1)}, u32[]{:S(2)}, u32[]{:S(2)}) %all-to-all-start.1) | async-done | bytes 262176 | tf_op jit(solution)/shard_map/all_to_all | solution.py:132
  45.6 4.8 %collective-permute-start.4 = (bf16[32,32,128]{2,1,0:T(8,128)(2,1)S(1)}, bf16[32,32,128]{2,1,0:T(8,128)(2,1)S(1)}, u32[]{:S(2)}, u32[]{:S(2)}) collective-permute-start(bf16[32,32,128]{2,1,0:T(8,128)(2,1)S(1)} %all-to-all-done.1), channel_id=1, source_target_pairs={{0,1},{1,2},{2,3},{3,4},{4,5},{5,6},{6,7},{7,256},{256,257},{257,2... | collective-permute-start | bytes 786440 | tf_op jit(solution)/shard_map/ppermute | solution.py:158
  50.3 1.3 %collective-permute-start.5 = (bf16[32,32,128]{2,1,0:T(8,128)(2,1)S(1)}, bf16[32,32,128]{2,1,0:T(8,128)(2,1)S(1)}, u32[]{:S(2)}, u32[]{:S(2)}) collective-permute-start(bf16[32,32,128]{2,1,0:T(8,128)(2,1)S(1)} %all-to-all-done.1), channel_id=1, source_target_pairs={{1,0},{2,1},{3,2},{4,3},{5,4},{6,5},{7,6},{256,7},{257,256},{258,2... | collective-permute-start | bytes 786440 | tf_op jit(solution)/shard_map/ppermute | solution.py:159
  51.7 0.0 copy-start.1
  51.7 0.0 collective-permute-done
  51.7 0.0 collective-permute-done.1
  51.7 0.0 collective-permute-done.2
  51.7 4.0 %collective-permute-start.3 = (s32[4,8]{1,0:T(4,128)S(1)}, s32[4,8]{1,0:T(4,128)S(1)}, u32[]{:S(2)}, u32[]{:S(2)}) collective-permute-start(s32[4,8]{1,0:T(4,128)S(1)} %pad_add_fusion), channel_id=1, source_target_pairs={{0,4},{1,5},{2,6},{3,7},{4,0},{5,1},{6,2},{7,3},{8,12},{9,13},{10,... | collective-permute-start | bytes 392 | tf_op jit(solution)/shard_map/ppermute | solution.py:136
  55.8 0.0 copy-done.1
  55.8 0.1 multiply_reduce_fusion
  55.9 4.1 %collective-permute-done.3 = s32[4,8]{1,0:T(4,128)S(1)} collective-permute-done((s32[4,8]{1,0:T(4,128)S(1)}, s32[4,8]{1,0:T(4,128)S(1)}, u32[]{:S(2)}, u32[]{:S(2)}) %collective-permute-start.3) | collective-permute-done | bytes 160 | tf_op jit(solution)/shard_map/ppermute | solution.py:136
  60.0 0.0 collective-permute-done.4
  60.0 0.0 collective-permute-done.5
  60.0 0.8 shard_map.73
  60.8 0.0 copy-start
  60.8 23.6 %all_to_all.21 = bf16[32,32,128]{2,1,0:T(8,128)(2,1)} all-to-all(bf16[32,32,128]{2,1,0:T(8,128)(2,1)S(1)} %bitcast.14), channel_id=1, replica_groups=mesh['zh'=4,'y'=4,'x'=4,'core'=2,'mom'=8] {'mom'}, dimensions={0} | all-to-all | bytes 524288 | tf_op jit(solution)/shard_map/all_to_all | solution.py:132
  84.4 0.0 copy-start.3
  84.4 10.6 %all-to-all-start.3 = ((bf16[32,32,128]{2,1,0:T(8,128)(2,1)}), bf16[32,32,128]{2,1,0:T(8,128)(2,1)S(1)}, u32[]{:S(2)}, u32[]{:S(2)}) async-start(bf16[32,32,128]{2,1,0:T(8,128)(2,1)} %all_to_all.21), calls=%async_computation.3 | async-start | bytes 524288 | tf_op jit(solution)/shard_map/all_to_all | solution.py:132
  95.0 0.0 copy-done.3
  95.0 0.1 copy.10.neighbours
  95.1 8.9 %all-to-all-done.3 = bf16[32,32,128]{2,1,0:T(8,128)(2,1)S(1)} async-done(((bf16[32,32,128]{2,1,0:T(8,128)(2,1)}), bf16[32,32,128]{2,1,0:T(8,128)(2,1)S(1)}, u32[]{:S(2)}, u32[]{:S(2)}) %all-to-all-start.3) | async-done | bytes 262176 | tf_op jit(solution)/shard_map/all_to_all | solution.py:132
  104.0 0.0 copy-done
  104.0 2.2 %shard_map.74 = f32[4,2,128,128]{3,2,1,0:T(8,128)} custom-call(s32[4,2]{1,0:T(4,128)S(1)} %copy.10.neighbours, bf16[4,2,2,128,128]{4,3,2,1,0:T(8,128)(2,1)S(1)} %bitcast.15, bf16[4,2,128,128]{3,2,1,0:T(8,128)(2,1)S(1)} %bitcast.12), custom_call_target="tpu_custom_call" | custom-call | tf_op jit(solution)/shard_map/pallas_call | solution.py:118
  (6 shorter events, 0.1 us)
Async XLA Ops:
  27.3 3.6 %copy-start.2 = (s32[1,8]{1,0:T(1,128)S(1)}, s32[1,8]{1,0:T(1,128)}, u32[]{:S(2)}) copy-start(s32[1,8]{1,0:T(1,128)} %param.13) | copy-start | bytes 100
  27.3 18.2 %all-to-all-start.1 = ((bf16[32,32,128]{2,1,0:T(8,128)(2,1)}), bf16[32,32,128]{2,1,0:T(8,128)(2,1)S(1)}, u32[]{:S(2)}, u32[]{:S(2)}) async-start(bf16[32,32,128]{2,1,0:T(8,128)(2,1)} %all_to_all.20), calls=%async_computation.1 | async-start | bytes 524288 | tf_op jit(solution)/shard_map/all_to_all | solution.py:132
  30.9 9.4 %copy-start.4 = (f32[4]{0:T(128)S(1)}, f32[4]{0:T(128)}, u32[]{:S(2)}) copy-start(f32[4]{0:T(128)} %param.10) | copy-start | bytes 52
  30.9 20.8 %collective-permute-start = (s32[1,8]{1,0:T(1,128)S(1)}, s32[1,8]{1,0:T(1,128)S(1)}, u32[]{:S(2)}, u32[]{:S(2)}) collective-permute-start(s32[1,8]{1,0:T(1,128)S(1)} %copy-done.2), channel_id=1, source_target_pairs={{0,1},{1,0},{2,3},{3,2},{4,5},{5,4},{6,7},{7,6},{8,9},{9,8},{10,11... | collective-permute-start | bytes 104 | tf_op jit(solution)/shard_map/ppermute | solution.py:136
  34.3 17.4 %collective-permute-start.1 = (s32[1,8]{1,0:T(1,128)S(1)}, s32[1,8]{1,0:T(1,128)S(1)}, u32[]{:S(2)}, u32[]{:S(2)}) collective-permute-start(s32[1,8]{1,0:T(1,128)S(1)} %copy-done.2), channel_id=1, source_target_pairs={{0,2},{1,3},{2,0},{3,1},{4,6},{5,7},{6,4},{7,5},{8,10},{9,11},{10,... | collective-permute-start | bytes 104 | tf_op jit(solution)/shard_map/ppermute | solution.py:136
  38.3 13.4 %collective-permute-start.2 = (s32[1,8]{1,0:T(1,128)S(1)}, s32[1,8]{1,0:T(1,128)S(1)}, u32[]{:S(2)}, u32[]{:S(2)}) collective-permute-start(s32[1,8]{1,0:T(1,128)S(1)} %copy-done.2), channel_id=1, source_target_pairs={{0,3},{1,2},{2,1},{3,0},{4,7},{5,6},{6,5},{7,4},{8,11},{9,10},{10,... | collective-permute-start | bytes 104 | tf_op jit(solution)/shard_map/ppermute | solution.py:136
  40.2 0.7 copy-start.5
  45.6 14.5 %collective-permute-start.4 = (bf16[32,32,128]{2,1,0:T(8,128)(2,1)S(1)}, bf16[32,32,128]{2,1,0:T(8,128)(2,1)S(1)}, u32[]{:S(2)}, u32[]{:S(2)}) collective-permute-start(bf16[32,32,128]{2,1,0:T(8,128)(2,1)S(1)} %all-to-all-done.1), channel_id=1, source_target_pairs={{0,1},{1,2},{2,3},{3,4},{4,5},{5,6},{6,7},{7,256},{256,257},{257,2... | collective-permute-start | bytes 786440 | tf_op jit(solution)/shard_map/ppermute | solution.py:158
  50.3 9.7 %collective-permute-start.5 = (bf16[32,32,128]{2,1,0:T(8,128)(2,1)S(1)}, bf16[32,32,128]{2,1,0:T(8,128)(2,1)S(1)}, u32[]{:S(2)}, u32[]{:S(2)}) collective-permute-start(bf16[32,32,128]{2,1,0:T(8,128)(2,1)S(1)} %all-to-all-done.1), channel_id=1, source_target_pairs={{1,0},{2,1},{3,2},{4,3},{5,4},{6,5},{7,6},{256,7},{257,256},{258,2... | collective-permute-start | bytes 786440 | tf_op jit(solution)/shard_map/ppermute | solution.py:159
  51.7 4.1 %copy-start.1 = (f32[8,4]{0,1:T(4,128)S(1)}, f32[8,4]{0,1:T(4,128)}, u32[]{:S(2)}) copy-start(f32[8,4]{0,1:T(4,128)} %param.9) | copy-start | bytes 388
  51.7 8.3 %collective-permute-start.3 = (s32[4,8]{1,0:T(4,128)S(1)}, s32[4,8]{1,0:T(4,128)S(1)}, u32[]{:S(2)}, u32[]{:S(2)}) collective-permute-start(s32[4,8]{1,0:T(4,128)S(1)} %pad_add_fusion), channel_id=1, source_target_pairs={{0,4},{1,5},{2,6},{3,7},{4,0},{5,1},{6,2},{7,3},{8,12},{9,13},{10,... | collective-permute-start | bytes 392 | tf_op jit(solution)/shard_map/ppermute | solution.py:136
  60.8 43.2 %copy-start = (bf16[1,4,2,2,128,128]{5,4,3,2,1,0:T(8,128)(2,1)S(1)}, bf16[1,4,2,2,128,128]{5,4,3,2,1,0:T(8,128)(2,1)}, u32[]{:S(2)}) copy-start(bf16[1,4,2,2,128,128]{5,4,3,2,1,0:T(8,128)(2,1)} %param.8) | copy-start | bytes 1572868
  84.4 10.6 %copy-start.3 = (s32[4,2]{0,1:T(2,128)S(1)}, s32[4,2]{0,1:T(2,128)}, u32[]{:S(2)}) copy-start(s32[4,2]{0,1:T(2,128)} %param.12) | copy-start | bytes 100
  84.4 19.6 %all-to-all-start.3 = ((bf16[32,32,128]{2,1,0:T(8,128)(2,1)}), bf16[32,32,128]{2,1,0:T(8,128)(2,1)S(1)}, u32[]{:S(2)}, u32[]{:S(2)}) async-start(bf16[32,32,128]{2,1,0:T(8,128)(2,1)} %all_to_all.21), calls=%async_computation.3 | async-start | bytes 524288 | tf_op jit(solution)/shard_map/all_to_all | solution.py:132

commit v6 on v4

--- a/solution.py
+++ b/solution.py
@@ -11,65 +11,64 @@
 LINE = ("zh", "mom")
 
 
-def mix_kernel(levels, table, before, here, after, out, rows_of):
-    momenta, quad, rows, lanes = here.shape
+def mix_kernel(levels, before, here, after, out, rows_of):
+    momenta, quad, rows, lanes = out.shape
     shifts = levels.shape[0]
     half = rows // 2
     height = momenta * half
-    me = lax.axis_index("mom")
     sublane = lax.broadcasted_iota(jnp.int32, (half, lanes), 0)
     lane = lax.broadcasted_iota(jnp.int32, (half, lanes), 1)
     diagonal = sublane == lax.rem(lane, half)
     values = levels[...]
     strengths = [jnp.broadcast_to(values[:, q : q + 1], (shifts, lanes)) for q in range(momenta)]
-    for i in range(momenta):
-        index = jnp.broadcast_to(table[i : i + 1], (shifts, lanes))
+    for k in range(momenta):
+        index = here[k, quad * rows :].astype(jnp.float32)
         weight = jnp.zeros((shifts, lanes), jnp.float32)
         for q, strength in enumerate(strengths):
-            weight = jnp.where(index == q, strength, weight)
+            weight = jnp.where(index == float(q), strength, weight)
         high = weight.astype(jnp.bfloat16).astype(jnp.float32)
         for n, part in enumerate((high, weight - high)):
             for d in range(shifts):
                 spread = jnp.broadcast_to(part[d : d + 1], (half, lanes))
                 block = jnp.where(diagonal, spread, 0.0).astype(jnp.bfloat16)
-                start = n * height + i * half
+                start = n * height + k * half
                 rows_of[start : start + half, d * lanes : (d + 1) * lanes] = block
 
     def near(j, e):
         if e < 0:
-            block = before[j, e + quad]
+            source, e = before, e + quad
         elif e < quad:
-            block = here[j, e]
+            source = here
         else:
-            block = after[j, e - quad]
-        return jnp.concatenate([block[:half], block[half:]], axis=1)
+            source, e = after, e - quad
+        start = e * rows
+        return jnp.concatenate(
+            [source[j, start : start + half], source[j, start + half : start + rows]], axis=1
+        )
 
-    spots = []
-    for i in range(momenta):
-        spots.append(((i & 1) << 1 | (i & 2) << 1 | (i & 4) >> 2) ^ me)
     for e in range(quad):
         blocks = [near(j, e - level) for level in range(1, quad + 1) for j in range(momenta)]
         blocks += [near(j, e + level) for level in range(1, quad + 1) for j in range(momenta)]
         both = jnp.dot(rows_of[...], jnp.concatenate(blocks, axis=0), preferred_element_type=jnp.float32)
         total = (both[:height] + both[height:]).astype(out.dtype)
-        for i in range(momenta):
-            piece = total[i * half : (i + 1) * half]
-            out[spots[i], e, :half] = piece[:, :lanes]
-            out[spots[i], e, half:] = piece[:, lanes:]
+        for k in range(momenta):
+            piece = total[k * half : (k + 1) * half]
+            out[k, e, :half] = piece[:, :lanes]
+            out[k, e, half:] = piece[:, lanes:]
 
 
-def mixed(levels, table, before, here, after):
+def mixed(levels, before, here, after, shape):
     vmem = pl.BlockSpec(memory_space=pltpu.VMEM)
-    momenta, _, rows, lanes = here.shape
+    momenta, _, rows, lanes = shape
     shifts = levels.shape[0]
     return pl.pallas_call(
         mix_kernel,
-        out_shape=jax.ShapeDtypeStruct(here.shape, jnp.bfloat16),
-        in_specs=[vmem] * 5,
+        out_shape=jax.ShapeDtypeStruct(shape, jnp.bfloat16),
+        in_specs=[vmem] * 4,
         out_specs=vmem,
         scratch_shapes=[pltpu.VMEM((momenta * rows, shifts * lanes), jnp.bfloat16)],
         compiler_params=pltpu.CompilerParams(vmem_limit_bytes=16 << 20),
-    )(levels, table, before, here, after)
+    )(levels, before, here, after)
 
 
 def dress_kernel(neighbours, grad, near, out, result, done):
@@ -130,11 +129,6 @@
     return lax.all_to_all(x, axis, split_axis=0, concat_axis=0, tiled=True)
 
 
-def paired(x, bit, momenta):
-    other = lax.ppermute(x, "mom", [(k, k ^ bit) for k in range(momenta)])
-    return jnp.concatenate([x, other])
-
-
 def shards(green, grad, coupling, occupation, offsets, neighbours, qtable):
     clusters, parts, orbits = green.shape[2:5]
     momenta = lax.axis_size("mom")
@@ -148,13 +142,13 @@
     level = jnp.arange(1, quad + 1, dtype=jnp.int32)
     chosen = jnp.where(offsets == level[:, None], rates[:, None], 0.0)
     levels = jnp.sum(chosen[:, :, None] * coupling, axis=-1).reshape(2 * quad, momenta)
-    table = paired(jnp.repeat(qtable, orbits // momenta, axis=1), 2, momenta)
-    here = swap(pieces, "mom")
-    table = paired(table, 4, momenta)
+    row = jnp.repeat(qtable, orbits // momenta, axis=1).astype(green.dtype)
+    row = jnp.broadcast_to(row, (momenta, 2 * quad, orbits))
+    slabs = jnp.concatenate([pieces.reshape(momenta, quad * rows, orbits), row], axis=1)
+    here = swap(slabs, "mom")
     before = lax.ppermute(here, LINE, [(z, z + 1) for z in range(quads - 1)])
     after = lax.ppermute(here, LINE, [(z + 1, z) for z in range(quads - 1)])
-    table = paired(table, 1, momenta)
-    total = mixed(levels, table, before.reshape(shape), here.reshape(shape), after.reshape(shape))
+    total = mixed(levels, before, here, after, shape)
     total = swap(swap(total.reshape(plane, rows, orbits), "mom"), PLANE)
     out = dressed(neighbours, grad[0], total.reshape(clusters, parts, orbits, orbits))
     return out[None, None]

time: 108 us -> 106 us (0.981)
  blocking collectives: 54.5 us -> 24.5 us
  waiting for transfers between devices: 12.7 us -> 38.4 us
  starting transfers between devices: 35.6 us -> 37.1 us
    all_to_all x2 -> x1, blocking collectives: 54.5 us -> 24.5 us  [swap(): return lax.all_to_all(x, axis, split_axis=0, concat_axis=0, tiled=True)]
    all_to_all x2 -> x3, waiting for transfers between devices: 8.77 us -> 31.3 us  [swap(): return lax.all_to_all(x, axis, split_axis=0, concat_axis=0, tiled=True)]
    ppermute x3 -> x0, starting transfers between devices: 20.1 us -> none  [paired(): other = lax.ppermute(x, 'mom', [(k, k ^ bit) for k in range(momenta)])]
    all_to_all x2 -> x3, starting transfers between devices: 12.9 us -> 30.8 us  [swap(): return lax.all_to_all(x, axis, split_axis=0, concat_axis=0, tiled=True)]
    ppermute x3 -> x0, waiting for transfers between devices: 3.94 us -> none  [paired(): other = lax.ppermute(x, 'mom', [(k, k ^ bit) for k in range(momenta)])]
    ppermute x1, waiting for transfers between devices: 0.01 us -> 3.85 us  [shards(): after = lax.ppermute(here, LINE, [(z + 1, z) for z in range(quads - 1)])]
    ppermute x1, starting transfers between devices: 1.31 us -> 5 us  [shards(): before = lax.ppermute(here, LINE, [(z, z + 1) for z in range(quads - 1)])]
    ppermute x1, waiting for transfers between devices: 0.01 us -> 3.26 us  [shards(): before = lax.ppermute(here, LINE, [(z, z + 1) for z in range(quads - 1)])]
  transfers between devices with their start and end apart: 7 -> 5, of which waited for: 3 -> 5; matrix products, arithmetic and copies ran while one was open for 0% -> 0% of each run, Pallas kernels for 0% -> 0%
where the time goes in v6:
time: 106 us
  waiting for transfers between devices  38.4 us (36%)
  starting transfers between devices  37.1 us (35%)
  blocking collectives  24.5 us (23%)
  Pallas kernels  2.95 us (3%)
  local copies, waits for them, and re-layouts  1.56 us (1%)
    all_to_all x3, waiting for transfers between devices, swap(): return lax.all_to_all(x, axis, split_axis=0, concat_axis=0, tiled=True)  31.3 us
    all_to_all x3, starting transfers between devices, swap(): return lax.all_to_all(x, axis, split_axis=0, concat_axis=0, tiled=True)  30.8 us
    all_to_all x1, blocking collectives, swap(): return lax.all_to_all(x, axis, split_axis=0, concat_axis=0, tiled=True)  24.5 us
    ppermute x1, starting transfers between devices, shards(): before = lax.ppermute(here, LINE, [(z, z + 1) for z in range(quads - 1)])  5 us
    ppermute x1, waiting for transfers between devices, shards(): after = lax.ppermute(here, LINE, [(z + 1, z) for z in range(quads - 1)])  3.85 us
    ppermute x1, waiting for transfers between devices, shards(): before = lax.ppermute(here, LINE, [(z, z + 1) for z in range(quads - 1)])  3.26 us
    pallas_call x1, Pallas kernels, dressed(): pl.pallas_call(dress_kernel, out_shape=jax.ShapeDtypeStruct(mixed_blocks....  2.18 us
  transfers between devices with their start and end apart: 5, of which 5 were waited for; matrix products, arithmetic and copies ran while one was open for 0% of the time, Pallas kernels for 0%

profile of v6, /device:TPU:1, one launch (start us, length us, event | category | flops | bytes accessed | tf_op | source)
XLA Modules:
  0.0 105.5 jit_solution(12804764825487254336)
XLA Ops:
  0.0 0.0 copy-start.4
  0.0 17.8 %all-to-all-start = ((bf16[32,32,128]{2,1,0:T(8,128)(2,1)}), bf16[32,32,128]{2,1,0:T(8,128)(2,1)S(1)}, u32[]{:S(2)}, u32[]{:S(2)}) async-start(bf16[32,32,128]{2,1,0:T(8,128)(2,1)} %bitcast.17), calls=%async_computation | async-start | bytes 524288 | tf_op jit(solution)/shard_map/all_to_all | solution.py:129
  17.8 0.0 copy-done.4
  17.8 0.1 broadcast_in_dim.35
  17.9 0.1 convert_element_type.15
  18.0 8.8 %all-to-all-done = bf16[32,32,128]{2,1,0:T(8,128)(2,1)S(1)} async-done(((bf16[32,32,128]{2,1,0:T(8,128)(2,1)}), bf16[32,32,128]{2,1,0:T(8,128)(2,1)S(1)}, u32[]{:S(2)}, u32[]{:S(2)}) %all-to-all-start) | async-done | bytes 262176 | tf_op jit(solution)/shard_map/all_to_all | solution.py:129
  26.8 0.7 pad_maximum_fusion
  27.5 3.4 %all-to-all-start.1 = ((bf16[8,136,128]{2,1,0:T(8,128)(2,1)}), bf16[8,136,128]{2,1,0:T(8,128)(2,1)S(1)}, u32[]{:S(2)}, u32[]{:S(2)}) async-start(bf16[8,136,128]{2,1,0:T(8,128)(2,1)} %pad_maximum_fusion), calls=%async_computation.1 | async-start | bytes 557056 | tf_op jit(solution)/shard_map/all_to_all | solution.py:129
  30.9 0.0 copy-start.3
  31.0 0.6 copy-done.3
  31.6 0.0 copy-start.5
  31.6 0.6 copy-done.5
  32.2 0.1 broadcast_compare_fusion
  32.3 0.0 copy-start.1
  32.3 13.7 %all-to-all-done.1.here = bf16[8,136,128]{2,1,0:T(8,128)(2,1)S(1)} async-done(((bf16[8,136,128]{2,1,0:T(8,128)(2,1)}), bf16[8,136,128]{2,1,0:T(8,128)(2,1)S(1)}, u32[]{:S(2)}, u32[]{:S(2)}) %all-to-all-start.1) | async-done | bytes 278560 | tf_op jit(solution)/shard_map/all_to_all | solution.py:129
  46.0 5.0 %collective-permute-start = (bf16[8,136,128]{2,1,0:T(8,128)(2,1)S(1)}, bf16[8,136,128]{2,1,0:T(8,128)(2,1)S(1)}, u32[]{:S(2)}, u32[]{:S(2)}) collective-permute-start(bf16[8,136,128]{2,1,0:T(8,128)(2,1)S(1)} %all-to-all-done.1.here), channel_id=1, source_target_pairs={{0,1},{1,2},{2,3},{3,4},{4,5},{5,6},{6,7},{7,256},{256,257},{257,2... | collective-permute-start | bytes 835592 | tf_op jit(solution)/shard_map/ppermute | solution.py:149
  51.1 1.3 %collective-permute-start.1 = (bf16[8,136,128]{2,1,0:T(8,128)(2,1)S(1)}, bf16[8,136,128]{2,1,0:T(8,128)(2,1)S(1)}, u32[]{:S(2)}, u32[]{:S(2)}) collective-permute-start(bf16[8,136,128]{2,1,0:T(8,128)(2,1)S(1)} %all-to-all-done.1.here), channel_id=1, source_target_pairs={{1,0},{2,1},{3,2},{4,3},{5,4},{6,5},{7,6},{256,7},{257,256},{258,2... | collective-permute-start | bytes 835592 | tf_op jit(solution)/shard_map/ppermute | solution.py:150
  52.4 0.0 copy-done.1
  52.4 0.1 multiply_reduce_fusion
  52.5 3.3 %collective-permute-done.before = bf16[8,136,128]{2,1,0:T(8,128)(2,1)S(1)} collective-permute-done((bf16[8,136,128]{2,1,0:T(8,128)(2,1)S(1)}, bf16[8,136,128]{2,1,0:T(8,128)(2,1)S(1)}, u32[]{:S(2)}, u32[]{:S(2)}) %collective-permute-start) | collective-permute-done | bytes 278560 | tf_op jit(solution)/shard_map/ppermute | solution.py:149
  55.7 3.8 %collective-permute-done.1.after = bf16[8,136,128]{2,1,0:T(8,128)(2,1)S(1)} collective-permute-done((bf16[8,136,128]{2,1,0:T(8,128)(2,1)S(1)}, bf16[8,136,128]{2,1,0:T(8,128)(2,1)S(1)}, u32[]{:S(2)}, u32[]{:S(2)}) %collective-permute-start.1) | collective-permute-done | bytes 278560 | tf_op jit(solution)/shard_map/ppermute | solution.py:150
  59.6 0.8 shard_map.73
  60.4 0.0 copy-start
  60.4 24.5 %all_to_all.20 = bf16[32,32,128]{2,1,0:T(8,128)(2,1)} all-to-all(bf16[32,32,128]{2,1,0:T(8,128)(2,1)S(1)} %bitcast.13), channel_id=1, replica_groups=mesh['zh'=4,'y'=4,'x'=4,'core'=2,'mom'=8] {'mom'}, dimensions={0} | all-to-all | bytes 524288 | tf_op jit(solution)/shard_map/all_to_all | solution.py:129
  84.8 0.0 copy-start.2
  84.8 9.6 %all-to-all-start.3 = ((bf16[32,32,128]{2,1,0:T(8,128)(2,1)}), bf16[32,32,128]{2,1,0:T(8,128)(2,1)S(1)}, u32[]{:S(2)}, u32[]{:S(2)}) async-start(bf16[32,32,128]{2,1,0:T(8,128)(2,1)} %all_to_all.20), calls=%async_computation.3 | async-start | bytes 524288 | tf_op jit(solution)/shard_map/all_to_all | solution.py:129
  94.5 0.0 copy-done.2
  94.5 0.1 copy.10.neighbours
  94.6 8.8 %all-to-all-done.3 = bf16[32,32,128]{2,1,0:T(8,128)(2,1)S(1)} async-done(((bf16[32,32,128]{2,1,0:T(8,128)(2,1)}), bf16[32,32,128]{2,1,0:T(8,128)(2,1)S(1)}, u32[]{:S(2)}, u32[]{:S(2)}) %all-to-all-start.3) | async-done | bytes 262176 | tf_op jit(solution)/shard_map/all_to_all | solution.py:129
  103.3 0.0 copy-done
  103.3 2.2 %shard_map.74 = f32[4,2,128,128]{3,2,1,0:T(8,128)} custom-call(s32[4,2]{1,0:T(4,128)S(1)} %copy.10.neighbours, bf16[4,2,2,128,128]{4,3,2,1,0:T(8,128)(2,1)S(1)} %bitcast.14, bf16[4,2,128,128]{3,2,1,0:T(8,128)(2,1)S(1)} %bitcast.12), custom_call_target="tpu_custom_call" | custom-call | tf_op jit(solution)/shard_map/pallas_call | solution.py:115
  (6 shorter events, 0.0 us)
Async XLA Ops:
  0.0 17.8 %copy-start.4 = (s32[1,8]{1,0:T(1,128)S(1)}, s32[1,8]{1,0:T(1,128)}, u32[]{:S(2)}) copy-start(s32[1,8]{1,0:T(1,128)} %param.13) | copy-start | bytes 100
  0.0 26.8 %all-to-all-start = ((bf16[32,32,128]{2,1,0:T(8,128)(2,1)}), bf16[32,32,128]{2,1,0:T(8,128)(2,1)S(1)}, u32[]{:S(2)}, u32[]{:S(2)}) async-start(bf16[32,32,128]{2,1,0:T(8,128)(2,1)} %bitcast.17), calls=%async_computation | async-start | bytes 524288 | tf_op jit(solution)/shard_map/all_to_all | solution.py:129
  27.5 18.5 %all-to-all-start.1 = ((bf16[8,136,128]{2,1,0:T(8,128)(2,1)}), bf16[8,136,128]{2,1,0:T(8,128)(2,1)S(1)}, u32[]{:S(2)}, u32[]{:S(2)}) async-start(bf16[8,136,128]{2,1,0:T(8,128)(2,1)} %pad_maximum_fusion), calls=%async_computation.1 | async-start | bytes 557056 | tf_op jit(solution)/shard_map/all_to_all | solution.py:129
  30.9 0.7 copy-start.3
  31.6 0.7 copy-start.5
  32.3 20.1 %copy-start.1 = (f32[8,4]{0,1:T(4,128)S(1)}, f32[8,4]{0,1:T(4,128)}, u32[]{:S(2)}) copy-start(f32[8,4]{0,1:T(4,128)} %param.9) | copy-start | bytes 388
  46.0 9.7 %collective-permute-start = (bf16[8,136,128]{2,1,0:T(8,128)(2,1)S(1)}, bf16[8,136,128]{2,1,0:T(8,128)(2,1)S(1)}, u32[]{:S(2)}, u32[]{:S(2)}) collective-permute-start(bf16[8,136,128]{2,1,0:T(8,128)(2,1)S(1)} %all-to-all-done.1.here), channel_id=1, source_target_pairs={{0,1},{1,2},{2,3},{3,4},{4,5},{5,6},{6,7},{7,256},{256,257},{257,2... | collective-permute-start | bytes 835592 | tf_op jit(solution)/shard_map/ppermute | solution.py:149
  51.1 8.5 %collective-permute-start.1 = (bf16[8,136,128]{2,1,0:T(8,128)(2,1)S(1)}, bf16[8,136,128]{2,1,0:T(8,128)(2,1)S(1)}, u32[]{:S(2)}, u32[]{:S(2)}) collective-permute-start(bf16[8,136,128]{2,1,0:T(8,128)(2,1)S(1)} %all-to-all-done.1.here), channel_id=1, source_target_pairs={{1,0},{2,1},{3,2},{4,3},{5,4},{6,5},{7,6},{256,7},{257,256},{258,2... | collective-permute-start | bytes 835592 | tf_op jit(solution)/shard_map/ppermute | solution.py:150
  60.4 43.0 %copy-start = (bf16[1,4,2,2,128,128]{5,4,3,2,1,0:T(8,128)(2,1)S(1)}, bf16[1,4,2,2,128,128]{5,4,3,2,1,0:T(8,128)(2,1)}, u32[]{:S(2)}) copy-start(bf16[1,4,2,2,128,128]{5,4,3,2,1,0:T(8,128)(2,1)} %param.8) | copy-start | bytes 1572868
  84.8 9.6 %copy-start.2 = (s32[4,2]{0,1:T(2,128)S(1)}, s32[4,2]{0,1:T(2,128)}, u32[]{:S(2)}) copy-start(s32[4,2]{0,1:T(2,128)} %param.12) | copy-start | bytes 100
  84.8 18.5 %all-to-all-start.3 = ((bf16[32,32,128]{2,1,0:T(8,128)(2,1)}), bf16[32,32,128]{2,1,0:T(8,128)(2,1)S(1)}, u32[]{:S(2)}, u32[]{:S(2)}) async-start(bf16[32,32,128]{2,1,0:T(8,128)(2,1)} %all_to_all.20), calls=%async_computation.3 | async-start | bytes 524288 | tf_op jit(solution)/shard_map/all_to_all | solution.py:129

commit v7 on v6

--- a/solution.py
+++ b/solution.py
@@ -16,13 +16,22 @@
     shifts = levels.shape[0]
     half = rows // 2
     height = momenta * half
+    body = momenta * quad * rows
+    me = lax.axis_index("mom")
     sublane = lax.broadcasted_iota(jnp.int32, (half, lanes), 0)
     lane = lax.broadcasted_iota(jnp.int32, (half, lanes), 1)
     diagonal = sublane == lax.rem(lane, half)
     values = levels[...]
     strengths = [jnp.broadcast_to(values[:, q : q + 1], (shifts, lanes)) for q in range(momenta)]
-    for k in range(momenta):
-        index = here[k, quad * rows :].astype(jnp.float32)
+    own = here[body:].astype(jnp.float32)
+    lower = before[body:].astype(jnp.float32)
+    upper = after[body:].astype(jnp.float32)
+    odd = jnp.zeros(own.shape, jnp.int32) + (me & 1)
+    partner = jnp.where(odd == 1, lower, upper)
+    for i in range(momenta):
+        table = partner if i >= momenta // 2 else own
+        spot = i % (momenta // 2)
+        index = jnp.broadcast_to(table[spot : spot + 1], (shifts, lanes))
         weight = jnp.zeros((shifts, lanes), jnp.float32)
         for q, strength in enumerate(strengths):
             weight = jnp.where(index == float(q), strength, weight)
@@ -31,7 +40,7 @@
             for d in range(shifts):
                 spread = jnp.broadcast_to(part[d : d + 1], (half, lanes))
                 block = jnp.where(diagonal, spread, 0.0).astype(jnp.bfloat16)
-                start = n * height + k * half
+                start = n * height + i * half
                 rows_of[start : start + half, d * lanes : (d + 1) * lanes] = block
 
     def near(j, e):
@@ -41,20 +50,19 @@
             source = here
         else:
             source, e = after, e - quad
-        start = e * rows
-        return jnp.concatenate(
-            [source[j, start : start + half], source[j, start + half : start + rows]], axis=1
-        )
+        start = (j * quad + e) * rows
+        return jnp.concatenate([source[start : start + half], source[start + half : start + rows]], axis=1)
 
+    spots = [((i & 1) << 1 | (i & 2) << 1 | (i & 4) >> 2) ^ me for i in range(momenta)]
     for e in range(quad):
         blocks = [near(j, e - level) for level in range(1, quad + 1) for j in range(momenta)]
         blocks += [near(j, e + level) for level in range(1, quad + 1) for j in range(momenta)]
         both = jnp.dot(rows_of[...], jnp.concatenate(blocks, axis=0), preferred_element_type=jnp.float32)
         total = (both[:height] + both[height:]).astype(out.dtype)
-        for k in range(momenta):
-            piece = total[k * half : (k + 1) * half]
-            out[k, e, :half] = piece[:, :lanes]
-            out[k, e, half:] = piece[:, lanes:]
+        for i in range(momenta):
+            piece = total[i * half : (i + 1) * half]
+            out[spots[i], e, :half] = piece[:, :lanes]
+            out[spots[i], e, half:] = piece[:, lanes:]
 
 
 def mixed(levels, before, here, after, shape):
@@ -129,6 +137,11 @@
     return lax.all_to_all(x, axis, split_axis=0, concat_axis=0, tiled=True)
 
 
+def paired(x, bit, momenta):
+    other = lax.ppermute(x, "mom", [(k, k ^ bit) for k in range(momenta)])
+    return jnp.concatenate([x, other])
+
+
 def shards(green, grad, coupling, occupation, offsets, neighbours, qtable):
     clusters, parts, orbits = green.shape[2:5]
     momenta = lax.axis_size("mom")
@@ -142,10 +155,11 @@
     level = jnp.arange(1, quad + 1, dtype=jnp.int32)
     chosen = jnp.where(offsets == level[:, None], rates[:, None], 0.0)
     levels = jnp.sum(chosen[:, :, None] * coupling, axis=-1).reshape(2 * quad, momenta)
-    row = jnp.repeat(qtable, orbits // momenta, axis=1).astype(green.dtype)
-    row = jnp.broadcast_to(row, (momenta, 2 * quad, orbits))
-    slabs = jnp.concatenate([pieces.reshape(momenta, quad * rows, orbits), row], axis=1)
-    here = swap(slabs, "mom")
+    table = paired(jnp.repeat(qtable, orbits // momenta, axis=1).astype(green.dtype), 2, momenta)
+    here = swap(pieces, "mom")
+    table = paired(table, 4, momenta)
+    table = jnp.pad(table, ((0, 16 - momenta // 2), (0, 0)))
+    here = jnp.concatenate([here.reshape(-1, orbits), table])
     before = lax.ppermute(here, LINE, [(z, z + 1) for z in range(quads - 1)])
     after = lax.ppermute(here, LINE, [(z + 1, z) for z in range(quads - 1)])
     total = mixed(levels, before, here, after, shape)

time: 106 us -> 110 us (1.038)
  blocking collectives: 24.5 us -> 54.2 us
  waiting for transfers between devices: 38.4 us -> 16.7 us
  starting transfers between devices: 37.1 us -> 33.9 us
    all_to_all x1 -> x2, blocking collectives: 24.5 us -> 54.2 us  [swap(): return lax.all_to_all(x, axis, split_axis=0, concat_axis=0, tiled=True)]
    all_to_all x3 -> x2, waiting for transfers between devices: 31.3 us -> 8.88 us  [swap(): return lax.all_to_all(x, axis, split_axis=0, concat_axis=0, tiled=True)]
    ppermute x0 -> x2, starting transfers between devices: none -> 17.3 us  [paired(): other = lax.ppermute(x, 'mom', [(k, k ^ bit) for k in range(momenta)])]
    all_to_all x3 -> x2, starting transfers between devices: 30.8 us -> 14 us  [swap(): return lax.all_to_all(x, axis, split_axis=0, concat_axis=0, tiled=True)]
    ppermute x1, starting transfers between devices: 5 us -> 1.31 us  [shards(): before = lax.ppermute(here, LINE, [(z, z + 1) for z in range(quads - 1)])]
    ppermute x0 -> x2, waiting for transfers between devices: none -> 1.29 us  [paired(): other = lax.ppermute(x, 'mom', [(k, k ^ bit) for k in range(momenta)])]
  transfers between devices with their start and end apart: 5 -> 6, of which waited for: 5 -> 5; matrix products, arithmetic and copies ran while one was open for 0% -> 0% of each run, Pallas kernels for 0% -> 0%
where the time goes in v7:
time: 110 us; the launch traced here: 109 us
  blocking collectives  54.2 us (49%)
  starting transfers between devices  33.9 us (31%)
  waiting for transfers between devices  16.7 us (15%)
  Pallas kernels  2.98 us (3%)
    all_to_all x2, blocking collectives, swap(): return lax.all_to_all(x, axis, split_axis=0, concat_axis=0, tiled=True)  54.2 us
    ppermute x2, starting transfers between devices, paired(): other = lax.ppermute(x, 'mom', [(k, k ^ bit) for k in range(momenta)])  17.3 us
    all_to_all x2, starting transfers between devices, swap(): return lax.all_to_all(x, axis, split_axis=0, concat_axis=0, tiled=True)  14 us
    all_to_all x2, waiting for transfers between devices, swap(): return lax.all_to_all(x, axis, split_axis=0, concat_axis=0, tiled=True)  8.88 us
    ppermute x1, waiting for transfers between devices, shards(): after = lax.ppermute(here, LINE, [(z + 1, z) for z in range(quads - 1)])  3.85 us
    ppermute x1, waiting for transfers between devices, shards(): before = lax.ppermute(here, LINE, [(z, z + 1) for z in range(quads - 1)])  2.7 us
  transfers between devices with their start and end apart: 6, of which 5 were waited for; matrix products, arithmetic and copies ran while one was open for 0% of the time, Pallas kernels for 0%

profile of v7, /device:TPU:1, one launch (start us, length us, event | category | flops | bytes accessed | tf_op | source)
XLA Modules:
  0.0 109.1 jit_solution(10520079837933834417)
XLA Ops:
  0.0 27.3 %all_to_all.20 = bf16[32,32,128]{2,1,0:T(8,128)(2,1)} all-to-all(bf16[32,32,128]{2,1,0:T(8,128)(2,1)} %bitcast.17), channel_id=1, replica_groups=mesh['zh'=4,'y'=4,'x'=4,'core'=2,'mom'=8] {'y','x','core'}, dimensions={0} | all-to-all | bytes 524288 | tf_op jit(solution)/shard_map/all_to_all | solution.py:137
  27.3 0.0 copy-start.4
  27.3 3.5 %all-to-all-start.1 = ((bf16[32,32,128]{2,1,0:T(8,128)(2,1)}), bf16[32,32,128]{2,1,0:T(8,128)(2,1)S(1)}, u32[]{:S(2)}, u32[]{:S(2)}) async-start(bf16[32,32,128]{2,1,0:T(8,128)(2,1)} %all_to_all.20), calls=%async_computation.1 | async-start | bytes 524288 | tf_op jit(solution)/shard_map/all_to_all | solution.py:137
  30.9 0.0 copy-done.4
  30.9 0.1 broadcast_in_dim.30
  31.0 0.1 convert_element_type.22
  31.0 0.0 copy-start.5
  31.0 4.3 %collective-permute-start = (bf16[1,128]{1,0:T(2,128)(2,1)S(1)}, bf16[1,128]{1,0:T(2,128)(2,1)S(1)}, u32[]{:S(2)}, u32[]{:S(2)}) collective-permute-start(bf16[1,128]{1,0:T(2,128)(2,1)S(1)} %convert_element_type.22), channel_id=1, source_target_pairs={{0,2},{1,3},{2,0},{3,1},{4,6},{5,7},{6,4},{7,5},{8,10},{9,11},{10,... | collective-permute-start | bytes 776 | tf_op jit(solution)/shard_map/ppermute | solution.py:141
  35.3 0.0 copy-done.5
  35.4 0.0 copy-start.3
  35.4 0.1 broadcast_compare_fusion
  35.4 0.6 copy-done.3
  36.0 0.4 collective-permute-done
  36.4 13.1 %collective-permute-start.1 = (bf16[2,128]{1,0:T(2,128)(2,1)S(1)}, bf16[2,128]{1,0:T(2,128)(2,1)S(1)}, u32[]{:S(2)}, u32[]{:S(2)}) collective-permute-start(bf16[2,128]{1,0:T(2,128)(2,1)S(1)} %pad_maximum_fusion.2), channel_id=1, source_target_pairs={{0,4},{1,5},{2,6},{3,7},{4,0},{5,1},{6,2},{7,3},{8,12},{9,13},{10,... | collective-permute-start | bytes 1544 | tf_op jit(solution)/shard_map/ppermute | solution.py:141
  49.5 0.9 collective-permute-done.1
  50.4 0.0 all-to-all-done.1
  50.5 0.0 copy-start.1
  50.5 1.3 %collective-permute-start.2 = (bf16[1040,128]{1,0:T(8,128)(2,1)S(1)}, bf16[1040,128]{1,0:T(8,128)(2,1)S(1)}, u32[]{:S(2)}, u32[]{:S(2)}) collective-permute-start(bf16[1040,128]{1,0:T(8,128)(2,1)S(1)} %pad_maximum_fusion.here), channel_id=1, source_target_pairs={{0,1},{1,2},{2,3},{3,4},{4,5},{5,6},{6,7},{7,256},{256,257},{257,2... | collective-permute-start | bytes 798728 | tf_op jit(solution)/shard_map/ppermute | solution.py:163
  51.8 1.3 %collective-permute-start.3 = (bf16[1040,128]{1,0:T(8,128)(2,1)S(1)}, bf16[1040,128]{1,0:T(8,128)(2,1)S(1)}, u32[]{:S(2)}, u32[]{:S(2)}) collective-permute-start(bf16[1040,128]{1,0:T(8,128)(2,1)S(1)} %pad_maximum_fusion.here), channel_id=1, source_target_pairs={{1,0},{2,1},{3,2},{4,3},{5,4},{6,5},{7,6},{256,7},{257,256},{258,2... | collective-permute-start | bytes 798728 | tf_op jit(solution)/shard_map/ppermute | solution.py:164
  53.1 0.0 copy-done.1
  53.1 0.1 multiply_reduce_fusion
  53.2 2.7 %collective-permute-done.2.before = bf16[1040,128]{1,0:T(8,128)(2,1)S(1)} collective-permute-done((bf16[1040,128]{1,0:T(8,128)(2,1)S(1)}, bf16[1040,128]{1,0:T(8,128)(2,1)S(1)}, u32[]{:S(2)}, u32[]{:S(2)}) %collective-permute-start.2) | collective-permute-done | bytes 266272 | tf_op jit(solution)/shard_map/ppermute | solution.py:163
  55.9 3.8 %collective-permute-done.3.after = bf16[1040,128]{1,0:T(8,128)(2,1)S(1)} collective-permute-done((bf16[1040,128]{1,0:T(8,128)(2,1)S(1)}, bf16[1040,128]{1,0:T(8,128)(2,1)S(1)}, u32[]{:S(2)}, u32[]{:S(2)}) %collective-permute-start.3) | collective-permute-done | bytes 266272 | tf_op jit(solution)/shard_map/ppermute | solution.py:164
  59.7 0.8 shard_map.73
  60.6 0.0 copy-start
  60.6 26.9 %all_to_all.21 = bf16[32,32,128]{2,1,0:T(8,128)(2,1)} all-to-all(bf16[32,32,128]{2,1,0:T(8,128)(2,1)S(1)} %bitcast.13), channel_id=1, replica_groups=mesh['zh'=4,'y'=4,'x'=4,'core'=2,'mom'=8] {'mom'}, dimensions={0} | all-to-all | bytes 524288 | tf_op jit(solution)/shard_map/all_to_all | solution.py:137
  87.5 0.0 copy-start.2
  87.5 10.5 %all-to-all-start.3 = ((bf16[32,32,128]{2,1,0:T(8,128)(2,1)}), bf16[32,32,128]{2,1,0:T(8,128)(2,1)S(1)}, u32[]{:S(2)}, u32[]{:S(2)}) async-start(bf16[32,32,128]{2,1,0:T(8,128)(2,1)} %all_to_all.21), calls=%async_computation.3 | async-start | bytes 524288 | tf_op jit(solution)/shard_map/all_to_all | solution.py:137
  98.0 0.0 copy-done.2
  98.0 0.1 copy.10.neighbours
  98.1 8.9 %all-to-all-done.3 = bf16[32,32,128]{2,1,0:T(8,128)(2,1)S(1)} async-done(((bf16[32,32,128]{2,1,0:T(8,128)(2,1)}), bf16[32,32,128]{2,1,0:T(8,128)(2,1)S(1)}, u32[]{:S(2)}, u32[]{:S(2)}) %all-to-all-start.3) | async-done | bytes 262176 | tf_op jit(solution)/shard_map/all_to_all | solution.py:137
  106.9 0.0 copy-done
  106.9 2.2 %shard_map.74 = f32[4,2,128,128]{3,2,1,0:T(8,128)} custom-call(s32[4,2]{1,0:T(4,128)S(1)} %copy.10.neighbours, bf16[4,2,2,128,128]{4,3,2,1,0:T(8,128)(2,1)S(1)} %bitcast.14, bf16[4,2,128,128]{3,2,1,0:T(8,128)(2,1)S(1)} %bitcast.12), custom_call_target="tpu_custom_call" | custom-call | tf_op jit(solution)/shard_map/pallas_call | solution.py:123
  (8 shorter events, 0.1 us)
Async XLA Ops:
  27.3 3.6 %copy-start.4 = (s32[1,8]{1,0:T(1,128)S(1)}, s32[1,8]{1,0:T(1,128)}, u32[]{:S(2)}) copy-start(s32[1,8]{1,0:T(1,128)} %param.13) | copy-start | bytes 100
  27.3 23.1 %all-to-all-start.1 = ((bf16[32,32,128]{2,1,0:T(8,128)(2,1)}), bf16[32,32,128]{2,1,0:T(8,128)(2,1)S(1)}, u32[]{:S(2)}, u32[]{:S(2)}) async-start(bf16[32,32,128]{2,1,0:T(8,128)(2,1)} %all_to_all.20), calls=%async_computation.1 | async-start | bytes 524288 | tf_op jit(solution)/shard_map/all_to_all | solution.py:137
  31.0 4.3 %copy-start.5 = (s32[4]{0:T(128)S(1)}, s32[4]{0:T(128)}, u32[]{:S(2)}) copy-start(s32[4]{0:T(128)} %param.11) | copy-start | bytes 52
  31.0 5.3 %collective-permute-start = (bf16[1,128]{1,0:T(2,128)(2,1)S(1)}, bf16[1,128]{1,0:T(2,128)(2,1)S(1)}, u32[]{:S(2)}, u32[]{:S(2)}) collective-permute-start(bf16[1,128]{1,0:T(2,128)(2,1)S(1)} %convert_element_type.22), channel_id=1, source_target_pairs={{0,2},{1,3},{2,0},{3,1},{4,6},{5,7},{6,4},{7,5},{8,10},{9,11},{10,... | collective-permute-start | bytes 776 | tf_op jit(solution)/shard_map/ppermute | solution.py:141
  35.4 0.7 copy-start.3
  36.4 14.0 %collective-permute-start.1 = (bf16[2,128]{1,0:T(2,128)(2,1)S(1)}, bf16[2,128]{1,0:T(2,128)(2,1)S(1)}, u32[]{:S(2)}, u32[]{:S(2)}) collective-permute-start(bf16[2,128]{1,0:T(2,128)(2,1)S(1)} %pad_maximum_fusion.2), channel_id=1, source_target_pairs={{0,4},{1,5},{2,6},{3,7},{4,0},{5,1},{6,2},{7,3},{8,12},{9,13},{10,... | collective-permute-start | bytes 1544 | tf_op jit(solution)/shard_map/ppermute | solution.py:141
  50.5 2.6 %copy-start.1 = (f32[8,4]{0,1:T(4,128)S(1)}, f32[8,4]{0,1:T(4,128)}, u32[]{:S(2)}) copy-start(f32[8,4]{0,1:T(4,128)} %param.9) | copy-start | bytes 388
  50.5 5.4 %collective-permute-start.2 = (bf16[1040,128]{1,0:T(8,128)(2,1)S(1)}, bf16[1040,128]{1,0:T(8,128)(2,1)S(1)}, u32[]{:S(2)}, u32[]{:S(2)}) collective-permute-start(bf16[1040,128]{1,0:T(8,128)(2,1)S(1)} %pad_maximum_fusion.here), channel_id=1, source_target_pairs={{0,1},{1,2},{2,3},{3,4},{4,5},{5,6},{6,7},{7,256},{256,257},{257,2... | collective-permute-start | bytes 798728 | tf_op jit(solution)/shard_map/ppermute | solution.py:163
  51.8 8.0 %collective-permute-start.3 = (bf16[1040,128]{1,0:T(8,128)(2,1)S(1)}, bf16[1040,128]{1,0:T(8,128)(2,1)S(1)}, u32[]{:S(2)}, u32[]{:S(2)}) collective-permute-start(bf16[1040,128]{1,0:T(8,128)(2,1)S(1)} %pad_maximum_fusion.here), channel_id=1, source_target_pairs={{1,0},{2,1},{3,2},{4,3},{5,4},{6,5},{7,6},{256,7},{257,256},{258,2... | collective-permute-start | bytes 798728 | tf_op jit(solution)/shard_map/ppermute | solution.py:164
  60.6 46.4 %copy-start = (bf16[1,4,2,2,128,128]{5,4,3,2,1,0:T(8,128)(2,1)S(1)}, bf16[1,4,2,2,128,128]{5,4,3,2,1,0:T(8,128)(2,1)}, u32[]{:S(2)}) copy-start(bf16[1,4,2,2,128,128]{5,4,3,2,1,0:T(8,128)(2,1)} %param.8) | copy-start | bytes 1572868
  87.5 10.5 %copy-start.2 = (s32[4,2]{0,1:T(2,128)S(1)}, s32[4,2]{0,1:T(2,128)}, u32[]{:S(2)}) copy-start(s32[4,2]{0,1:T(2,128)} %param.12) | copy-start | bytes 100
  87.5 19.4 %all-to-all-start.3 = ((bf16[32,32,128]{2,1,0:T(8,128)(2,1)}), bf16[32,32,128]{2,1,0:T(8,128)(2,1)S(1)}, u32[]{:S(2)}, u32[]{:S(2)}) async-start(bf16[32,32,128]{2,1,0:T(8,128)(2,1)} %all_to_all.21), calls=%async_computation.3 | async-start | bytes 524288 | tf_op jit(solution)/shard_map/all_to_all | solution.py:137

commit v8 on v7

--- a/solution.py
+++ b/solution.py
@@ -86,7 +86,7 @@
     for c in range(clusters):
         total = None
         for s in range(listed):
-            spot = neighbours[c, s]
+            spot = neighbours[s, c]
             re = near[spot, 0]
             im = near[spot, 1]
             d_re = grad[c, s, 0]
@@ -153,8 +153,9 @@
     pieces = swap(green.reshape(plane, rows, orbits), PLANE)
     rates = jnp.stack([1.0 + occupation, occupation])
     level = jnp.arange(1, quad + 1, dtype=jnp.int32)
-    chosen = jnp.where(offsets == level[:, None], rates[:, None], 0.0)
-    levels = jnp.sum(chosen[:, :, None] * coupling, axis=-1).reshape(2 * quad, momenta)
+    active = jnp.where(offsets == level[:, None], rates[:, None], 0.0)
+    levels = jnp.sum(active[:, :, None] * coupling, axis=-1).reshape(2 * quad, momenta)
+    chosen = jnp.pad(neighbours.T, ((0, 0), (0, quad)))
     table = paired(jnp.repeat(qtable, orbits // momenta, axis=1).astype(green.dtype), 2, momenta)
     here = swap(pieces, "mom")
     table = paired(table, 4, momenta)
@@ -164,7 +165,7 @@
     after = lax.ppermute(here, LINE, [(z + 1, z) for z in range(quads - 1)])
     total = mixed(levels, before, here, after, shape)
     total = swap(swap(total.reshape(plane, rows, orbits), "mom"), PLANE)
-    out = dressed(neighbours, grad[0], total.reshape(clusters, parts, orbits, orbits))
+    out = dressed(chosen, grad[0], total.reshape(clusters, parts, orbits, orbits))
     return out[None, None]
 
 

time: 110 us -> 110 us (level)
  no operation moved by 1% of the time
where the time goes in v8:
time: 110 us; the launch traced here: 109 us
  blocking collectives  54.2 us (49%)
  starting transfers between devices  33.8 us (31%)
  waiting for transfers between devices  16.1 us (15%)
  Pallas kernels  2.97 us (3%)
  local copies, waits for them, and re-layouts  1.44 us (1%)
    all_to_all x2, blocking collectives, swap(): return lax.all_to_all(x, axis, split_axis=0, concat_axis=0, tiled=True)  54.2 us
    ppermute x2, starting transfers between devices, paired(): other = lax.ppermute(x, 'mom', [(k, k ^ bit) for k in range(momenta)])  17.3 us
    all_to_all x2, starting transfers between devices, swap(): return lax.all_to_all(x, axis, split_axis=0, concat_axis=0, tiled=True)  13.9 us
    all_to_all x2, waiting for transfers between devices, swap(): return lax.all_to_all(x, axis, split_axis=0, concat_axis=0, tiled=True)  8.3 us
    ppermute x1, waiting for transfers between devices, shards(): after = lax.ppermute(here, LINE, [(z + 1, z) for z in range(quads - 1)])  3.85 us
    ppermute x1, waiting for transfers between devices, shards(): before = lax.ppermute(here, LINE, [(z, z + 1) for z in range(quads - 1)])  2.7 us
  transfers between devices with their start and end apart: 6, of which 5 were waited for; matrix products, arithmetic and copies ran while one was open for 0% of the time, Pallas kernels for 0%

profile of v8, /device:TPU:1, one launch (start us, length us, event | category | flops | bytes accessed | tf_op | source)
XLA Modules:
  0.0 109.0 jit_solution(7231483516993065544)
XLA Ops:
  0.0 27.3 %all_to_all.20 = bf16[32,32,128]{2,1,0:T(8,128)(2,1)} all-to-all(bf16[32,32,128]{2,1,0:T(8,128)(2,1)} %bitcast.18), channel_id=1, replica_groups=mesh['zh'=4,'y'=4,'x'=4,'core'=2,'mom'=8] {'y','x','core'}, dimensions={0} | all-to-all | bytes 524288 | tf_op jit(solution)/shard_map/all_to_all | solution.py:137
  27.3 0.0 copy-start.4
  27.3 3.5 %all-to-all-start.1 = ((bf16[32,32,128]{2,1,0:T(8,128)(2,1)}), bf16[32,32,128]{2,1,0:T(8,128)(2,1)S(1)}, u32[]{:S(2)}, u32[]{:S(2)}) async-start(bf16[32,32,128]{2,1,0:T(8,128)(2,1)} %all_to_all.20), calls=%async_computation.1 | async-start | bytes 524288 | tf_op jit(solution)/shard_map/all_to_all | solution.py:137
  30.9 0.0 copy-done.4
  30.9 0.1 broadcast_in_dim.30
  31.0 0.1 convert_element_type.22
  31.0 0.0 copy-start.5
  31.0 4.3 %collective-permute-start = (bf16[1,128]{1,0:T(2,128)(2,1)S(1)}, bf16[1,128]{1,0:T(2,128)(2,1)S(1)}, u32[]{:S(2)}, u32[]{:S(2)}) collective-permute-start(bf16[1,128]{1,0:T(2,128)(2,1)S(1)} %convert_element_type.22), channel_id=1, source_target_pairs={{0,2},{1,3},{2,0},{3,1},{4,6},{5,7},{6,4},{7,5},{8,10},{9,11},{10,... | collective-permute-start | bytes 776 | tf_op jit(solution)/shard_map/ppermute | solution.py:141
  35.3 0.0 copy-done.5
  35.4 0.0 copy-start.3
  35.4 0.1 broadcast_compare_fusion
  35.4 0.6 copy-done.3
  36.0 0.4 collective-permute-done
  36.4 13.1 %collective-permute-start.1 = (bf16[2,128]{1,0:T(2,128)(2,1)S(1)}, bf16[2,128]{1,0:T(2,128)(2,1)S(1)}, u32[]{:S(2)}, u32[]{:S(2)}) collective-permute-start(bf16[2,128]{1,0:T(2,128)(2,1)S(1)} %pad_maximum_fusion.2), channel_id=1, source_target_pairs={{0,4},{1,5},{2,6},{3,7},{4,0},{5,1},{6,2},{7,3},{8,12},{9,13},{10,... | collective-permute-start | bytes 1544 | tf_op jit(solution)/shard_map/ppermute | solution.py:141
  49.5 0.9 collective-permute-done.1
  50.4 0.0 all-to-all-done.1
  50.5 0.0 copy-start.1
  50.5 1.3 %collective-permute-start.2 = (bf16[1040,128]{1,0:T(8,128)(2,1)S(1)}, bf16[1040,128]{1,0:T(8,128)(2,1)S(1)}, u32[]{:S(2)}, u32[]{:S(2)}) collective-permute-start(bf16[1040,128]{1,0:T(8,128)(2,1)S(1)} %pad_maximum_fusion.here), channel_id=1, source_target_pairs={{0,1},{1,2},{2,3},{3,4},{4,5},{5,6},{6,7},{7,256},{256,257},{257,2... | collective-permute-start | bytes 798728 | tf_op jit(solution)/shard_map/ppermute | solution.py:164
  51.8 1.3 %collective-permute-start.3 = (bf16[1040,128]{1,0:T(8,128)(2,1)S(1)}, bf16[1040,128]{1,0:T(8,128)(2,1)S(1)}, u32[]{:S(2)}, u32[]{:S(2)}) collective-permute-start(bf16[1040,128]{1,0:T(8,128)(2,1)S(1)} %pad_maximum_fusion.here), channel_id=1, source_target_pairs={{1,0},{2,1},{3,2},{4,3},{5,4},{6,5},{7,6},{256,7},{257,256},{258,2... | collective-permute-start | bytes 798728 | tf_op jit(solution)/shard_map/ppermute | solution.py:165
  53.1 0.0 copy-done.1
  53.1 0.1 multiply_reduce_fusion
  53.2 2.7 %collective-permute-done.2.before = bf16[1040,128]{1,0:T(8,128)(2,1)S(1)} collective-permute-done((bf16[1040,128]{1,0:T(8,128)(2,1)S(1)}, bf16[1040,128]{1,0:T(8,128)(2,1)S(1)}, u32[]{:S(2)}, u32[]{:S(2)}) %collective-permute-start.2) | collective-permute-done | bytes 266272 | tf_op jit(solution)/shard_map/ppermute | solution.py:164
  55.9 3.8 %collective-permute-done.3.after = bf16[1040,128]{1,0:T(8,128)(2,1)S(1)} collective-permute-done((bf16[1040,128]{1,0:T(8,128)(2,1)S(1)}, bf16[1040,128]{1,0:T(8,128)(2,1)S(1)}, u32[]{:S(2)}, u32[]{:S(2)}) %collective-permute-start.3) | collective-permute-done | bytes 266272 | tf_op jit(solution)/shard_map/ppermute | solution.py:165
  59.7 0.8 shard_map.73
  60.6 0.0 copy-start
  60.6 26.9 %all_to_all.21 = bf16[32,32,128]{2,1,0:T(8,128)(2,1)} all-to-all(bf16[32,32,128]{2,1,0:T(8,128)(2,1)S(1)} %bitcast.14), channel_id=1, replica_groups=mesh['zh'=4,'y'=4,'x'=4,'core'=2,'mom'=8] {'mom'}, dimensions={0} | all-to-all | bytes 524288 | tf_op jit(solution)/shard_map/all_to_all | solution.py:137
  87.5 10.3 %all-to-all-start.3 = ((bf16[32,32,128]{2,1,0:T(8,128)(2,1)}), bf16[32,32,128]{2,1,0:T(8,128)(2,1)S(1)}, u32[]{:S(2)}, u32[]{:S(2)}) async-start(bf16[32,32,128]{2,1,0:T(8,128)(2,1)} %all_to_all.21), calls=%async_computation.3 | async-start | bytes 524288 | tf_op jit(solution)/shard_map/all_to_all | solution.py:137
  97.8 0.0 copy-start.2
  97.8 0.7 copy-done.2
  98.5 8.3 %all-to-all-done.3 = bf16[32,32,128]{2,1,0:T(8,128)(2,1)S(1)} async-done(((bf16[32,32,128]{2,1,0:T(8,128)(2,1)}), bf16[32,32,128]{2,1,0:T(8,128)(2,1)S(1)}, u32[]{:S(2)}, u32[]{:S(2)}) %all-to-all-start.3) | async-done | bytes 262176 | tf_op jit(solution)/shard_map/all_to_all | solution.py:137
  106.8 0.0 copy-done
  106.8 2.2 %shard_map.74 = f32[4,2,128,128]{3,2,1,0:T(8,128)} custom-call(s32[2,8]{1,0:T(2,128)S(1)} %pad.8.neighbours, bf16[4,2,2,128,128]{4,3,2,1,0:T(8,128)(2,1)S(1)} %bitcast.15, bf16[4,2,128,128]{3,2,1,0:T(8,128)(2,1)S(1)} %bitcast.13), custom_call_target="tpu_custom_call" | custom-call | tf_op jit(solution)/shard_map/pallas_call | solution.py:123
  (9 shorter events, 0.1 us)
Async XLA Ops:
  27.3 3.6 %copy-start.4 = (s32[1,8]{1,0:T(1,128)S(1)}, s32[1,8]{1,0:T(1,128)}, u32[]{:S(2)}) copy-start(s32[1,8]{1,0:T(1,128)} %param.13) | copy-start | bytes 100
  27.3 23.1 %all-to-all-start.1 = ((bf16[32,32,128]{2,1,0:T(8,128)(2,1)}), bf16[32,32,128]{2,1,0:T(8,128)(2,1)S(1)}, u32[]{:S(2)}, u32[]{:S(2)}) async-start(bf16[32,32,128]{2,1,0:T(8,128)(2,1)} %all_to_all.20), calls=%async_computation.1 | async-start | bytes 524288 | tf_op jit(solution)/shard_map/all_to_all | solution.py:137
  31.0 4.3 %copy-start.5 = (s32[4]{0:T(128)S(1)}, s32[4]{0:T(128)}, u32[]{:S(2)}) copy-start(s32[4]{0:T(128)} %param.11) | copy-start | bytes 52
  31.0 5.3 %collective-permute-start = (bf16[1,128]{1,0:T(2,128)(2,1)S(1)}, bf16[1,128]{1,0:T(2,128)(2,1)S(1)}, u32[]{:S(2)}, u32[]{:S(2)}) collective-permute-start(bf16[1,128]{1,0:T(2,128)(2,1)S(1)} %convert_element_type.22), channel_id=1, source_target_pairs={{0,2},{1,3},{2,0},{3,1},{4,6},{5,7},{6,4},{7,5},{8,10},{9,11},{10,... | collective-permute-start | bytes 776 | tf_op jit(solution)/shard_map/ppermute | solution.py:141
  35.4 0.7 copy-start.3
  36.4 14.0 %collective-permute-start.1 = (bf16[2,128]{1,0:T(2,128)(2,1)S(1)}, bf16[2,128]{1,0:T(2,128)(2,1)S(1)}, u32[]{:S(2)}, u32[]{:S(2)}) collective-permute-start(bf16[2,128]{1,0:T(2,128)(2,1)S(1)} %pad_maximum_fusion.2), channel_id=1, source_target_pairs={{0,4},{1,5},{2,6},{3,7},{4,0},{5,1},{6,2},{7,3},{8,12},{9,13},{10,... | collective-permute-start | bytes 1544 | tf_op jit(solution)/shard_map/ppermute | solution.py:141
  50.5 2.6 %copy-start.1 = (f32[8,4]{0,1:T(4,128)S(1)}, f32[8,4]{0,1:T(4,128)}, u32[]{:S(2)}) copy-start(f32[8,4]{0,1:T(4,128)} %param.9) | copy-start | bytes 388
  50.5 5.4 %collective-permute-start.2 = (bf16[1040,128]{1,0:T(8,128)(2,1)S(1)}, bf16[1040,128]{1,0:T(8,128)(2,1)S(1)}, u32[]{:S(2)}, u32[]{:S(2)}) collective-permute-start(bf16[1040,128]{1,0:T(8,128)(2,1)S(1)} %pad_maximum_fusion.here), channel_id=1, source_target_pairs={{0,1},{1,2},{2,3},{3,4},{4,5},{5,6},{6,7},{7,256},{256,257},{257,2... | collective-permute-start | bytes 798728 | tf_op jit(solution)/shard_map/ppermute | solution.py:164
  51.8 8.0 %collective-permute-start.3 = (bf16[1040,128]{1,0:T(8,128)(2,1)S(1)}, bf16[1040,128]{1,0:T(8,128)(2,1)S(1)}, u32[]{:S(2)}, u32[]{:S(2)}) collective-permute-start(bf16[1040,128]{1,0:T(8,128)(2,1)S(1)} %pad_maximum_fusion.here), channel_id=1, source_target_pairs={{1,0},{2,1},{3,2},{4,3},{5,4},{6,5},{7,6},{256,7},{257,256},{258,2... | collective-permute-start | bytes 798728 | tf_op jit(solution)/shard_map/ppermute | solution.py:165
  60.6 46.3 %copy-start = (bf16[1,4,2,2,128,128]{5,4,3,2,1,0:T(8,128)(2,1)S(1)}, bf16[1,4,2,2,128,128]{5,4,3,2,1,0:T(8,128)(2,1)}, u32[]{:S(2)}) copy-start(bf16[1,4,2,2,128,128]{5,4,3,2,1,0:T(8,128)(2,1)} %param.8) | copy-start | bytes 1572868
  87.5 19.3 %all-to-all-start.3 = ((bf16[32,32,128]{2,1,0:T(8,128)(2,1)}), bf16[32,32,128]{2,1,0:T(8,128)(2,1)S(1)}, u32[]{:S(2)}, u32[]{:S(2)}) async-start(bf16[32,32,128]{2,1,0:T(8,128)(2,1)} %all_to_all.21), calls=%async_computation.3 | async-start | bytes 524288 | tf_op jit(solution)/shard_map/all_to_all | solution.py:137
  97.8 0.7 copy-start.2

commit v9 on v8

--- a/solution.py
+++ b/solution.py
@@ -84,7 +84,7 @@
     orbits = out.shape[-1]
     copies = []
     for c in range(clusters):
-        total = None
+        prods, rights = [], []
         for s in range(listed):
             spot = neighbours[s, c]
             re = near[spot, 0]
@@ -95,18 +95,18 @@
             middle = jnp.concatenate(
                 [jnp.concatenate([re, im], axis=1), jnp.concatenate([-im, re], axis=1)], axis=0
             )
-            right = jnp.concatenate([left, jnp.concatenate([-d_im, d_re], axis=1)], axis=0)
-            prod = jnp.dot(left, middle, preferred_element_type=jnp.float32)
-            high = prod.astype(jnp.bfloat16)
-            low = (prod - high.astype(jnp.float32)).astype(jnp.bfloat16)
-            part = lax.dot_general(
-                jnp.concatenate([high, low], axis=0),
-                right,
-                (((1,), (1,)), ((), ())),
-                preferred_element_type=jnp.float32,
-            )
-            part = part[:orbits] + part[orbits:]
-            total = part if total is None else total + part
+            rights.append(jnp.concatenate([left, jnp.concatenate([-d_im, d_re], axis=1)], axis=0))
+            prods.append(jnp.dot(left, middle, preferred_element_type=jnp.float32))
+        prod = jnp.concatenate(prods, axis=1)
+        high = prod.astype(jnp.bfloat16)
+        low = (prod - high.astype(jnp.float32)).astype(jnp.bfloat16)
+        both = lax.dot_general(
+            jnp.concatenate([high, low], axis=0),
+            jnp.concatenate(rights, axis=1),
+            (((1,), (1,)), ((), ())),
+            preferred_element_type=jnp.float32,
+        )
+        total = both[:orbits] + both[orbits:]
         result[c, 0] = total[:, :orbits]
         result[c, 1] = total[:, orbits:]
         copy = pltpu.make_async_copy(result.at[c], out.at[c], done.at[c])

time: 110 us -> 109 us (level)
  no operation moved by 1% of the time
where the time goes in v9:
time: 109 us
  blocking collectives  54.2 us (50%)
  starting transfers between devices  33.8 us (31%)
  waiting for transfers between devices  16.1 us (15%)
  Pallas kernels  2.78 us (3%)
  local copies, waits for them, and re-layouts  1.44 us (1%)
    all_to_all x2, blocking collectives, swap(): return lax.all_to_all(x, axis, split_axis=0, concat_axis=0, tiled=True)  54.2 us
    ppermute x2, starting transfers between devices, paired(): other = lax.ppermute(x, 'mom', [(k, k ^ bit) for k in range(momenta)])  17.3 us
    all_to_all x2, starting transfers between devices, swap(): return lax.all_to_all(x, axis, split_axis=0, concat_axis=0, tiled=True)  13.9 us
    all_to_all x2, waiting for transfers between devices, swap(): return lax.all_to_all(x, axis, split_axis=0, concat_axis=0, tiled=True)  8.3 us
    ppermute x1, waiting for transfers between devices, shards(): after = lax.ppermute(here, LINE, [(z + 1, z) for z in range(quads - 1)])  3.85 us
    ppermute x1, waiting for transfers between devices, shards(): before = lax.ppermute(here, LINE, [(z, z + 1) for z in range(quads - 1)])  2.7 us
  transfers between devices with their start and end apart: 6, of which 5 were waited for; matrix products, arithmetic and copies ran while one was open for 0% of the time, Pallas kernels for 0%

profile of v9, /device:TPU:1, one launch (start us, length us, event | category | flops | bytes accessed | tf_op | source)
XLA Modules:
  0.0 108.8 jit_solution(9090728516088838528)
XLA Ops:
  0.0 27.3 %all_to_all.20 = bf16[32,32,128]{2,1,0:T(8,128)(2,1)} all-to-all(bf16[32,32,128]{2,1,0:T(8,128)(2,1)} %bitcast.18), channel_id=1, replica_groups=mesh['zh'=4,'y'=4,'x'=4,'core'=2,'mom'=8] {'y','x','core'}, dimensions={0} | all-to-all | bytes 524288 | tf_op jit(solution)/shard_map/all_to_all | solution.py:137
  27.3 0.0 copy-start.4
  27.3 3.5 %all-to-all-start.1 = ((bf16[32,32,128]{2,1,0:T(8,128)(2,1)}), bf16[32,32,128]{2,1,0:T(8,128)(2,1)S(1)}, u32[]{:S(2)}, u32[]{:S(2)}) async-start(bf16[32,32,128]{2,1,0:T(8,128)(2,1)} %all_to_all.20), calls=%async_computation.1 | async-start | bytes 524288 | tf_op jit(solution)/shard_map/all_to_all | solution.py:137
  30.9 0.0 copy-done.4
  30.9 0.1 broadcast_in_dim.30
  31.0 0.1 convert_element_type.22
  31.0 0.0 copy-start.5
  31.0 4.3 %collective-permute-start = (bf16[1,128]{1,0:T(2,128)(2,1)S(1)}, bf16[1,128]{1,0:T(2,128)(2,1)S(1)}, u32[]{:S(2)}, u32[]{:S(2)}) collective-permute-start(bf16[1,128]{1,0:T(2,128)(2,1)S(1)} %convert_element_type.22), channel_id=1, source_target_pairs={{0,2},{1,3},{2,0},{3,1},{4,6},{5,7},{6,4},{7,5},{8,10},{9,11},{10,... | collective-permute-start | bytes 776 | tf_op jit(solution)/shard_map/ppermute | solution.py:141
  35.3 0.0 copy-done.5
  35.4 0.0 copy-start.3
  35.4 0.1 broadcast_compare_fusion
  35.4 0.6 copy-done.3
  36.0 0.4 collective-permute-done
  36.4 13.1 %collective-permute-start.1 = (bf16[2,128]{1,0:T(2,128)(2,1)S(1)}, bf16[2,128]{1,0:T(2,128)(2,1)S(1)}, u32[]{:S(2)}, u32[]{:S(2)}) collective-permute-start(bf16[2,128]{1,0:T(2,128)(2,1)S(1)} %pad_maximum_fusion.2), channel_id=1, source_target_pairs={{0,4},{1,5},{2,6},{3,7},{4,0},{5,1},{6,2},{7,3},{8,12},{9,13},{10,... | collective-permute-start | bytes 1544 | tf_op jit(solution)/shard_map/ppermute | solution.py:141
  49.5 0.9 collective-permute-done.1
  50.4 0.0 all-to-all-done.1
  50.5 0.0 copy-start.1
  50.5 1.3 %collective-permute-start.2 = (bf16[1040,128]{1,0:T(8,128)(2,1)S(1)}, bf16[1040,128]{1,0:T(8,128)(2,1)S(1)}, u32[]{:S(2)}, u32[]{:S(2)}) collective-permute-start(bf16[1040,128]{1,0:T(8,128)(2,1)S(1)} %pad_maximum_fusion.here), channel_id=1, source_target_pairs={{0,1},{1,2},{2,3},{3,4},{4,5},{5,6},{6,7},{7,256},{256,257},{257,2... | collective-permute-start | bytes 798728 | tf_op jit(solution)/shard_map/ppermute | solution.py:164
  51.8 1.3 %collective-permute-start.3 = (bf16[1040,128]{1,0:T(8,128)(2,1)S(1)}, bf16[1040,128]{1,0:T(8,128)(2,1)S(1)}, u32[]{:S(2)}, u32[]{:S(2)}) collective-permute-start(bf16[1040,128]{1,0:T(8,128)(2,1)S(1)} %pad_maximum_fusion.here), channel_id=1, source_target_pairs={{1,0},{2,1},{3,2},{4,3},{5,4},{6,5},{7,6},{256,7},{257,256},{258,2... | collective-permute-start | bytes 798728 | tf_op jit(solution)/shard_map/ppermute | solution.py:165
  53.1 0.0 copy-done.1
  53.1 0.1 multiply_reduce_fusion
  53.2 2.7 %collective-permute-done.2.before = bf16[1040,128]{1,0:T(8,128)(2,1)S(1)} collective-permute-done((bf16[1040,128]{1,0:T(8,128)(2,1)S(1)}, bf16[1040,128]{1,0:T(8,128)(2,1)S(1)}, u32[]{:S(2)}, u32[]{:S(2)}) %collective-permute-start.2) | collective-permute-done | bytes 266272 | tf_op jit(solution)/shard_map/ppermute | solution.py:164
  55.9 3.8 %collective-permute-done.3.after = bf16[1040,128]{1,0:T(8,128)(2,1)S(1)} collective-permute-done((bf16[1040,128]{1,0:T(8,128)(2,1)S(1)}, bf16[1040,128]{1,0:T(8,128)(2,1)S(1)}, u32[]{:S(2)}, u32[]{:S(2)}) %collective-permute-start.3) | collective-permute-done | bytes 266272 | tf_op jit(solution)/shard_map/ppermute | solution.py:165
  59.7 0.8 shard_map.73
  60.6 0.0 copy-start
  60.6 26.9 %all_to_all.21 = bf16[32,32,128]{2,1,0:T(8,128)(2,1)} all-to-all(bf16[32,32,128]{2,1,0:T(8,128)(2,1)S(1)} %bitcast.14), channel_id=1, replica_groups=mesh['zh'=4,'y'=4,'x'=4,'core'=2,'mom'=8] {'mom'}, dimensions={0} | all-to-all | bytes 524288 | tf_op jit(solution)/shard_map/all_to_all | solution.py:137
  87.5 10.3 %all-to-all-start.3 = ((bf16[32,32,128]{2,1,0:T(8,128)(2,1)}), bf16[32,32,128]{2,1,0:T(8,128)(2,1)S(1)}, u32[]{:S(2)}, u32[]{:S(2)}) async-start(bf16[32,32,128]{2,1,0:T(8,128)(2,1)} %all_to_all.21), calls=%async_computation.3 | async-start | bytes 524288 | tf_op jit(solution)/shard_map/all_to_all | solution.py:137
  97.8 0.0 copy-start.2
  97.8 0.7 copy-done.2
  98.5 8.3 %all-to-all-done.3 = bf16[32,32,128]{2,1,0:T(8,128)(2,1)S(1)} async-done(((bf16[32,32,128]{2,1,0:T(8,128)(2,1)}), bf16[32,32,128]{2,1,0:T(8,128)(2,1)S(1)}, u32[]{:S(2)}, u32[]{:S(2)}) %all-to-all-start.3) | async-done | bytes 262176 | tf_op jit(solution)/shard_map/all_to_all | solution.py:137
  106.8 0.0 copy-done
  106.8 2.0 %shard_map.74 = f32[4,2,128,128]{3,2,1,0:T(8,128)} custom-call(s32[2,8]{1,0:T(2,128)S(1)} %pad.8.neighbours, bf16[4,2,2,128,128]{4,3,2,1,0:T(8,128)(2,1)S(1)} %bitcast.15, bf16[4,2,128,128]{3,2,1,0:T(8,128)(2,1)S(1)} %bitcast.13), custom_call_target="tpu_custom_call" | custom-call | tf_op jit(solution)/shard_map/pallas_call | solution.py:123
  (9 shorter events, 0.1 us)
Async XLA Ops:
  27.3 3.6 %copy-start.4 = (s32[1,8]{1,0:T(1,128)S(1)}, s32[1,8]{1,0:T(1,128)}, u32[]{:S(2)}) copy-start(s32[1,8]{1,0:T(1,128)} %param.13) | copy-start | bytes 100
  27.3 23.1 %all-to-all-start.1 = ((bf16[32,32,128]{2,1,0:T(8,128)(2,1)}), bf16[32,32,128]{2,1,0:T(8,128)(2,1)S(1)}, u32[]{:S(2)}, u32[]{:S(2)}) async-start(bf16[32,32,128]{2,1,0:T(8,128)(2,1)} %all_to_all.20), calls=%async_computation.1 | async-start | bytes 524288 | tf_op jit(solution)/shard_map/all_to_all | solution.py:137
  31.0 4.3 %copy-start.5 = (s32[4]{0:T(128)S(1)}, s32[4]{0:T(128)}, u32[]{:S(2)}) copy-start(s32[4]{0:T(128)} %param.11) | copy-start | bytes 52
  31.0 5.3 %collective-permute-start = (bf16[1,128]{1,0:T(2,128)(2,1)S(1)}, bf16[1,128]{1,0:T(2,128)(2,1)S(1)}, u32[]{:S(2)}, u32[]{:S(2)}) collective-permute-start(bf16[1,128]{1,0:T(2,128)(2,1)S(1)} %convert_element_type.22), channel_id=1, source_target_pairs={{0,2},{1,3},{2,0},{3,1},{4,6},{5,7},{6,4},{7,5},{8,10},{9,11},{10,... | collective-permute-start | bytes 776 | tf_op jit(solution)/shard_map/ppermute | solution.py:141
  35.4 0.7 copy-start.3
  36.4 14.0 %collective-permute-start.1 = (bf16[2,128]{1,0:T(2,128)(2,1)S(1)}, bf16[2,128]{1,0:T(2,128)(2,1)S(1)}, u32[]{:S(2)}, u32[]{:S(2)}) collective-permute-start(bf16[2,128]{1,0:T(2,128)(2,1)S(1)} %pad_maximum_fusion.2), channel_id=1, source_target_pairs={{0,4},{1,5},{2,6},{3,7},{4,0},{5,1},{6,2},{7,3},{8,12},{9,13},{10,... | collective-permute-start | bytes 1544 | tf_op jit(solution)/shard_map/ppermute | solution.py:141
  50.5 2.6 %copy-start.1 = (f32[8,4]{0,1:T(4,128)S(1)}, f32[8,4]{0,1:T(4,128)}, u32[]{:S(2)}) copy-start(f32[8,4]{0,1:T(4,128)} %param.9) | copy-start | bytes 388
  50.5 5.4 %collective-permute-start.2 = (bf16[1040,128]{1,0:T(8,128)(2,1)S(1)}, bf16[1040,128]{1,0:T(8,128)(2,1)S(1)}, u32[]{:S(2)}, u32[]{:S(2)}) collective-permute-start(bf16[1040,128]{1,0:T(8,128)(2,1)S(1)} %pad_maximum_fusion.here), channel_id=1, source_target_pairs={{0,1},{1,2},{2,3},{3,4},{4,5},{5,6},{6,7},{7,256},{256,257},{257,2... | collective-permute-start | bytes 798728 | tf_op jit(solution)/shard_map/ppermute | solution.py:164
  51.8 8.0 %collective-permute-start.3 = (bf16[1040,128]{1,0:T(8,128)(2,1)S(1)}, bf16[1040,128]{1,0:T(8,128)(2,1)S(1)}, u32[]{:S(2)}, u32[]{:S(2)}) collective-permute-start(bf16[1040,128]{1,0:T(8,128)(2,1)S(1)} %pad_maximum_fusion.here), channel_id=1, source_target_pairs={{1,0},{2,1},{3,2},{4,3},{5,4},{6,5},{7,6},{256,7},{257,256},{258,2... | collective-permute-start | bytes 798728 | tf_op jit(solution)/shard_map/ppermute | solution.py:165
  60.6 46.3 %copy-start = (bf16[1,4,2,2,128,128]{5,4,3,2,1,0:T(8,128)(2,1)S(1)}, bf16[1,4,2,2,128,128]{5,4,3,2,1,0:T(8,128)(2,1)}, u32[]{:S(2)}) copy-start(bf16[1,4,2,2,128,128]{5,4,3,2,1,0:T(8,128)(2,1)} %param.8) | copy-start | bytes 1572868
  87.5 19.3 %all-to-all-start.3 = ((bf16[32,32,128]{2,1,0:T(8,128)(2,1)}), bf16[32,32,128]{2,1,0:T(8,128)(2,1)S(1)}, u32[]{:S(2)}, u32[]{:S(2)}) async-start(bf16[32,32,128]{2,1,0:T(8,128)(2,1)} %all_to_all.21), calls=%async_computation.3 | async-start | bytes 524288 | tf_op jit(solution)/shard_map/all_to_all | solution.py:137
  97.8 0.7 copy-start.2

commit v10 on v9

--- a/solution.py
+++ b/solution.py
@@ -7,8 +7,11 @@
 from jax.sharding import PartitionSpec as P
 
 
-PLANE = ("y", "x", "core")
-LINE = ("zh", "mom")
+PLANE = ("y0", "xh", "y1", "xl", "core")
+ENERGY = ("y1", "y0", "xh", "xl", "core")
+MOM = ("m4", "m2", "m1")
+FAR = ("m2", "m1", "m4")
+LINE = ("zh", *MOM)
 
 
 def mix_kernel(levels, before, here, after, out, rows_of):
@@ -17,7 +20,7 @@
     half = rows // 2
     height = momenta * half
     body = momenta * quad * rows
-    me = lax.axis_index("mom")
+    me = lax.axis_index("m4") * 4 + lax.axis_index("m2") * 2 + lax.axis_index("m1")
     sublane = lax.broadcasted_iota(jnp.int32, (half, lanes), 0)
     lane = lax.broadcasted_iota(jnp.int32, (half, lanes), 1)
     diagonal = sublane == lax.rem(lane, half)
@@ -53,7 +56,10 @@
         start = (j * quad + e) * rows
         return jnp.concatenate([source[start : start + half], source[start + half : start + rows]], axis=1)
 
-    spots = [((i & 1) << 1 | (i & 2) << 1 | (i & 4) >> 2) ^ me for i in range(momenta)]
+    spots = []
+    for i in range(momenta):
+        k = ((i & 1) << 1 | (i & 2) << 1 | (i & 4) >> 2) ^ me
+        spots.append((k & 3) * 2 + (k >> 2))
     for e in range(quad):
         blocks = [near(j, e - level) for level in range(1, quad + 1) for j in range(momenta)]
         blocks += [near(j, e + level) for level in range(1, quad + 1) for j in range(momenta)]
@@ -138,14 +144,16 @@
 
 
 def paired(x, bit, momenta):
-    other = lax.ppermute(x, "mom", [(k, k ^ bit) for k in range(momenta)])
+    other = lax.ppermute(x, MOM, [(k, k ^ bit) for k in range(momenta)])
     return jnp.concatenate([x, other])
 
 
 def shards(green, grad, coupling, occupation, offsets, neighbours, qtable):
     clusters, parts, orbits = green.shape[2:5]
-    momenta = lax.axis_size("mom")
-    plane = lax.axis_size("y") * lax.axis_size("x") * lax.axis_size("core")
+    momenta = coupling.shape[0]
+    plane = 1
+    for axis in PLANE:
+        plane *= lax.axis_size(axis)
     quads = lax.axis_size("zh") * momenta
     rows = clusters * parts * orbits // plane
     quad = plane // momenta
@@ -156,30 +164,31 @@
     active = jnp.where(offsets == level[:, None], rates[:, None], 0.0)
     levels = jnp.sum(active[:, :, None] * coupling, axis=-1).reshape(2 * quad, momenta)
     chosen = jnp.pad(neighbours.T, ((0, 0), (0, quad)))
-    table = paired(jnp.repeat(qtable, orbits // momenta, axis=1).astype(green.dtype), 2, momenta)
-    here = swap(pieces, "mom")
+    ordered = qtable.reshape(1, 2, 4).swapaxes(1, 2).reshape(1, momenta)
+    table = paired(jnp.repeat(ordered, orbits // momenta, axis=1).astype(green.dtype), 2, momenta)
+    here = swap(pieces, FAR)
     table = paired(table, 4, momenta)
     table = jnp.pad(table, ((0, 16 - momenta // 2), (0, 0)))
     here = jnp.concatenate([here.reshape(-1, orbits), table])
     before = lax.ppermute(here, LINE, [(z, z + 1) for z in range(quads - 1)])
     after = lax.ppermute(here, LINE, [(z + 1, z) for z in range(quads - 1)])
     total = mixed(levels, before, here, after, shape)
-    total = swap(swap(total.reshape(plane, rows, orbits), "mom"), PLANE)
+    total = swap(swap(total.reshape(plane, rows, orbits), FAR), PLANE)
     out = dressed(chosen, grad[0], total.reshape(clusters, parts, orbits, orbits))
     return out[None, None]
 
 
 def solution(mesh):
-    split = Mesh(mesh.devices.reshape(4, 4, 4, 2, 8), ("zh", "y", "x", "core", "mom"))
-    energy = ("zh", "y", "x", "core")
+    split = Mesh(mesh.devices.reshape(4, *[2] * 8), ("zh", *ENERGY, *MOM))
+    energy = ("zh", *ENERGY)
     in_specs = (
-        P("mom", energy, None, None, None, None),
-        P("mom", None, None, None, None, None),
+        P(MOM, energy, None, None, None, None),
+        P(MOM, None, None, None, None, None),
         P(),
         P(),
         P(),
         P(),
-        P("mom", None),
+        P(MOM, None),
     )
-    out_specs = P("mom", energy, None, None, None, None)
+    out_specs = P(MOM, energy, None, None, None, None)
     return jax.shard_map(shards, mesh=split, in_specs=in_specs, out_specs=out_specs, check_vma=False)

time: 109 us -> 109 us (level)
    ppermute x2, starting transfers between devices: 17.3 us -> 16.1 us  [paired(): other = lax.ppermute(x, MOM, [(k, k ^ bit) for k in range(momenta)])]
  transfers between devices with their start and end apart: 6 -> 6, of which waited for: 5 -> 5; matrix products, arithmetic and copies ran while one was open for 0% -> 1% of each run, Pallas kernels for 0% -> 0%
where the time goes in v10:
time: 109 us
  blocking collectives  54.1 us (50%)
  starting transfers between devices  32.8 us (30%)
  waiting for transfers between devices  17 us (16%)
  Pallas kernels  2.78 us (3%)
  local copies, waits for them, and re-layouts  1.72 us (2%)
    all_to_all x2, blocking collectives, swap(): return lax.all_to_all(x, axis, split_axis=0, concat_axis=0, tiled=True)  54.1 us
    ppermute x2, starting transfers between devices, paired(): other = lax.ppermute(x, MOM, [(k, k ^ bit) for k in range(momenta)])  16.1 us
    all_to_all x2, starting transfers between devices, swap(): return lax.all_to_all(x, axis, split_axis=0, concat_axis=0, tiled=True)  14.1 us
    all_to_all x2, waiting for transfers between devices, swap(): return lax.all_to_all(x, axis, split_axis=0, concat_axis=0, tiled=True)  8.34 us
    ppermute x1, waiting for transfers between devices, shards(): after = lax.ppermute(here, LINE, [(z + 1, z) for z in range(quads - 1)])  3.77 us
    ppermute x1, waiting for transfers between devices, shards(): before = lax.ppermute(here, LINE, [(z, z + 1) for z in range(quads - 1)])  2.61 us
    ppermute x2, waiting for transfers between devices, paired(): other = lax.ppermute(x, MOM, [(k, k ^ bit) for k in range(momenta)])  2.26 us
  transfers between devices with their start and end apart: 6, of which 5 were waited for; matrix products, arithmetic and copies ran while one was open for 1% of the time, Pallas kernels for 0%

profile of v10, /device:TPU:1, one launch (start us, length us, event | category | flops | bytes accessed | tf_op | source)
XLA Modules:
  0.0 108.8 jit_solution(7477394178209500266)
XLA Ops:
  0.0 27.4 %all_to_all.20 = bf16[32,32,128]{2,1,0:T(8,128)(2,1)} all-to-all(bf16[32,32,128]{2,1,0:T(8,128)(2,1)} %bitcast.17), channel_id=1, replica_groups=mesh['zh'=4,'y1'=2,'y0'=2,'xh'=2,'xl'=2,'core'=2,'m4'=2,'m2'=2,'m1'=2] {..., dimensions={0} | all-to-all | bytes 524288 | tf_op jit(solution)/shard_map/all_to_all | solution.py:143
  27.4 0.0 copy-start.4
  27.4 3.5 %all-to-all-start.1 = ((bf16[32,32,128]{2,1,0:T(8,128)(2,1)}), bf16[32,32,128]{2,1,0:T(8,128)(2,1)S(1)}, u32[]{:S(2)}, u32[]{:S(2)}) async-start(bf16[32,32,128]{2,1,0:T(8,128)(2,1)} %all_to_all.20), calls=%async_computation.1 | async-start | bytes 524288 | tf_op jit(solution)/shard_map/all_to_all | solution.py:143
  31.0 0.0 copy-done.4
  31.0 0.1 convert_element_type.27
  31.1 0.1 copy.12
  31.2 0.1 convert_element_type.29
  31.3 0.1 broadcast_in_dim.30
  31.4 0.1 convert_element_type.30
  31.5 0.0 copy-start.5
  31.5 4.3 %collective-permute-start = (bf16[1,128]{1,0:T(2,128)(2,1)S(1)}, bf16[1,128]{1,0:T(2,128)(2,1)S(1)}, u32[]{:S(2)}, u32[]{:S(2)}) collective-permute-start(bf16[1,128]{1,0:T(2,128)(2,1)S(1)} %convert_element_type.30), channel_id=1, source_target_pairs={{0,2},{1,3},{2,0},{3,1},{4,6},{5,7},{6,4},{7,5},{8,10},{9,11},{10,... | collective-permute-start | bytes 776 | tf_op jit(solution)/shard_map/ppermute | solution.py:147
  35.8 0.0 copy-done.5
  35.8 0.0 copy-start.3
  35.8 0.1 broadcast_compare_fusion
  35.9 0.6 copy-done.3
  36.5 1.3 %collective-permute-done = bf16[1,128]{1,0:T(2,128)(2,1)S(1)} collective-permute-done((bf16[1,128]{1,0:T(2,128)(2,1)S(1)}, bf16[1,128]{1,0:T(2,128)(2,1)S(1)}, u32[]{:S(2)}, u32[]{:S(2)}) %collective-permute-start) | collective-permute-done | bytes 288 | tf_op jit(solution)/shard_map/ppermute | solution.py:147
  37.8 11.7 %collective-permute-start.1 = (bf16[2,128]{1,0:T(2,128)(2,1)S(1)}, bf16[2,128]{1,0:T(2,128)(2,1)S(1)}, u32[]{:S(2)}, u32[]{:S(2)}) collective-permute-start(bf16[2,128]{1,0:T(2,128)(2,1)S(1)} %pad_maximum_fusion.2), channel_id=1, source_target_pairs={{0,4},{1,5},{2,6},{3,7},{4,0},{5,1},{6,2},{7,3},{8,12},{9,13},{10,... | collective-permute-start | bytes 1544 | tf_op jit(solution)/shard_map/ppermute | solution.py:147
  49.6 0.9 collective-permute-done.1
  50.5 0.0 all-to-all-done.1
  50.6 0.0 copy-start.1
  50.6 1.3 %collective-permute-start.2 = (bf16[1040,128]{1,0:T(8,128)(2,1)S(1)}, bf16[1040,128]{1,0:T(8,128)(2,1)S(1)}, u32[]{:S(2)}, u32[]{:S(2)}) collective-permute-start(bf16[1040,128]{1,0:T(8,128)(2,1)S(1)} %pad_maximum_fusion.here), channel_id=1, source_target_pairs={{0,1},{1,2},{2,3},{3,4},{4,5},{5,6},{6,7},{7,256},{256,257},{257,2... | collective-permute-start | bytes 798728 | tf_op jit(solution)/shard_map/ppermute | solution.py:173
  51.9 1.3 %collective-permute-start.3 = (bf16[1040,128]{1,0:T(8,128)(2,1)S(1)}, bf16[1040,128]{1,0:T(8,128)(2,1)S(1)}, u32[]{:S(2)}, u32[]{:S(2)}) collective-permute-start(bf16[1040,128]{1,0:T(8,128)(2,1)S(1)} %pad_maximum_fusion.here), channel_id=1, source_target_pairs={{1,0},{2,1},{3,2},{4,3},{5,4},{6,5},{7,6},{256,7},{257,256},{258,2... | collective-permute-start | bytes 798728 | tf_op jit(solution)/shard_map/ppermute | solution.py:174
  53.2 0.0 copy-done.1
  53.2 0.1 multiply_reduce_fusion
  53.3 2.6 %collective-permute-done.2.before = bf16[1040,128]{1,0:T(8,128)(2,1)S(1)} collective-permute-done((bf16[1040,128]{1,0:T(8,128)(2,1)S(1)}, bf16[1040,128]{1,0:T(8,128)(2,1)S(1)}, u32[]{:S(2)}, u32[]{:S(2)}) %collective-permute-start.2) | collective-permute-done | bytes 266272 | tf_op jit(solution)/shard_map/ppermute | solution.py:173
  55.9 3.8 %collective-permute-done.3.after = bf16[1040,128]{1,0:T(8,128)(2,1)S(1)} collective-permute-done((bf16[1040,128]{1,0:T(8,128)(2,1)S(1)}, bf16[1040,128]{1,0:T(8,128)(2,1)S(1)}, u32[]{:S(2)}, u32[]{:S(2)}) %collective-permute-start.3) | collective-permute-done | bytes 266272 | tf_op jit(solution)/shard_map/ppermute | solution.py:174
  59.7 0.8 shard_map.73
  60.5 0.0 copy-start
  60.5 26.7 %all_to_all.21 = bf16[32,32,128]{2,1,0:T(8,128)(2,1)} all-to-all(bf16[32,32,128]{2,1,0:T(8,128)(2,1)S(1)} %bitcast.13), channel_id=1, replica_groups=mesh['zh'=4,'y1'=2,'y0'=2,'xh'=2,'xl'=2,'core'=2,'m4'=2,'m2'=2,'m1'=2] {..., dimensions={0} | all-to-all | bytes 524288 | tf_op jit(solution)/shard_map/all_to_all | solution.py:143
  87.2 10.6 %all-to-all-start.3 = ((bf16[32,32,128]{2,1,0:T(8,128)(2,1)}), bf16[32,32,128]{2,1,0:T(8,128)(2,1)S(1)}, u32[]{:S(2)}, u32[]{:S(2)}) async-start(bf16[32,32,128]{2,1,0:T(8,128)(2,1)} %all_to_all.21), calls=%async_computation.3 | async-start | bytes 524288 | tf_op jit(solution)/shard_map/all_to_all | solution.py:143
  97.8 0.0 copy-start.2
  97.8 0.7 copy-done.2
  98.5 8.3 %all-to-all-done.3 = bf16[32,32,128]{2,1,0:T(8,128)(2,1)S(1)} async-done(((bf16[32,32,128]{2,1,0:T(8,128)(2,1)}), bf16[32,32,128]{2,1,0:T(8,128)(2,1)S(1)}, u32[]{:S(2)}, u32[]{:S(2)}) %all-to-all-start.3) | async-done | bytes 262176 | tf_op jit(solution)/shard_map/all_to_all | solution.py:143
  106.8 0.0 copy-done
  106.8 2.0 %shard_map.74 = f32[4,2,128,128]{3,2,1,0:T(8,128)} custom-call(s32[2,8]{1,0:T(2,128)S(1)} %pad.8.neighbours, bf16[4,2,2,128,128]{4,3,2,1,0:T(8,128)(2,1)S(1)} %bitcast.14, bf16[4,2,128,128]{3,2,1,0:T(8,128)(2,1)S(1)} %bitcast.12), custom_call_target="tpu_custom_call" | custom-call | tf_op jit(solution)/shard_map/pallas_call | solution.py:129
  (9 shorter events, 0.1 us)
Async XLA Ops:
  27.4 3.6 %copy-start.4 = (s32[1,8]{1,0:T(1,128)S(1)}, s32[1,8]{1,0:T(1,128)}, u32[]{:S(2)}) copy-start(s32[1,8]{1,0:T(1,128)} %param.13) | copy-start | bytes 100
  27.4 23.1 %all-to-all-start.1 = ((bf16[32,32,128]{2,1,0:T(8,128)(2,1)}), bf16[32,32,128]{2,1,0:T(8,128)(2,1)S(1)}, u32[]{:S(2)}, u32[]{:S(2)}) async-start(bf16[32,32,128]{2,1,0:T(8,128)(2,1)} %all_to_all.20), calls=%async_computation.1 | async-start | bytes 524288 | tf_op jit(solution)/shard_map/all_to_all | solution.py:143
  31.5 4.3 %copy-start.5 = (s32[4]{0:T(128)S(1)}, s32[4]{0:T(128)}, u32[]{:S(2)}) copy-start(s32[4]{0:T(128)} %param.11) | copy-start | bytes 52
  31.5 6.3 %collective-permute-start = (bf16[1,128]{1,0:T(2,128)(2,1)S(1)}, bf16[1,128]{1,0:T(2,128)(2,1)S(1)}, u32[]{:S(2)}, u32[]{:S(2)}) collective-permute-start(bf16[1,128]{1,0:T(2,128)(2,1)S(1)} %convert_element_type.30), channel_id=1, source_target_pairs={{0,2},{1,3},{2,0},{3,1},{4,6},{5,7},{6,4},{7,5},{8,10},{9,11},{10,... | collective-permute-start | bytes 776 | tf_op jit(solution)/shard_map/ppermute | solution.py:147
  35.8 0.7 copy-start.3
  37.8 12.7 %collective-permute-start.1 = (bf16[2,128]{1,0:T(2,128)(2,1)S(1)}, bf16[2,128]{1,0:T(2,128)(2,1)S(1)}, u32[]{:S(2)}, u32[]{:S(2)}) collective-permute-start(bf16[2,128]{1,0:T(2,128)(2,1)S(1)} %pad_maximum_fusion.2), channel_id=1, source_target_pairs={{0,4},{1,5},{2,6},{3,7},{4,0},{5,1},{6,2},{7,3},{8,12},{9,13},{10,... | collective-permute-start | bytes 1544 | tf_op jit(solution)/shard_map/ppermute | solution.py:147
  50.6 2.6 %copy-start.1 = (f32[8,4]{0,1:T(4,128)S(1)}, f32[8,4]{0,1:T(4,128)}, u32[]{:S(2)}) copy-start(f32[8,4]{0,1:T(4,128)} %param.9) | copy-start | bytes 388
  50.6 5.3 %collective-permute-start.2 = (bf16[1040,128]{1,0:T(8,128)(2,1)S(1)}, bf16[1040,128]{1,0:T(8,128)(2,1)S(1)}, u32[]{:S(2)}, u32[]{:S(2)}) collective-permute-start(bf16[1040,128]{1,0:T(8,128)(2,1)S(1)} %pad_maximum_fusion.here), channel_id=1, source_target_pairs={{0,1},{1,2},{2,3},{3,4},{4,5},{5,6},{6,7},{7,256},{256,257},{257,2... | collective-permute-start | bytes 798728 | tf_op jit(solution)/shard_map/ppermute | solution.py:173
  51.9 7.8 %collective-permute-start.3 = (bf16[1040,128]{1,0:T(8,128)(2,1)S(1)}, bf16[1040,128]{1,0:T(8,128)(2,1)S(1)}, u32[]{:S(2)}, u32[]{:S(2)}) collective-permute-start(bf16[1040,128]{1,0:T(8,128)(2,1)S(1)} %pad_maximum_fusion.here), channel_id=1, source_target_pairs={{1,0},{2,1},{3,2},{4,3},{5,4},{6,5},{7,6},{256,7},{257,256},{258,2... | collective-permute-start | bytes 798728 | tf_op jit(solution)/shard_map/ppermute | solution.py:174
  60.5 46.3 %copy-start = (bf16[1,4,2,2,128,128]{5,4,3,2,1,0:T(8,128)(2,1)S(1)}, bf16[1,4,2,2,128,128]{5,4,3,2,1,0:T(8,128)(2,1)}, u32[]{:S(2)}) copy-start(bf16[1,4,2,2,128,128]{5,4,3,2,1,0:T(8,128)(2,1)} %param.8) | copy-start | bytes 1572868
  87.2 19.6 %all-to-all-start.3 = ((bf16[32,32,128]{2,1,0:T(8,128)(2,1)}), bf16[32,32,128]{2,1,0:T(8,128)(2,1)S(1)}, u32[]{:S(2)}, u32[]{:S(2)}) async-start(bf16[32,32,128]{2,1,0:T(8,128)(2,1)} %all_to_all.21), calls=%async_computation.3 | async-start | bytes 524288 | tf_op jit(solution)/shard_map/all_to_all | solution.py:143
  97.8 0.7 copy-start.2

commit v11 on v9

--- a/solution.py
+++ b/solution.py
@@ -79,9 +79,15 @@
     )(levels, before, here, after)
 
 
-def dress_kernel(neighbours, grad, near, out, result, done):
+def dress_kernel(chosen, grad, near, out, result, minus, neighbours, done, ready):
     clusters, listed = grad.shape[:2]
     orbits = out.shape[-1]
+    copy = pltpu.make_async_copy(chosen, neighbours, ready)
+    copy.start()
+    for c in range(clusters):
+        for s in range(listed):
+            minus[c, s] = -grad[c, s, 1]
+    copy.wait()
     copies = []
     for c in range(clusters):
         prods, rights = [], []
@@ -95,7 +101,7 @@
             middle = jnp.concatenate(
                 [jnp.concatenate([re, im], axis=1), jnp.concatenate([-im, re], axis=1)], axis=0
             )
-            rights.append(jnp.concatenate([left, jnp.concatenate([-d_im, d_re], axis=1)], axis=0))
+            rights.append(jnp.concatenate([left, jnp.concatenate([minus[c, s], d_re], axis=1)], axis=0))
             prods.append(jnp.dot(left, middle, preferred_element_type=jnp.float32))
         prod = jnp.concatenate(prods, axis=1)
         high = prod.astype(jnp.bfloat16)
@@ -117,17 +123,20 @@
 
 
 def dressed(neighbours, grad, mixed_blocks):
-    smem = pl.BlockSpec(memory_space=pltpu.SMEM)
+    free = pl.BlockSpec(memory_space=pl.ANY)
     vmem = pl.BlockSpec(memory_space=pltpu.VMEM)
     clusters = grad.shape[0]
     return pl.pallas_call(
         dress_kernel,
         out_shape=jax.ShapeDtypeStruct(mixed_blocks.shape, jnp.float32),
-        in_specs=[smem, vmem, vmem],
-        out_specs=pl.BlockSpec(memory_space=pl.ANY),
+        in_specs=[free, vmem, vmem],
+        out_specs=free,
         scratch_shapes=[
             pltpu.VMEM(mixed_blocks.shape, jnp.float32),
+            pltpu.VMEM((clusters, grad.shape[1], *mixed_blocks.shape[2:]), grad.dtype),
+            pltpu.SMEM(neighbours.shape, jnp.int32),
             pltpu.SemaphoreType.DMA((clusters,)),
+            pltpu.SemaphoreType.DMA,
         ],
         compiler_params=pltpu.CompilerParams(vmem_limit_bytes=16 << 20),
     )(neighbours, grad, mixed_blocks)

time: 109 us -> 109 us (level)
  no operation moved by 1% of the time
where the time goes in v11:
time: 109 us
  blocking collectives  54.2 us (50%)
  starting transfers between devices  33.8 us (31%)
  waiting for transfers between devices  16.1 us (15%)
  Pallas kernels  2.79 us (3%)
  local copies, waits for them, and re-layouts  1.44 us (1%)
    all_to_all x2, blocking collectives, swap(): return lax.all_to_all(x, axis, split_axis=0, concat_axis=0, tiled=True)  54.2 us
    ppermute x2, starting transfers between devices, paired(): other = lax.ppermute(x, 'mom', [(k, k ^ bit) for k in range(momenta)])  17.3 us
    all_to_all x2, starting transfers between devices, swap(): return lax.all_to_all(x, axis, split_axis=0, concat_axis=0, tiled=True)  13.9 us
    all_to_all x2, waiting for transfers between devices, swap(): return lax.all_to_all(x, axis, split_axis=0, concat_axis=0, tiled=True)  8.3 us
    ppermute x1, waiting for transfers between devices, shards(): after = lax.ppermute(here, LINE, [(z + 1, z) for z in range(quads - 1)])  3.85 us
    ppermute x1, waiting for transfers between devices, shards(): before = lax.ppermute(here, LINE, [(z, z + 1) for z in range(quads - 1)])  2.7 us
  transfers between devices with their start and end apart: 6, of which 5 were waited for; matrix products, arithmetic and copies ran while one was open for 0% of the time, Pallas kernels for 0%

profile of v11, /device:TPU:1, one launch (start us, length us, event | category | flops | bytes accessed | tf_op | source)
XLA Modules:
  0.0 108.8 jit_solution(436808099640827482)
XLA Ops:
  0.0 27.3 %all_to_all.20 = bf16[32,32,128]{2,1,0:T(8,128)(2,1)} all-to-all(bf16[32,32,128]{2,1,0:T(8,128)(2,1)} %bitcast.18), channel_id=1, replica_groups=mesh['zh'=4,'y'=4,'x'=4,'core'=2,'mom'=8] {'y','x','core'}, dimensions={0} | all-to-all | bytes 524288 | tf_op jit(solution)/shard_map/all_to_all | solution.py:146
  27.3 0.0 copy-start.4
  27.3 3.5 %all-to-all-start.1 = ((bf16[32,32,128]{2,1,0:T(8,128)(2,1)}), bf16[32,32,128]{2,1,0:T(8,128)(2,1)S(1)}, u32[]{:S(2)}, u32[]{:S(2)}) async-start(bf16[32,32,128]{2,1,0:T(8,128)(2,1)} %all_to_all.20), calls=%async_computation.1 | async-start | bytes 524288 | tf_op jit(solution)/shard_map/all_to_all | solution.py:146
  30.9 0.0 copy-done.4
  30.9 0.1 broadcast_in_dim.30
  31.0 0.1 convert_element_type.22
  31.0 0.0 copy-start.5
  31.0 4.3 %collective-permute-start = (bf16[1,128]{1,0:T(2,128)(2,1)S(1)}, bf16[1,128]{1,0:T(2,128)(2,1)S(1)}, u32[]{:S(2)}, u32[]{:S(2)}) collective-permute-start(bf16[1,128]{1,0:T(2,128)(2,1)S(1)} %convert_element_type.22), channel_id=1, source_target_pairs={{0,2},{1,3},{2,0},{3,1},{4,6},{5,7},{6,4},{7,5},{8,10},{9,11},{10,... | collective-permute-start | bytes 776 | tf_op jit(solution)/shard_map/ppermute | solution.py:150
  35.3 0.0 copy-done.5
  35.4 0.0 copy-start.3
  35.4 0.1 broadcast_compare_fusion
  35.4 0.6 copy-done.3
  36.0 0.4 collective-permute-done
  36.4 13.1 %collective-permute-start.1 = (bf16[2,128]{1,0:T(2,128)(2,1)S(1)}, bf16[2,128]{1,0:T(2,128)(2,1)S(1)}, u32[]{:S(2)}, u32[]{:S(2)}) collective-permute-start(bf16[2,128]{1,0:T(2,128)(2,1)S(1)} %pad_maximum_fusion.2), channel_id=1, source_target_pairs={{0,4},{1,5},{2,6},{3,7},{4,0},{5,1},{6,2},{7,3},{8,12},{9,13},{10,... | collective-permute-start | bytes 1544 | tf_op jit(solution)/shard_map/ppermute | solution.py:150
  49.5 0.9 collective-permute-done.1
  50.4 0.0 all-to-all-done.1
  50.5 0.0 copy-start.1
  50.5 1.3 %collective-permute-start.2 = (bf16[1040,128]{1,0:T(8,128)(2,1)S(1)}, bf16[1040,128]{1,0:T(8,128)(2,1)S(1)}, u32[]{:S(2)}, u32[]{:S(2)}) collective-permute-start(bf16[1040,128]{1,0:T(8,128)(2,1)S(1)} %pad_maximum_fusion.here), channel_id=1, source_target_pairs={{0,1},{1,2},{2,3},{3,4},{4,5},{5,6},{6,7},{7,256},{256,257},{257,2... | collective-permute-start | bytes 798728 | tf_op jit(solution)/shard_map/ppermute | solution.py:173
  51.8 1.3 %collective-permute-start.3 = (bf16[1040,128]{1,0:T(8,128)(2,1)S(1)}, bf16[1040,128]{1,0:T(8,128)(2,1)S(1)}, u32[]{:S(2)}, u32[]{:S(2)}) collective-permute-start(bf16[1040,128]{1,0:T(8,128)(2,1)S(1)} %pad_maximum_fusion.here), channel_id=1, source_target_pairs={{1,0},{2,1},{3,2},{4,3},{5,4},{6,5},{7,6},{256,7},{257,256},{258,2... | collective-permute-start | bytes 798728 | tf_op jit(solution)/shard_map/ppermute | solution.py:174
  53.1 0.0 copy-done.1
  53.1 0.1 multiply_reduce_fusion
  53.2 2.7 %collective-permute-done.2.before = bf16[1040,128]{1,0:T(8,128)(2,1)S(1)} collective-permute-done((bf16[1040,128]{1,0:T(8,128)(2,1)S(1)}, bf16[1040,128]{1,0:T(8,128)(2,1)S(1)}, u32[]{:S(2)}, u32[]{:S(2)}) %collective-permute-start.2) | collective-permute-done | bytes 266272 | tf_op jit(solution)/shard_map/ppermute | solution.py:173
  55.9 3.8 %collective-permute-done.3.after = bf16[1040,128]{1,0:T(8,128)(2,1)S(1)} collective-permute-done((bf16[1040,128]{1,0:T(8,128)(2,1)S(1)}, bf16[1040,128]{1,0:T(8,128)(2,1)S(1)}, u32[]{:S(2)}, u32[]{:S(2)}) %collective-permute-start.3) | collective-permute-done | bytes 266272 | tf_op jit(solution)/shard_map/ppermute | solution.py:174
  59.7 0.8 shard_map.73
  60.6 0.0 copy-start
  60.6 26.9 %all_to_all.21 = bf16[32,32,128]{2,1,0:T(8,128)(2,1)} all-to-all(bf16[32,32,128]{2,1,0:T(8,128)(2,1)S(1)} %bitcast.14), channel_id=1, replica_groups=mesh['zh'=4,'y'=4,'x'=4,'core'=2,'mom'=8] {'mom'}, dimensions={0} | all-to-all | bytes 524288 | tf_op jit(solution)/shard_map/all_to_all | solution.py:146
  87.5 10.3 %all-to-all-start.3 = ((bf16[32,32,128]{2,1,0:T(8,128)(2,1)}), bf16[32,32,128]{2,1,0:T(8,128)(2,1)S(1)}, u32[]{:S(2)}, u32[]{:S(2)}) async-start(bf16[32,32,128]{2,1,0:T(8,128)(2,1)} %all_to_all.21), calls=%async_computation.3 | async-start | bytes 524288 | tf_op jit(solution)/shard_map/all_to_all | solution.py:146
  97.8 0.0 copy-start.2
  97.8 0.7 copy-done.2
  98.5 8.3 %all-to-all-done.3 = bf16[32,32,128]{2,1,0:T(8,128)(2,1)S(1)} async-done(((bf16[32,32,128]{2,1,0:T(8,128)(2,1)}), bf16[32,32,128]{2,1,0:T(8,128)(2,1)S(1)}, u32[]{:S(2)}, u32[]{:S(2)}) %all-to-all-start.3) | async-done | bytes 262176 | tf_op jit(solution)/shard_map/all_to_all | solution.py:146
  106.8 0.0 copy-done
  106.8 2.0 %shard_map.74 = f32[4,2,128,128]{3,2,1,0:T(8,128)} custom-call(s32[2,8]{1,0:T(2,128)S(1)} %pad.8.chosen, bf16[4,2,2,128,128]{4,3,2,1,0:T(8,128)(2,1)S(1)} %bitcast.15, bf16[4,2,128,128]{3,2,1,0:T(8,128)(2,1)S(1)} %bitcast.13), custom_call_target="tpu_custom_call" | custom-call | tf_op jit(solution)/shard_map/pallas_call | solution.py:129
  (9 shorter events, 0.1 us)
Async XLA Ops:
  27.3 3.6 %copy-start.4 = (s32[1,8]{1,0:T(1,128)S(1)}, s32[1,8]{1,0:T(1,128)}, u32[]{:S(2)}) copy-start(s32[1,8]{1,0:T(1,128)} %param.13) | copy-start | bytes 100
  27.3 23.1 %all-to-all-start.1 = ((bf16[32,32,128]{2,1,0:T(8,128)(2,1)}), bf16[32,32,128]{2,1,0:T(8,128)(2,1)S(1)}, u32[]{:S(2)}, u32[]{:S(2)}) async-start(bf16[32,32,128]{2,1,0:T(8,128)(2,1)} %all_to_all.20), calls=%async_computation.1 | async-start | bytes 524288 | tf_op jit(solution)/shard_map/all_to_all | solution.py:146
  31.0 4.3 %copy-start.5 = (s32[4]{0:T(128)S(1)}, s32[4]{0:T(128)}, u32[]{:S(2)}) copy-start(s32[4]{0:T(128)} %param.11) | copy-start | bytes 52
  31.0 5.3 %collective-permute-start = (bf16[1,128]{1,0:T(2,128)(2,1)S(1)}, bf16[1,128]{1,0:T(2,128)(2,1)S(1)}, u32[]{:S(2)}, u32[]{:S(2)}) collective-permute-start(bf16[1,128]{1,0:T(2,128)(2,1)S(1)} %convert_element_type.22), channel_id=1, source_target_pairs={{0,2},{1,3},{2,0},{3,1},{4,6},{5,7},{6,4},{7,5},{8,10},{9,11},{10,... | collective-permute-start | bytes 776 | tf_op jit(solution)/shard_map/ppermute | solution.py:150
  35.4 0.7 copy-start.3
  36.4 14.0 %collective-permute-start.1 = (bf16[2,128]{1,0:T(2,128)(2,1)S(1)}, bf16[2,128]{1,0:T(2,128)(2,1)S(1)}, u32[]{:S(2)}, u32[]{:S(2)}) collective-permute-start(bf16[2,128]{1,0:T(2,128)(2,1)S(1)} %pad_maximum_fusion.2), channel_id=1, source_target_pairs={{0,4},{1,5},{2,6},{3,7},{4,0},{5,1},{6,2},{7,3},{8,12},{9,13},{10,... | collective-permute-start | bytes 1544 | tf_op jit(solution)/shard_map/ppermute | solution.py:150
  50.5 2.6 %copy-start.1 = (f32[8,4]{0,1:T(4,128)S(1)}, f32[8,4]{0,1:T(4,128)}, u32[]{:S(2)}) copy-start(f32[8,4]{0,1:T(4,128)} %param.9) | copy-start | bytes 388
  50.5 5.4 %collective-permute-start.2 = (bf16[1040,128]{1,0:T(8,128)(2,1)S(1)}, bf16[1040,128]{1,0:T(8,128)(2,1)S(1)}, u32[]{:S(2)}, u32[]{:S(2)}) collective-permute-start(bf16[1040,128]{1,0:T(8,128)(2,1)S(1)} %pad_maximum_fusion.here), channel_id=1, source_target_pairs={{0,1},{1,2},{2,3},{3,4},{4,5},{5,6},{6,7},{7,256},{256,257},{257,2... | collective-permute-start | bytes 798728 | tf_op jit(solution)/shard_map/ppermute | solution.py:173
  51.8 8.0 %collective-permute-start.3 = (bf16[1040,128]{1,0:T(8,128)(2,1)S(1)}, bf16[1040,128]{1,0:T(8,128)(2,1)S(1)}, u32[]{:S(2)}, u32[]{:S(2)}) collective-permute-start(bf16[1040,128]{1,0:T(8,128)(2,1)S(1)} %pad_maximum_fusion.here), channel_id=1, source_target_pairs={{1,0},{2,1},{3,2},{4,3},{5,4},{6,5},{7,6},{256,7},{257,256},{258,2... | collective-permute-start | bytes 798728 | tf_op jit(solution)/shard_map/ppermute | solution.py:174
  60.6 46.3 %copy-start = (bf16[1,4,2,2,128,128]{5,4,3,2,1,0:T(8,128)(2,1)S(1)}, bf16[1,4,2,2,128,128]{5,4,3,2,1,0:T(8,128)(2,1)}, u32[]{:S(2)}) copy-start(bf16[1,4,2,2,128,128]{5,4,3,2,1,0:T(8,128)(2,1)} %param.8) | copy-start | bytes 1572868
  87.5 19.3 %all-to-all-start.3 = ((bf16[32,32,128]{2,1,0:T(8,128)(2,1)}), bf16[32,32,128]{2,1,0:T(8,128)(2,1)S(1)}, u32[]{:S(2)}, u32[]{:S(2)}) async-start(bf16[32,32,128]{2,1,0:T(8,128)(2,1)} %all_to_all.21), calls=%async_computation.3 | async-start | bytes 524288 | tf_op jit(solution)/shard_map/all_to_all | solution.py:146
  97.8 0.7 copy-start.2
